TPU v7x, 32 devices: a whole 2x2x4 slice. The times are simulated.
32 devices in a mesh: pair: 16 (over z, x, core), cuts: 2 (over y).
Axes of the slice: x: 2, y: 2, z: 4, core: 2. Of those that a mesh axis runs over, the one named last changes fastest.
Arguments:
- amplitudes: bfloat16 [16384, 2048], P('pair'), may hold values from -6 to 6
- factors: bfloat16 [32, 6, 128, 128], P('pair', 'cuts'), may hold values from -0.5 to 0.5
- screening: int32 [8, 16], replicated, may hold values from 0 to 31, as said below
- tile_slot: int32 [32], replicated, may hold values from 0 to 31, as said below
- pair_orbitals: int32 [8, 2], replicated, may hold values from 0 to 3999
- occupied_energy: float32 [4000], replicated, may hold values from -2 to -0.3
- virtual_energy: float32 [32, 128], replicated, may hold values from 0.2 to 3
Outputs:
- scaled_residual: float32 [16384, 2048], P(('pair', 'cuts'))
Inputs may be any that keep to these rules, and one draw needn't show every extreme that they name: `screening`: call tile_slot[t] // 2 the owner of tile t. The 16 tiles named by one pair have 16 different owners. `tile_slot`: every tile has its own slot.
All inputs are finite; a program needn't handle non-finite values.
Results may differ from a plain program's by a relative error of at most 0.012.
Values may be sent and summed in bfloat16 or wider, within the bound.
No kernel may reach another device: no remote copies, remote signals or barrier semaphores. Data moves between devices by JAX's collectives and lax.ppermute only.
A program may use at most 64 MiB of HBM per device.

v0:
```python
import functools

import jax
import jax.numpy as jnp
from jax import lax
from jax.experimental import pallas as pl
from jax.experimental.pallas import tpu as pltpu
from jax.sharding import PartitionSpec as P


BOTH = ("pair", "cuts")
ANY = pl.BlockSpec(memory_space=pl.ANY)
SMEM = pl.BlockSpec(memory_space=pltpu.SMEM)
VMEM = pl.BlockSpec(memory_space=pltpu.VMEM)


def pick_kernel(tile_dev, group, screening, tile_slot, factors, *refs):
    outs, sems = refs[:-1], refs[-1]
    count = screening.shape[1]
    me = lax.axis_index("pair")
    copies = []
    for shift, out in enumerate(outs):
        peer = (me // group) ^ shift
        local = jnp.int32(0)
        for t in range(count):
            slot = tile_slot[screening[peer, t]]
            local = jnp.where(slot // tile_dev == me, slot % tile_dev, local)
        copy = pltpu.make_async_copy(factors.at[local], out, sems.at[shift])
        copy.start()
        copies.append(copy)
    for copy in copies:
        copy.wait()


def pick(screening, tile_slot, factors, group, shifts):
    tile_dev, *tail = factors.shape
    return pl.pallas_call(
        functools.partial(pick_kernel, tile_dev, group),
        out_shape=[jax.ShapeDtypeStruct(tail, factors.dtype)] * shifts,
        in_specs=[SMEM, SMEM, VMEM],
        out_specs=[ANY] * shifts,
        scratch_shapes=[pltpu.SemaphoreType.DMA((shifts,))],
        name="pick",
    )(screening, tile_slot, factors)


def ladder_kernel(
    dims, screening, tile_slot, occ, virt, amp, *refs
):
    tile_dev, group, row_tiles, shifts, n_q, tile, wide = dims
    mine, other, (out, left, row_den, held, sem, out_sem) = refs[:3], refs[3:6], refs[6:]
    me, cut = lax.axis_index("pair"), lax.axis_index("cuts")
    pair_id, core = me // group, me % group
    count = screening.shape[1]
    first = core * (count // group) + cut * row_tiles
    half_q, half_s = n_q // 2, shifts // 2

    for t in range(count):
        slot = tile_slot[screening[pair_id, t]]
        owner = slot // tile_dev
        shift = (owner // group) ^ pair_id
        same = owner % group == core
        near = shift < half_s
        far = shift - half_s
        for part in range(2):
            dst = left.at[t, pl.ds(part * half_q, half_q)]
            for held_by, bufs in ((same, mine), (jnp.logical_not(same), other)):

                @pl.when(held_by & near)
                def _():
                    pltpu.make_async_copy(bufs[0].at[part * half_s + shift], dst, sem).start()

                @pl.when(held_by & jnp.logical_not(near))
                def _():
                    pltpu.make_async_copy(bufs[1 + part].at[far], dst, sem).start()

    for i in range(row_tiles):
        row = virt[pl.ds(screening[pair_id, first + i], 1), :] - occ[0]
        row_den[i] = jnp.broadcast_to(row, (tile, tile)).T
    pltpu.make_async_copy(left, left, sem).wait()

    def write(step, slot):
        at = pl.ds(pl.multiple_of(step * wide, wide), wide)
        return pltpu.make_async_copy(held.at[slot], out.at[:, at], out_sem.at[slot])

    steps = out.shape[1] // wide

    @pl.loop(0, steps)
    def _(step):
        slot = step % 2

        @pl.when(step >= 2)
        def _():
            write(step - 2, slot).wait()

        halves = []
        for i in range(row_tiles):
            lhs = left[first + i].reshape(n_q * tile, tile)
            block = amp[i * tile : (i + 1) * tile, pl.ds(pl.multiple_of(step * wide, wide), wide)]
            half = jnp.dot(lhs, block, preferred_element_type=jnp.float32)
            halves.append(half.astype(jnp.bfloat16))
        for j in range(wide // tile):
            col = step * (wide // tile) + j
            cols = slice(j * tile, (j + 1) * tile)
            lhs = jnp.concatenate(
                [
                    jnp.concatenate(
                        [h[q * tile : (q + 1) * tile, cols] for q in range(n_q)], axis=1
                    )
                    for h in halves
                ],
                axis=0,
            )
            rhs = jnp.concatenate([left[col, q] for q in range(n_q)], axis=1)
            acc = lax.dot_general(
                lhs, rhs, (((1,), (1,)), ((), ())), preferred_element_type=jnp.float32
            )
            col_e = virt[pl.ds(screening[pair_id, col], 1), :] - occ[1]
            for i in range(row_tiles):
                rows = slice(i * tile, (i + 1) * tile)
                held[slot, rows, cols] = acc[rows] / (row_den[i] + col_e)
        write(step, slot).start()

    for step in range(max(0, steps - 2), steps):
        write(step, step % 2).wait()


def ladder(screening, tile_slot, occ, virt, amp, mine, other, dims):
    _, _, row_tiles, _, n_q, tile, wide = dims
    rows, columns = amp.shape
    return pl.pallas_call(
        functools.partial(ladder_kernel, dims),
        out_shape=jax.ShapeDtypeStruct((rows, columns), jnp.float32),
        in_specs=[SMEM, SMEM, SMEM, VMEM, VMEM] + [ANY] * 6,
        out_specs=ANY,
        scratch_shapes=[
            pltpu.VMEM((screening.shape[1], n_q, tile, tile), jnp.bfloat16),
            pltpu.VMEM((row_tiles, tile, tile), jnp.float32),
            pltpu.VMEM((2, rows, wide), jnp.float32),
            pltpu.SemaphoreType.DMA,
            pltpu.SemaphoreType.DMA((2,)),
        ],
        compiler_params=pltpu.CompilerParams(vmem_limit_bytes=24 * 2**20),
        name="ladder",
    )(screening, tile_slot, occ, virt, amp, *mine, *other)


def direct(
    amplitudes, factors, screening, tile_slot, pair_orbitals, occupied_energy, virtual_energy
):
    tile_dev, q_cut, tile, _ = factors.shape
    n_pair, n_cut = lax.axis_size("pair"), lax.axis_size("cuts")
    group = n_pair // screening.shape[0]
    shifts = n_pair // group
    row_tiles = amplitudes.shape[0] // tile // n_cut
    me = lax.axis_index("pair")

    def send(x, move):
        pairs = [
            (p * n_cut + c, dst[0] * n_cut + dst[1])
            for p in range(n_pair)
            for c in range(n_cut)
            for dst in [move(p, c)]
        ]
        return lax.ppermute(x, BOTH, pairs)

    picked = pick(screening, tile_slot, factors, group, shifts)
    got = [picked[0]] + [None] * (shifts - 1)
    for s in range(1, shifts):
        got[s] = send(picked[s], lambda p, c: (p ^ (s * group), c))
    crossed = []
    for s in range(shifts):
        crossed.append(send(got[s], lambda p, c: (p, c ^ 1)))
    half = shifts // 2
    mine = [
        jnp.stack(got[:half] + crossed[:half]),
        jnp.stack(got[half:]),
        jnp.stack(crossed[half:]),
    ]
    other = []
    for x in mine:
        other.append(send(x, lambda p, c: (p ^ 1, c)))
    occ = occupied_energy[pair_orbitals[me // group]]
    rows = row_tiles * tile
    amp = lax.dynamic_slice_in_dim(amplitudes, lax.axis_index("cuts") * rows, rows, 0)
    dims = (tile_dev, group, row_tiles, shifts, q_cut * n_cut, tile, 2 * tile)
    return ladder(screening, tile_slot, occ, virtual_energy, amp, mine, other, dims)


def general(
    amplitudes, factors, screening, tile_slot, pair_orbitals, occupied_energy, virtual_energy
):
    tile_dev, q_cut, tile, _ = factors.shape
    count = screening.shape[1]
    me = lax.axis_index("pair")
    row_tiles = amplitudes.shape[0] // tile
    first_tile = me * row_tiles
    pair_id, tile_start = first_tile // count, first_tile % count
    my_tiles = screening[pair_id]
    my_slots = tile_slot[my_tiles]
    device_pairs = jnp.arange(lax.axis_size("pair"), dtype=jnp.int32) * row_tiles // count
    slot_table = tile_slot[screening[device_pairs]]
    wanted = slot_table // tile_dev == me
    local = jnp.sum(jnp.where(wanted, slot_table % tile_dev, 0), axis=1)
    needed = jnp.any(wanted, axis=1)
    outgoing = jnp.where(
        needed[:, None, None, None], factors[local], jnp.zeros((), factors.dtype)
    )
    incoming = lax.all_to_all(outgoing, "pair", split_axis=0, concat_axis=0, tiled=True)
    chosen = incoming[my_slots // tile_dev]
    left = lax.dynamic_slice_in_dim(chosen, tile_start, row_tiles, 0)
    blocks = amplitudes.reshape(row_tiles, tile, count * tile)
    total = jnp.zeros((row_tiles, tile, count, tile), jnp.float32)
    for q in range(q_cut):
        half = jnp.einsum(
            "iac,icx->iax", left[:, q], blocks, preferred_element_type=jnp.float32
        )
        half = half.astype(jnp.bfloat16).reshape(row_tiles, tile, count, tile)
        total = total + jnp.einsum(
            "iajd,jbd->iajb", half, chosen[:, q], preferred_element_type=jnp.float32
        )
    partial = total.reshape(row_tiles * tile, count * tile).astype(jnp.bfloat16)
    summed = lax.psum_scatter(partial, "cuts", scatter_dimension=0, tiled=True)
    occ = occupied_energy[pair_orbitals[pair_id]]
    energy = virtual_energy[my_tiles].reshape(count * tile)
    rows = summed.shape[0]
    begin = tile_start * tile + lax.axis_index("cuts") * rows
    row_energy = lax.dynamic_slice_in_dim(energy - occ[0], begin, rows, 0)
    return summed.astype(jnp.float32) / (row_energy[:, None] + (energy - occ[1])[None, :])


def solution(mesh):
    n_pair, n_cut = mesh.shape["pair"], mesh.shape["cuts"]

    def build(body):
        return jax.shard_map(
            body,
            mesh=mesh,
            in_specs=(P("pair", None), P("pair", "cuts", None, None), P(), P(), P(), P(), P()),
            out_specs=P(BOTH, None),
            check_vma=False,
        )

    def whole(amplitudes, factors, screening, *rest):
        n_pos, count = screening.shape
        every_owner = count == n_pair and n_pair == 2 * n_pos and n_pos & (n_pos - 1) == 0
        if not (every_owner and n_cut == 2):
            return build(general)(amplitudes, factors, screening, *rest)
        step = build(direct)
        return step(amplitudes, factors, screening, *rest)

    return whole
```

profile of v0, /device:TPU:0, one launch (start us, length us, event | category | flops | bytes accessed | tf_op | source)
XLA Modules:
  0.0 54.2 jit_solution(16591632498655660592)
XLA Ops:
  0.0 0.0 copy-start
  0.0 2.5 %pick.1 = (bf16[3,128,128]{2,1,0:T(8,128)(2,1)}, bf16[3,128,128]{2,1,0:T(8,128)(2,1)}, bf16[3,128,128]{2,1,0:T(8,128)(2,1)}, bf16[3,128,128]{2,1,0:T(8,128)(2,1)...) custom-call(s32[8,16]{1,0:T(8,128)} %screening.3, ...), custom_call_target="tpu_custom_call" | custom-call | tf_op jit(solution)/shard_map/pick/pallas_call | solution.py:37
  2.6 3.0 %collective-permute-start = (bf16[3,128,128]{2,1,0:T(8,128)(2,1)}, bf16[3,128,128]{2,1,0:T(8,128)(2,1)S(1)}, u32[]{:S(2)}, u32[]{:S(2)}) collective-permute-start(bf16[3,128,128]{2,1,0:T(8,128)(2,1)} %get-tuple-element.14), channel_id=1, source_target_pairs={{0,4},{1,5},{2,6},{3,7},{4,0},{5,1},{6,2},{7,3},{8,12},{9,13},{10,... | collective-permute-start | bytes 294920 | tf_op jit(solution)/shard_map/ppermute | solution.py:165
  5.6 1.6 %collective-permute-start.1 = (bf16[3,128,128]{2,1,0:T(8,128)(2,1)}, bf16[3,128,128]{2,1,0:T(8,128)(2,1)S(1)}, u32[]{:S(2)}, u32[]{:S(2)}) collective-permute-start(bf16[3,128,128]{2,1,0:T(8,128)(2,1)} %get-tuple-element.15), channel_id=1, source_target_pairs={{0,8},{1,9},{2,10},{3,11},{4,12},{5,13},{6,14},{7,15},{8,0},{9,1},... | collective-permute-start | bytes 294920 | tf_op jit(solution)/shard_map/ppermute | solution.py:165
  7.2 0.0 collective-permute-start.2
  7.2 3.0 %collective-permute-start.7 = (bf16[3,128,128]{2,1,0:T(8,128)(2,1)}, bf16[3,128,128]{2,1,0:T(8,128)(2,1)S(1)}, u32[]{:S(2)}, u32[]{:S(2)}) collective-permute-start(bf16[3,128,128]{2,1,0:T(8,128)(2,1)} %get-tuple-element.17), channel_id=1, source_target_pairs={{0,16},{1,17},{2,18},{3,19},{4,20},{5,21},{6,22},{7,23},{8,24},{9,... | collective-permute-start | bytes 294920 | tf_op jit(solution)/shard_map/ppermute | solution.py:165
  10.2 1.5 %collective-permute-start.3 = (bf16[3,128,128]{2,1,0:T(8,128)(2,1)}, bf16[3,128,128]{2,1,0:T(8,128)(2,1)S(1)}, u32[]{:S(2)}, u32[]{:S(2)}) collective-permute-start(bf16[3,128,128]{2,1,0:T(8,128)(2,1)} %get-tuple-element.13), channel_id=1, source_target_pairs={{0,1},{1,0},{2,3},{3,2},{4,5},{5,4},{6,7},{7,6},{8,9},{9,8},{10,11... | collective-permute-start | bytes 294920 | tf_op jit(solution)/shard_map/ppermute | solution.py:165
  11.7 0.9 %bitcast_dynamic-update-slice_fusion.7 = bf16[8,3,128,128]{3,2,1,0:T(8,128)(2,1)S(1)} fusion(bf16[3,128,128]{2,1,0:T(8,128)(2,1)} %get-tuple-element.13), kind=kLoop, calls=%fused_computation.10 | loop fusion | bytes 196608
  12.6 0.9 %dynamic-slice_reduce_fusion = s32[2]{0:T(128)S(1)} fusion(s32[8,2]{0,1:T(2,128)} %param.11, s32[]{:T(128)S(6)} %select_n.22), kind=kLoop, calls=%fused_computation.13 | loop fusion | bytes 20 | tf_op jit(solution)/shard_map/dynamic_slice | solution.py:183
  13.5 0.0 collective-permute-done
  13.5 1.3 %collective-permute-start.8 = (bf16[3,128,128]{2,1,0:T(8,128)(2,1)}, bf16[3,128,128]{2,1,0:T(8,128)(2,1)S(1)}, u32[]{:S(2)}, u32[]{:S(2)}) collective-permute-start(bf16[3,128,128]{2,1,0:T(8,128)(2,1)} %get-tuple-element.18), channel_id=1, source_target_pairs={{0,20},{1,21},{2,22},{3,23},{4,16},{5,17},{6,18},{7,19},{8,28},{9,... | collective-permute-start | bytes 294920 | tf_op jit(solution)/shard_map/ppermute | solution.py:165
  14.9 0.0 collective-permute-done.1
  14.9 3.7 %collective-permute-start.9 = (bf16[3,128,128]{2,1,0:T(8,128)(2,1)}, bf16[3,128,128]{2,1,0:T(8,128)(2,1)S(1)}, u32[]{:S(2)}, u32[]{:S(2)}) collective-permute-start(bf16[3,128,128]{2,1,0:T(8,128)(2,1)} %get-tuple-element.19), channel_id=1, source_target_pairs={{0,24},{1,25},{2,26},{3,27},{4,28},{5,29},{6,30},{7,31},{8,16},{9,... | collective-permute-start | bytes 294920 | tf_op jit(solution)/shard_map/ppermute | solution.py:165
  18.5 0.0 collective-permute-done.2
  18.6 0.3 collective-permute-start.10
  18.8 0.0 collective-permute-done.3
  18.8 1.1 %collective-permute-start.4 = (bf16[3,128,128]{2,1,0:T(8,128)(2,1)S(1)}, bf16[3,128,128]{2,1,0:T(8,128)(2,1)S(1)}, u32[]{:S(2)}, u32[]{:S(2)}) collective-permute-start(bf16[3,128,128]{2,1,0:T(8,128)(2,1)S(1)} %collective-permute-done), channel_id=1, source_target_pairs={{0,1},{1,0},{2,3},{3,2},{4,5},{5,4},{6,7},{7,6},{8,9},{9,8},{10,11... | collective-permute-start | bytes 294920 | tf_op jit(solution)/shard_map/ppermute | solution.py:165
  20.0 4.1 %collective-permute-done.4 = bf16[3,128,128]{2,1,0:T(8,128)(2,1)S(1)} collective-permute-done((bf16[3,128,128]{2,1,0:T(8,128)(2,1)S(1)}, bf16[3,128,128]{2,1,0:T(8,128)(2,1)S(1)}, u32[]{:S(2)}, u32[]{:S(2)}) %collective-permute-start.4) | collective-permute-done | bytes 98336 | tf_op jit(solution)/shard_map/ppermute | solution.py:165
  24.1 1.6 %collective-permute-start.5 = (bf16[3,128,128]{2,1,0:T(8,128)(2,1)S(1)}, bf16[3,128,128]{2,1,0:T(8,128)(2,1)S(1)}, u32[]{:S(2)}, u32[]{:S(2)}) collective-permute-start(bf16[3,128,128]{2,1,0:T(8,128)(2,1)S(1)} %collective-permute-done.1), channel_id=1, source_target_pairs={{0,1},{1,0},{2,3},{3,2},{4,5},{5,4},{6,7},{7,6},{8,9},{9,8},{10,11... | collective-permute-start | bytes 294920 | tf_op jit(solution)/shard_map/ppermute | solution.py:165
  25.7 0.0 collective-permute-done.7
  25.7 0.5 collective-permute-start.6
  26.2 0.0 collective-permute-done.8
  26.2 1.6 %collective-permute-start.11 = (bf16[3,128,128]{2,1,0:T(8,128)(2,1)S(1)}, bf16[3,128,128]{2,1,0:T(8,128)(2,1)S(1)}, u32[]{:S(2)}, u32[]{:S(2)}) collective-permute-start(bf16[3,128,128]{2,1,0:T(8,128)(2,1)S(1)} %collective-permute-done.7), channel_id=1, source_target_pairs={{0,1},{1,0},{2,3},{3,2},{4,5},{5,4},{6,7},{7,6},{8,9},{9,8},{10,11... | collective-permute-start | bytes 294920 | tf_op jit(solution)/shard_map/ppermute | solution.py:165
  27.8 0.0 collective-permute-done.9
  27.8 0.5 collective-permute-start.12
  28.2 0.0 collective-permute-done.10
  28.2 1.6 %collective-permute-start.13 = (bf16[3,128,128]{2,1,0:T(8,128)(2,1)S(1)}, bf16[3,128,128]{2,1,0:T(8,128)(2,1)S(1)}, u32[]{:S(2)}, u32[]{:S(2)}) collective-permute-start(bf16[3,128,128]{2,1,0:T(8,128)(2,1)S(1)} %collective-permute-done.9), channel_id=1, source_target_pairs={{0,1},{1,0},{2,3},{3,2},{4,5},{5,4},{6,7},{7,6},{8,9},{9,8},{10,11... | collective-permute-start | bytes 294920 | tf_op jit(solution)/shard_map/ppermute | solution.py:165
  29.8 0.0 collective-permute-done.5
  29.8 1.5 %collective-permute-start.14 = (bf16[3,128,128]{2,1,0:T(8,128)(2,1)S(1)}, bf16[3,128,128]{2,1,0:T(8,128)(2,1)S(1)}, u32[]{:S(2)}, u32[]{:S(2)}) collective-permute-start(bf16[3,128,128]{2,1,0:T(8,128)(2,1)S(1)} %collective-permute-done.10), channel_id=1, source_target_pairs={{0,1},{1,0},{2,3},{3,2},{4,5},{5,4},{6,7},{7,6},{8,9},{9,8},{10,11... | collective-permute-start | bytes 294920 | tf_op jit(solution)/shard_map/ppermute | solution.py:165
  31.3 0.2 collective-permute-done.6
  31.6 0.1 collective-permute-start.15
  31.6 0.1 pad_maximum_fusion.refs_1_
  31.7 1.9 %collective-permute-done.11 = bf16[3,128,128]{2,1,0:T(8,128)(2,1)S(1)} collective-permute-done((bf16[3,128,128]{2,1,0:T(8,128)(2,1)S(1)}, bf16[3,128,128]{2,1,0:T(8,128)(2,1)S(1)}, u32[]{:S(2)}, u32[]{:S(2)}) %collective-permute-start.11) | collective-permute-done | bytes 98336 | tf_op jit(solution)/shard_map/ppermute | solution.py:165
  33.7 0.0 collective-permute-start.16
  33.7 1.4 %collective-permute-done.12 = bf16[3,128,128]{2,1,0:T(8,128)(2,1)S(1)} collective-permute-done((bf16[3,128,128]{2,1,0:T(8,128)(2,1)S(1)}, bf16[3,128,128]{2,1,0:T(8,128)(2,1)S(1)}, u32[]{:S(2)}, u32[]{:S(2)}) %collective-permute-start.12) | collective-permute-done | bytes 98336 | tf_op jit(solution)/shard_map/ppermute | solution.py:165
  35.0 1.1 %collective-permute-done.13 = bf16[3,128,128]{2,1,0:T(8,128)(2,1)S(1)} collective-permute-done((bf16[3,128,128]{2,1,0:T(8,128)(2,1)S(1)}, bf16[3,128,128]{2,1,0:T(8,128)(2,1)S(1)}, u32[]{:S(2)}, u32[]{:S(2)}) %collective-permute-start.13) | collective-permute-done | bytes 98336 | tf_op jit(solution)/shard_map/ppermute | solution.py:165
  36.1 1.1 %collective-permute-done.14 = bf16[3,128,128]{2,1,0:T(8,128)(2,1)S(1)} collective-permute-done((bf16[3,128,128]{2,1,0:T(8,128)(2,1)S(1)}, bf16[3,128,128]{2,1,0:T(8,128)(2,1)S(1)}, u32[]{:S(2)}, u32[]{:S(2)}) %collective-permute-start.14) | collective-permute-done | bytes 98336 | tf_op jit(solution)/shard_map/ppermute | solution.py:165
  37.1 0.1 pad_maximum_fusion.1.refs_2_
  37.2 0.1 collective-permute-start.17
  37.3 0.6 %gather_fusion = f32[2]{0:T(128)S(1)} fusion(f32[4000]{0:T(1024)S(1)} %copy-done, s32[1024]{0:T(1024)S(1)} %pad_clamp_fusion), kind=kCustom, calls=%fused_computation | custom fusion | bytes 24 | tf_op jit(solution)/shard_map/gather | solution.py:183
  37.9 1.8 %constant_dynamic-slice_fusion.amp = bf16[512,2048]{1,0:T(8,128)(2,1)S(1)} fusion(bf16[1024,2048]{1,0:T(8,128)(2,1)} %param.7, s32[]{:T(128)S(6)} %select_n.24), kind=kLoop, calls=%fused_computation.15 | loop fusion | bytes 4194308 | tf_op jit(solution)/shard_map/dynamic_slice | solution.py:185
  39.8 0.0 collective-permute-done.16.refs_4_
  39.8 0.0 collective-permute-done.17.refs_5_
  39.8 0.0 collective-permute-done.15.refs_3_
  39.8 0.0 copy-done.3
  39.8 0.0 copy-done.2
  39.8 0.0 copy-done.1
  39.8 14.3 %ladder.1 = f32[512,2048]{1,0:T(8,128)} custom-call(s32[8,16]{1,0:T(8,128)S(1)} %copy-done.2, s32[32]{0:T(128)S(1)} %copy-done.3, f32[2]{0:T(128)S(1)} %gather_fusion, f32[32,128]{1,0:T(8,128)S(1)} %copy-done.1, bf16[512,2048]{1,0:T(8,128)(2,1)S(1)} %constant_dynamic-slice_fusion.amp, bf16[8,3,128,128]{3,2,1,0:T(8,128)(2,1)S(1)} %bitcast_dynamic-update-slice_fusion.refs_0_, ...), custom_call_target="tpu_custom_call" | custom-call | tf_op jit(solution)/shard_map/ladder/pallas_call | solution.py:131
  (13 shorter events, 0.1 us)
Async XLA Ops:
  0.0 37.3 %copy-start = (f32[4000]{0:T(1024)S(1)}, f32[4000]{0:T(1024)}, u32[]{:S(2)}) copy-start(f32[4000]{0:T(1024)} %param.12) | copy-start | bytes 48004
  0.0 39.8 %copy-start.3 = (s32[32]{0:T(128)S(1)}, s32[32]{0:T(128)}, u32[]{:S(2)}) copy-start(s32[32]{0:T(128)} %tile_slot.3) | copy-start | bytes 388
  0.0 39.8 %copy-start.2 = (s32[8,16]{1,0:T(8,128)S(1)}, s32[8,16]{1,0:T(8,128)}, u32[]{:S(2)}) copy-start(s32[8,16]{1,0:T(8,128)} %screening.3) | copy-start | bytes 1540
  0.0 39.8 %copy-start.1 = (f32[32,128]{1,0:T(8,128)S(1)}, f32[32,128]{1,0:T(8,128)}, u32[]{:S(2)}) copy-start(f32[32,128]{1,0:T(8,128)} %virt.1) | copy-start | bytes 49156
  2.6 10.9 %collective-permute-start = (bf16[3,128,128]{2,1,0:T(8,128)(2,1)}, bf16[3,128,128]{2,1,0:T(8,128)(2,1)S(1)}, u32[]{:S(2)}, u32[]{:S(2)}) collective-permute-start(bf16[3,128,128]{2,1,0:T(8,128)(2,1)} %get-tuple-element.14), channel_id=1, source_target_pairs={{0,4},{1,5},{2,6},{3,7},{4,0},{5,1},{6,2},{7,3},{8,12},{9,13},{10,... | collective-permute-start | bytes 294920 | tf_op jit(solution)/shard_map/ppermute | solution.py:165
  5.6 9.3 %collective-permute-start.1 = (bf16[3,128,128]{2,1,0:T(8,128)(2,1)}, bf16[3,128,128]{2,1,0:T(8,128)(2,1)S(1)}, u32[]{:S(2)}, u32[]{:S(2)}) collective-permute-start(bf16[3,128,128]{2,1,0:T(8,128)(2,1)} %get-tuple-element.15), channel_id=1, source_target_pairs={{0,8},{1,9},{2,10},{3,11},{4,12},{5,13},{6,14},{7,15},{8,0},{9,1},... | collective-permute-start | bytes 294920 | tf_op jit(solution)/shard_map/ppermute | solution.py:165
  7.2 11.4 %collective-permute-start.2 = (bf16[3,128,128]{2,1,0:T(8,128)(2,1)}, bf16[3,128,128]{2,1,0:T(8,128)(2,1)S(1)}, u32[]{:S(2)}, u32[]{:S(2)}) collective-permute-start(bf16[3,128,128]{2,1,0:T(8,128)(2,1)} %get-tuple-element.16), channel_id=1, source_target_pairs={{0,12},{1,13},{2,14},{3,15},{4,8},{5,9},{6,10},{7,11},{8,4},{9,5},... | collective-permute-start | bytes 294920 | tf_op jit(solution)/shard_map/ppermute | solution.py:165
  7.2 18.5 %collective-permute-start.7 = (bf16[3,128,128]{2,1,0:T(8,128)(2,1)}, bf16[3,128,128]{2,1,0:T(8,128)(2,1)S(1)}, u32[]{:S(2)}, u32[]{:S(2)}) collective-permute-start(bf16[3,128,128]{2,1,0:T(8,128)(2,1)} %get-tuple-element.17), channel_id=1, source_target_pairs={{0,16},{1,17},{2,18},{3,19},{4,20},{5,21},{6,22},{7,23},{8,24},{9,... | collective-permute-start | bytes 294920 | tf_op jit(solution)/shard_map/ppermute | solution.py:165
  10.2 8.6 %collective-permute-start.3 = (bf16[3,128,128]{2,1,0:T(8,128)(2,1)}, bf16[3,128,128]{2,1,0:T(8,128)(2,1)S(1)}, u32[]{:S(2)}, u32[]{:S(2)}) collective-permute-start(bf16[3,128,128]{2,1,0:T(8,128)(2,1)} %get-tuple-element.13), channel_id=1, source_target_pairs={{0,1},{1,0},{2,3},{3,2},{4,5},{5,4},{6,7},{7,6},{8,9},{9,8},{10,11... | collective-permute-start | bytes 294920 | tf_op jit(solution)/shard_map/ppermute | solution.py:165
  13.5 12.7 %collective-permute-start.8 = (bf16[3,128,128]{2,1,0:T(8,128)(2,1)}, bf16[3,128,128]{2,1,0:T(8,128)(2,1)S(1)}, u32[]{:S(2)}, u32[]{:S(2)}) collective-permute-start(bf16[3,128,128]{2,1,0:T(8,128)(2,1)} %get-tuple-element.18), channel_id=1, source_target_pairs={{0,20},{1,21},{2,22},{3,23},{4,16},{5,17},{6,18},{7,19},{8,28},{9,... | collective-permute-start | bytes 294920 | tf_op jit(solution)/shard_map/ppermute | solution.py:165
  14.9 12.9 %collective-permute-start.9 = (bf16[3,128,128]{2,1,0:T(8,128)(2,1)}, bf16[3,128,128]{2,1,0:T(8,128)(2,1)S(1)}, u32[]{:S(2)}, u32[]{:S(2)}) collective-permute-start(bf16[3,128,128]{2,1,0:T(8,128)(2,1)} %get-tuple-element.19), channel_id=1, source_target_pairs={{0,24},{1,25},{2,26},{3,27},{4,28},{5,29},{6,30},{7,31},{8,16},{9,... | collective-permute-start | bytes 294920 | tf_op jit(solution)/shard_map/ppermute | solution.py:165
  18.6 9.7 %collective-permute-start.10 = (bf16[3,128,128]{2,1,0:T(8,128)(2,1)}, bf16[3,128,128]{2,1,0:T(8,128)(2,1)S(1)}, u32[]{:S(2)}, u32[]{:S(2)}) collective-permute-start(bf16[3,128,128]{2,1,0:T(8,128)(2,1)} %get-tuple-element.20), channel_id=1, source_target_pairs={{0,28},{1,29},{2,30},{3,31},{4,24},{5,25},{6,26},{7,27},{8,20},{9,... | collective-permute-start | bytes 294920 | tf_op jit(solution)/shard_map/ppermute | solution.py:165
  18.8 5.2 %collective-permute-start.4 = (bf16[3,128,128]{2,1,0:T(8,128)(2,1)S(1)}, bf16[3,128,128]{2,1,0:T(8,128)(2,1)S(1)}, u32[]{:S(2)}, u32[]{:S(2)}) collective-permute-start(bf16[3,128,128]{2,1,0:T(8,128)(2,1)S(1)} %collective-permute-done), channel_id=1, source_target_pairs={{0,1},{1,0},{2,3},{3,2},{4,5},{5,4},{6,7},{7,6},{8,9},{9,8},{10,11... | collective-permute-start | bytes 294920 | tf_op jit(solution)/shard_map/ppermute | solution.py:165
  24.1 5.7 %collective-permute-start.5 = (bf16[3,128,128]{2,1,0:T(8,128)(2,1)S(1)}, bf16[3,128,128]{2,1,0:T(8,128)(2,1)S(1)}, u32[]{:S(2)}, u32[]{:S(2)}) collective-permute-start(bf16[3,128,128]{2,1,0:T(8,128)(2,1)S(1)} %collective-permute-done.1), channel_id=1, source_target_pairs={{0,1},{1,0},{2,3},{3,2},{4,5},{5,4},{6,7},{7,6},{8,9},{9,8},{10,11... | collective-permute-start | bytes 294920 | tf_op jit(solution)/shard_map/ppermute | solution.py:165
  25.7 5.9 %collective-permute-start.6 = (bf16[3,128,128]{2,1,0:T(8,128)(2,1)S(1)}, bf16[3,128,128]{2,1,0:T(8,128)(2,1)S(1)}, u32[]{:S(2)}, u32[]{:S(2)}) collective-permute-start(bf16[3,128,128]{2,1,0:T(8,128)(2,1)S(1)} %collective-permute-done.2), channel_id=1, source_target_pairs={{0,1},{1,0},{2,3},{3,2},{4,5},{5,4},{6,7},{7,6},{8,9},{9,8},{10,11... | collective-permute-start | bytes 294920 | tf_op jit(solution)/shard_map/ppermute | solution.py:165
  26.2 7.4 %collective-permute-start.11 = (bf16[3,128,128]{2,1,0:T(8,128)(2,1)S(1)}, bf16[3,128,128]{2,1,0:T(8,128)(2,1)S(1)}, u32[]{:S(2)}, u32[]{:S(2)}) collective-permute-start(bf16[3,128,128]{2,1,0:T(8,128)(2,1)S(1)} %collective-permute-done.7), channel_id=1, source_target_pairs={{0,1},{1,0},{2,3},{3,2},{4,5},{5,4},{6,7},{7,6},{8,9},{9,8},{10,11... | collective-permute-start | bytes 294920 | tf_op jit(solution)/shard_map/ppermute | solution.py:165
  27.8 7.2 %collective-permute-start.12 = (bf16[3,128,128]{2,1,0:T(8,128)(2,1)S(1)}, bf16[3,128,128]{2,1,0:T(8,128)(2,1)S(1)}, u32[]{:S(2)}, u32[]{:S(2)}) collective-permute-start(bf16[3,128,128]{2,1,0:T(8,128)(2,1)S(1)} %collective-permute-done.8), channel_id=1, source_target_pairs={{0,1},{1,0},{2,3},{3,2},{4,5},{5,4},{6,7},{7,6},{8,9},{9,8},{10,11... | collective-permute-start | bytes 294920 | tf_op jit(solution)/shard_map/ppermute | solution.py:165
  28.2 7.8 %collective-permute-start.13 = (bf16[3,128,128]{2,1,0:T(8,128)(2,1)S(1)}, bf16[3,128,128]{2,1,0:T(8,128)(2,1)S(1)}, u32[]{:S(2)}, u32[]{:S(2)}) collective-permute-start(bf16[3,128,128]{2,1,0:T(8,128)(2,1)S(1)} %collective-permute-done.9), channel_id=1, source_target_pairs={{0,1},{1,0},{2,3},{3,2},{4,5},{5,4},{6,7},{7,6},{8,9},{9,8},{10,11... | collective-permute-start | bytes 294920 | tf_op jit(solution)/shard_map/ppermute | solution.py:165
  29.8 7.3 %collective-permute-start.14 = (bf16[3,128,128]{2,1,0:T(8,128)(2,1)S(1)}, bf16[3,128,128]{2,1,0:T(8,128)(2,1)S(1)}, u32[]{:S(2)}, u32[]{:S(2)}) collective-permute-start(bf16[3,128,128]{2,1,0:T(8,128)(2,1)S(1)} %collective-permute-done.10), channel_id=1, source_target_pairs={{0,1},{1,0},{2,3},{3,2},{4,5},{5,4},{6,7},{7,6},{8,9},{9,8},{10,11... | collective-permute-start | bytes 294920 | tf_op jit(solution)/shard_map/ppermute | solution.py:165
  31.6 8.2 %collective-permute-start.15 = (bf16[8,3,128,128]{3,2,1,0:T(8,128)(2,1)S(1)}, bf16[8,3,128,128]{3,2,1,0:T(8,128)(2,1)S(1)}, u32[]{:S(2)}, u32[]{:S(2)}) collective-permute-start(bf16[8,3,128,128]{3,2,1,0:T(8,128)(2,1)S(1)} %bitcast_dynamic-update-slice_fusion.refs_0_), channel_id=1, source_target_pairs={{0,2},{1,3},{2,0},{3,1},{4,6},{5,7},{6,4},{7,5},{8,10},{9,11},{10,... | collective-permute-start | bytes 2359304 | tf_op jit(solution)/shard_map/ppermute | solution.py:165
  33.7 6.1 %collective-permute-start.16 = (bf16[4,3,128,128]{3,2,1,0:T(8,128)(2,1)S(1)}, bf16[4,3,128,128]{3,2,1,0:T(8,128)(2,1)S(1)}, u32[]{:S(2)}, u32[]{:S(2)}) collective-permute-start(bf16[4,3,128,128]{3,2,1,0:T(8,128)(2,1)S(1)} %pad_maximum_fusion.refs_1_), channel_id=1, source_target_pairs={{0,2},{1,3},{2,0},{3,1},{4,6},{5,7},{6,4},{7,5},{8,10},{9,11},{10,... | collective-permute-start | bytes 1179656 | tf_op jit(solution)/shard_map/ppermute | solution.py:165
  37.2 2.6 %collective-permute-start.17 = (bf16[4,3,128,128]{3,2,1,0:T(8,128)(2,1)S(1)}, bf16[4,3,128,128]{3,2,1,0:T(8,128)(2,1)S(1)}, u32[]{:S(2)}, u32[]{:S(2)}) collective-permute-start(bf16[4,3,128,128]{3,2,1,0:T(8,128)(2,1)S(1)} %pad_maximum_fusion.1.refs_2_), channel_id=1, source_target_pairs={{0,2},{1,3},{2,0},{3,1},{4,6},{5,7},{6,4},{7,5},{8,10},{9,11},{10,... | collective-permute-start | bytes 1179656 | tf_op jit(solution)/shard_map/ppermute | solution.py:165
where the time goes:
time: 54.4 us; the launch traced here: 54.2 us
  starting transfers between devices  22.9 us (42%)
  Pallas kernels  16.9 us (31%)
  waiting for transfers between devices  9.75 us (18%)
  local copies, waits for them, and re-layouts  4.36 us (8%)
    ppermute x18, starting transfers between devices, send(): return lax.ppermute(x, BOTH, pairs)  22.9 us
    pallas_call x1, Pallas kernels, ladder(): pl.pallas_call(functools.partial(ladder_kernel, dims), out_shape=jax.Shap...  14.3 us
    ppermute x18, waiting for transfers between devices, send(): return lax.ppermute(x, BOTH, pairs)  9.75 us
    pallas_call x1, Pallas kernels, pick(): pl.pallas_call(functools.partial(pick_kernel, tile_dev, group), out_shape...  2.55 us
    dynamic_slice x1, local copies, waits for them, and re-layouts, direct(): lax.dynamic_slice_in_dim(amplitudes, lax.axis_index('cuts') * rows, rows, 0)  1.83 us
  transfers between devices with their start and end apart: 18, of which 6 were waited for; matrix products, arithmetic and copies ran while one was open for 8% of the time, Pallas kernels for 0%

commit v1 on v0

--- a/solution.py
+++ b/solution.py
@@ -14,22 +14,16 @@
 VMEM = pl.BlockSpec(memory_space=pltpu.VMEM)
 
 
-def pick_kernel(tile_dev, group, screening, tile_slot, factors, *refs):
-    outs, sems = refs[:-1], refs[-1]
+def pick_kernel(tile_dev, group, screening, tile_slot, factors, *outs):
     count = screening.shape[1]
     me = lax.axis_index("pair")
-    copies = []
     for shift, out in enumerate(outs):
         peer = (me // group) ^ shift
         local = jnp.int32(0)
         for t in range(count):
             slot = tile_slot[screening[peer, t]]
             local = jnp.where(slot // tile_dev == me, slot % tile_dev, local)
-        copy = pltpu.make_async_copy(factors.at[local], out, sems.at[shift])
-        copy.start()
-        copies.append(copy)
-    for copy in copies:
-        copy.wait()
+        out[...] = factors[local]
 
 
 def pick(screening, tile_slot, factors, group, shifts):
@@ -38,46 +32,45 @@
         functools.partial(pick_kernel, tile_dev, group),
         out_shape=[jax.ShapeDtypeStruct(tail, factors.dtype)] * shifts,
         in_specs=[SMEM, SMEM, VMEM],
-        out_specs=[ANY] * shifts,
-        scratch_shapes=[pltpu.SemaphoreType.DMA((shifts,))],
+        out_specs=[VMEM] * shifts,
+        compiler_params=pltpu.CompilerParams(vmem_limit_bytes=8 * 2**20),
         name="pick",
     )(screening, tile_slot, factors)
 
 
-def ladder_kernel(
-    dims, screening, tile_slot, occ, virt, amp, *refs
-):
-    tile_dev, group, row_tiles, shifts, n_q, tile, wide = dims
-    mine, other, (out, left, row_den, held, sem, out_sem) = refs[:3], refs[3:6], refs[6:]
+def ladder_kernel(dims, last, screening, tile_slot, occ, virt, amp, *refs):
+    tile_dev, group, row_tiles, shifts, tile, wide = dims
+    (near, far, near_other, far_other), refs = refs[:4], refs[4:]
+    if last:
+        before, out, left, row_den, held, out_sem = refs
+    else:
+        out, left = refs
     me, cut = lax.axis_index("pair"), lax.axis_index("cuts")
     pair_id, core = me // group, me % group
-    count = screening.shape[1]
+    count, n_q = screening.shape[1], left.shape[1]
     first = core * (count // group) + cut * row_tiles
-    half_q, half_s = n_q // 2, shifts // 2
+    half = shifts // 2
 
     for t in range(count):
         slot = tile_slot[screening[pair_id, t]]
         owner = slot // tile_dev
         shift = (owner // group) ^ pair_id
         same = owner % group == core
-        near = shift < half_s
-        far = shift - half_s
-        for part in range(2):
-            dst = left.at[t, pl.ds(part * half_q, half_q)]
-            for held_by, bufs in ((same, mine), (jnp.logical_not(same), other)):
-
-                @pl.when(held_by & near)
-                def _():
-                    pltpu.make_async_copy(bufs[0].at[part * half_s + shift], dst, sem).start()
-
-                @pl.when(held_by & jnp.logical_not(near))
-                def _():
-                    pltpu.make_async_copy(bufs[1 + part].at[far], dst, sem).start()
-
-    for i in range(row_tiles):
-        row = virt[pl.ds(screening[pair_id, first + i], 1), :] - occ[0]
-        row_den[i] = jnp.broadcast_to(row, (tile, tile)).T
-    pltpu.make_async_copy(left, left, sem).wait()
+        close = shift < half
+        for bufs, held_by in (((near, far), same), ((near_other, far_other), jnp.logical_not(same))):
+
+            @pl.when(held_by & close)
+            def _():
+                left[t] = bufs[0][shift]
+
+            @pl.when(held_by & jnp.logical_not(close))
+            def _():
+                left[t] = bufs[1][shift - half]
+
+    if last:
+        for i in range(row_tiles):
+            row = virt[pl.ds(screening[pair_id, first + i], 1), :] - occ[0]
+            row_den[i] = jnp.broadcast_to(row, (tile, tile)).T
 
     def write(step, slot):
         at = pl.ds(pl.multiple_of(step * wide, wide), wide)
@@ -88,17 +81,20 @@
     @pl.loop(0, steps)
     def _(step):
         slot = step % 2
-
-        @pl.when(step >= 2)
-        def _():
-            write(step - 2, slot).wait()
+        base = pl.multiple_of(step * wide, wide)
+
+        if last:
+
+            @pl.when(step >= 2)
+            def _():
+                write(step - 2, slot).wait()
 
         halves = []
         for i in range(row_tiles):
             lhs = left[first + i].reshape(n_q * tile, tile)
-            block = amp[i * tile : (i + 1) * tile, pl.ds(pl.multiple_of(step * wide, wide), wide)]
-            half = jnp.dot(lhs, block, preferred_element_type=jnp.float32)
-            halves.append(half.astype(jnp.bfloat16))
+            block = amp[i * tile : (i + 1) * tile, pl.ds(base, wide)]
+            half_done = jnp.dot(lhs, block, preferred_element_type=jnp.float32)
+            halves.append(half_done.astype(jnp.bfloat16))
         for j in range(wide // tile):
             col = step * (wide // tile) + j
             cols = slice(j * tile, (j + 1) * tile)
@@ -115,43 +111,66 @@
             acc = lax.dot_general(
                 lhs, rhs, (((1,), (1,)), ((), ())), preferred_element_type=jnp.float32
             )
+            at = pl.ds(pl.multiple_of(base + j * tile, tile), tile)
+            if not last:
+                out[:, at] = acc
+                continue
+            acc = acc + before[:, at]
             col_e = virt[pl.ds(screening[pair_id, col], 1), :] - occ[1]
             for i in range(row_tiles):
                 rows = slice(i * tile, (i + 1) * tile)
                 held[slot, rows, cols] = acc[rows] / (row_den[i] + col_e)
-        write(step, slot).start()
-
-    for step in range(max(0, steps - 2), steps):
-        write(step, step % 2).wait()
-
-
-def ladder(screening, tile_slot, occ, virt, amp, mine, other, dims):
-    _, _, row_tiles, _, n_q, tile, wide = dims
+        if last:
+            write(step, slot).start()
+
+    if last:
+        for step in range(max(0, steps - 2), steps):
+            write(step, step % 2).wait()
+
+
+def ladder(screening, tile_slot, occ, virt, amp, tiles, dims, before=None):
+    _, _, row_tiles, _, tile, wide = dims
     rows, columns = amp.shape
-    return pl.pallas_call(
-        functools.partial(ladder_kernel, dims),
-        out_shape=jax.ShapeDtypeStruct((rows, columns), jnp.float32),
-        in_specs=[SMEM, SMEM, SMEM, VMEM, VMEM] + [ANY] * 6,
-        out_specs=ANY,
-        scratch_shapes=[
-            pltpu.VMEM((screening.shape[1], n_q, tile, tile), jnp.bfloat16),
+    last = before is not None
+    n_q = tiles[0].shape[1]
+    scratch = [pltpu.VMEM((screening.shape[1], n_q, tile, tile), jnp.bfloat16)]
+    if last:
+        scratch += [
             pltpu.VMEM((row_tiles, tile, tile), jnp.float32),
             pltpu.VMEM((2, rows, wide), jnp.float32),
-            pltpu.SemaphoreType.DMA,
             pltpu.SemaphoreType.DMA((2,)),
-        ],
-        compiler_params=pltpu.CompilerParams(vmem_limit_bytes=24 * 2**20),
-        name="ladder",
-    )(screening, tile_slot, occ, virt, amp, *mine, *other)
+        ]
+    extra = [before] if last else []
+    flops = 4 * n_q * rows * columns * tile
+    return pl.pallas_call(
+        functools.partial(ladder_kernel, dims, last),
+        out_shape=jax.ShapeDtypeStruct((rows, columns), jnp.float32),
+        in_specs=[SMEM, SMEM, SMEM] + [VMEM] * (6 + len(extra)),
+        out_specs=ANY if last else VMEM,
+        scratch_shapes=scratch,
+        compiler_params=pltpu.CompilerParams(vmem_limit_bytes=(16 if last else 12) * 2**20),
+        cost_estimate=pl.CostEstimate(flops=flops, bytes_accessed=0, transcendentals=0),
+        name="ladder_last" if last else "ladder_first",
+    )(screening, tile_slot, occ, virt, amp, *tiles, *extra)
+
+
+def crossings(shifts):
+    near = [[s, s + 1] for s in range(2, shifts // 2, 2)]
+    far = [[s, s + 1] for s in range(shifts // 2, shifts, 2)]
+    groups = [[0], [1]]
+    while near or far:
+        groups += [x.pop(0) for x in (far, near) if x and (x is near or len(x) > 1 or not near)]
+    return groups
 
 
 def direct(
     amplitudes, factors, screening, tile_slot, pair_orbitals, occupied_energy, virtual_energy
 ):
-    tile_dev, q_cut, tile, _ = factors.shape
+    tile_dev, _, tile, _ = factors.shape
     n_pair, n_cut = lax.axis_size("pair"), lax.axis_size("cuts")
     group = n_pair // screening.shape[0]
     shifts = n_pair // group
+    half = shifts // 2
     row_tiles = amplitudes.shape[0] // tile // n_cut
     me = lax.axis_index("pair")
 
@@ -164,27 +183,31 @@
         ]
         return lax.ppermute(x, BOTH, pairs)
 
+    def over(x):
+        return send(x, lambda p, c: (p ^ 1, c))
+
     picked = pick(screening, tile_slot, factors, group, shifts)
-    got = [picked[0]] + [None] * (shifts - 1)
-    for s in range(1, shifts):
-        got[s] = send(picked[s], lambda p, c: (p ^ (s * group), c))
-    crossed = []
-    for s in range(shifts):
-        crossed.append(send(got[s], lambda p, c: (p, c ^ 1)))
-    half = shifts // 2
-    mine = [
-        jnp.stack(got[:half] + crossed[:half]),
-        jnp.stack(got[half:]),
-        jnp.stack(crossed[half:]),
+    got = [picked[0]] + [
+        send(picked[s], lambda p, c: (p ^ (s * group), c))
+        for s in range(1, shifts)
     ]
-    other = []
-    for x in mine:
-        other.append(send(x, lambda p, c: (p ^ 1, c)))
+    crossed = [None] * shifts
+    for members in crossings(shifts):
+        x = jnp.stack([got[s] for s in members])
+        x = send(x, lambda p, c: (p, c ^ 1))
+        for n, s in enumerate(members):
+            crossed[s] = x[n]
     occ = occupied_energy[pair_orbitals[me // group]]
     rows = row_tiles * tile
     amp = lax.dynamic_slice_in_dim(amplitudes, lax.axis_index("cuts") * rows, rows, 0)
-    dims = (tile_dev, group, row_tiles, shifts, q_cut * n_cut, tile, 2 * tile)
-    return ladder(screening, tile_slot, occ, virtual_energy, amp, mine, other, dims)
+    dims = (tile_dev, group, row_tiles, shifts, tile, 2 * tile)
+    out = None
+    for held in (got, crossed):
+        near = jnp.stack(held[:half])
+        far = jnp.stack(held[half:])
+        tiles = [near, far, over(near), over(far)]
+        out = ladder(screening, tile_slot, occ, virtual_energy, amp, tiles, dims, out)
+    return out
 
 
 def general(

time: 54.4 us -> 57.2 us (1.051)
  waiting for transfers between devices: 9.75 us -> 17.4 us
  starting transfers between devices: 22.9 us -> 19.4 us
  Pallas kernels: 16.9 us -> 15.7 us
    ppermute x18 -> x16, waiting for transfers between devices: 9.75 us -> 17.4 us  [send(): return lax.ppermute(x, BOTH, pairs)]
    ppermute x18 -> x16, starting transfers between devices: 22.9 us -> 19.4 us  [send(): return lax.ppermute(x, BOTH, pairs)]
    dynamic_slice x1, local copies, waits for them, and re-layouts: 1.83 us -> 0.24 us  [direct(): lax.dynamic_slice_in_dim(amplitudes, lax.axis_index('cuts') * rows, rows, 0)]
    unnamed x15 -> x19, local copies, waits for them, and re-layouts: 1.03 us -> 2.34 us
    pallas_call x1, Pallas kernels: 2.55 us -> 1.45 us  [pick(): pl.pallas_call(functools.partial(pick_kernel, tile_dev, group), out_shape...]
    pallas_call x1 -> x2, Pallas kernels: 14.3 us -> 14.3 us  [ladder(): pl.pallas_call(functools.partial(ladder_kernel, dims, last), out_shape=ja...]
  transfers between devices with their start and end apart: 18 -> 16, of which waited for: 6 -> 5; matrix products, arithmetic and copies ran while one was open for 8% -> 4% of each run, Pallas kernels for 0% -> 11%
where the time goes in v1:
time: 57.2 us; the launch traced here: 57 us
  starting transfers between devices  19.4 us (34%)
  waiting for transfers between devices  17.4 us (30%)
  Pallas kernels  15.7 us (27%)
  local copies, waits for them, and re-layouts  4.12 us (7%)
    ppermute x16, starting transfers between devices, send(): return lax.ppermute(x, BOTH, pairs)  19.4 us
    ppermute x16, waiting for transfers between devices, send(): return lax.ppermute(x, BOTH, pairs)  17.4 us
    pallas_call x2, Pallas kernels, ladder(): pl.pallas_call(functools.partial(ladder_kernel, dims, last), out_shape=ja...  14.3 us
    unnamed x19, local copies, waits for them, and re-layouts  2.34 us
    pallas_call x1, Pallas kernels, pick(): pl.pallas_call(functools.partial(pick_kernel, tile_dev, group), out_shape...  1.45 us
  transfers between devices with their start and end apart: 16, of which 5 were waited for; matrix products, arithmetic and copies ran while one was open for 4% of the time, Pallas kernels for 11%

profile of v1, /device:TPU:0, one launch (start us, length us, event | category | flops | bytes accessed | tf_op | source)
XLA Modules:
  0.0 57.0 jit_solution(12219995058202413543)
XLA Ops:
  0.0 0.0 copy-start
  0.0 0.9 %copy-done.1 = bf16[2,3,128,128]{3,2,1,0:T(8,128)(2,1)S(1)} copy-done((bf16[2,3,128,128]{3,2,1,0:T(8,128)(2,1)S(1)}, bf16[2,3,128,128]{3,2,1,0:T(8,128)(2,1)}, u32[]{:S(2)}) %copy-start.1) | copy-done | bytes 196632
  0.9 0.7 %copy-done.3 = s32[8,16]{1,0:T(8,128)S(1)} copy-done((s32[8,16]{1,0:T(8,128)S(1)}, s32[8,16]{1,0:T(8,128)}, u32[]{:S(2)}) %copy-start.3) | copy-done | bytes 536
  1.6 0.7 %copy-done.5 = s32[32]{0:T(128)S(1)} copy-done((s32[32]{0:T(128)S(1)}, s32[32]{0:T(128)}, u32[]{:S(2)}) %copy-start.5) | copy-done | bytes 152
  2.3 1.4 %pick.1 = (bf16[3,128,128]{2,1,0:T(8,128)(2,1)S(1)}, bf16[3,128,128]{2,1,0:T(8,128)(2,1)S(1)}, bf16[3,128,128]{2,1,0:T(8,128)(2,1)S(1)}, bf16[3,128,128]{2,1,0:T...) custom-call(s32[8,16]{1,0:T(8,128)S(1)} %copy-done.3, ...), custom_call_target="tpu_custom_call" | custom-call | tf_op jit(solution)/shard_map/pick/pallas_call | solution.py:31
  3.7 3.1 %collective-permute-start = (bf16[1,3,128,128]{3,2,1,0:T(8,128)(2,1)S(1)}, bf16[1,3,128,128]{3,2,1,0:T(8,128)(2,1)S(1)}, u32[]{:S(2)}, u32[]{:S(2)}) collective-permute-start(bf16[1,3,128,128]{3,2,1,0:T(8,128)(2,1)S(1)} %bitcast.12), channel_id=1, source_target_pairs={{0,1},{1,0},{2,3},{3,2},{4,5},{5,4},{6,7},{7,6},{8,9},{9,8},{10,11... | collective-permute-start | bytes 294920 | tf_op jit(solution)/shard_map/ppermute | solution.py:184
  6.8 1.5 %collective-permute-start.1 = (bf16[3,128,128]{2,1,0:T(8,128)(2,1)S(1)}, bf16[3,128,128]{2,1,0:T(8,128)(2,1)S(1)}, u32[]{:S(2)}, u32[]{:S(2)}) collective-permute-start(bf16[3,128,128]{2,1,0:T(8,128)(2,1)S(1)} %get-tuple-element.14), channel_id=1, source_target_pairs={{0,4},{1,5},{2,6},{3,7},{4,0},{5,1},{6,2},{7,3},{8,12},{9,13},{10,... | collective-permute-start | bytes 294920 | tf_op jit(solution)/shard_map/ppermute | solution.py:184
  8.3 1.6 %collective-permute-start.3 = (bf16[3,128,128]{2,1,0:T(8,128)(2,1)S(1)}, bf16[3,128,128]{2,1,0:T(8,128)(2,1)S(1)}, u32[]{:S(2)}, u32[]{:S(2)}) collective-permute-start(bf16[3,128,128]{2,1,0:T(8,128)(2,1)S(1)} %get-tuple-element.15), channel_id=1, source_target_pairs={{0,8},{1,9},{2,10},{3,11},{4,12},{5,13},{6,14},{7,15},{8,0},{9,1},... | collective-permute-start | bytes 294920 | tf_op jit(solution)/shard_map/ppermute | solution.py:184
  9.9 2.6 %collective-permute-start.6 = (bf16[3,128,128]{2,1,0:T(8,128)(2,1)S(1)}, bf16[3,128,128]{2,1,0:T(8,128)(2,1)S(1)}, u32[]{:S(2)}, u32[]{:S(2)}) collective-permute-start(bf16[3,128,128]{2,1,0:T(8,128)(2,1)S(1)} %get-tuple-element.17), channel_id=1, source_target_pairs={{0,16},{1,17},{2,18},{3,19},{4,20},{5,21},{6,22},{7,23},{8,24},{9,... | collective-permute-start | bytes 294920 | tf_op jit(solution)/shard_map/ppermute | solution.py:184
  12.5 0.3 collective-permute-start.7
  12.8 0.9 %dynamic-slice_reduce_fusion = s32[2]{0:T(128)S(1)} fusion(s32[8,2]{0,1:T(2,128)} %param.11, s32[]{:T(128)S(6)} %select_n.22), kind=kLoop, calls=%fused_computation.13 | loop fusion | bytes 20 | tf_op jit(solution)/shard_map/dynamic_slice | solution.py:200
  13.6 0.0 copy-done
  13.7 0.6 %gather_fusion = f32[2]{0:T(128)S(1)} fusion(f32[4000]{0:T(1024)S(1)} %copy-done, s32[1024]{0:T(1024)S(1)} %pad_clamp_fusion), kind=kCustom, calls=%fused_computation | custom fusion | bytes 24 | tf_op jit(solution)/shard_map/gather | solution.py:200
  14.3 5.3 %collective-permute-done.6 = bf16[3,128,128]{2,1,0:T(8,128)(2,1)S(1)} collective-permute-done((bf16[3,128,128]{2,1,0:T(8,128)(2,1)S(1)}, bf16[3,128,128]{2,1,0:T(8,128)(2,1)S(1)}, u32[]{:S(2)}, u32[]{:S(2)}) %collective-permute-start.6) | collective-permute-done | bytes 98336 | tf_op jit(solution)/shard_map/ppermute | solution.py:184
  19.6 0.0 collective-permute-start.4
  19.6 1.2 %collective-permute-done.7 = bf16[3,128,128]{2,1,0:T(8,128)(2,1)S(1)} collective-permute-done((bf16[3,128,128]{2,1,0:T(8,128)(2,1)S(1)}, bf16[3,128,128]{2,1,0:T(8,128)(2,1)S(1)}, u32[]{:S(2)}, u32[]{:S(2)}) %collective-permute-start.7) | collective-permute-done | bytes 98336 | tf_op jit(solution)/shard_map/ppermute | solution.py:184
  20.8 2.4 %collective-permute-start.9 = (bf16[3,128,128]{2,1,0:T(8,128)(2,1)S(1)}, bf16[3,128,128]{2,1,0:T(8,128)(2,1)S(1)}, u32[]{:S(2)}, u32[]{:S(2)}) collective-permute-start(bf16[3,128,128]{2,1,0:T(8,128)(2,1)S(1)} %get-tuple-element.19), channel_id=1, source_target_pairs={{0,24},{1,25},{2,26},{3,27},{4,28},{5,29},{6,30},{7,31},{8,16},{9,... | collective-permute-start | bytes 294920 | tf_op jit(solution)/shard_map/ppermute | solution.py:184
  23.3 0.0 collective-permute-done.1
  23.3 2.6 %collective-permute-start.10 = (bf16[3,128,128]{2,1,0:T(8,128)(2,1)S(1)}, bf16[3,128,128]{2,1,0:T(8,128)(2,1)S(1)}, u32[]{:S(2)}, u32[]{:S(2)}) collective-permute-start(bf16[3,128,128]{2,1,0:T(8,128)(2,1)S(1)} %get-tuple-element.20), channel_id=1, source_target_pairs={{0,28},{1,29},{2,30},{3,31},{4,24},{5,25},{6,26},{7,27},{8,20},{9,... | collective-permute-start | bytes 294920 | tf_op jit(solution)/shard_map/ppermute | solution.py:184
  25.9 0.0 collective-permute-done.3
  25.9 0.5 collective-permute-start.2
  26.4 0.0 collective-permute-done.4
  26.4 1.5 %collective-permute-start.8 = (bf16[2,3,128,128]{3,2,1,0:T(8,128)(2,1)S(1)}, bf16[2,3,128,128]{3,2,1,0:T(8,128)(2,1)S(1)}, u32[]{:S(2)}, u32[]{:S(2)}) collective-permute-start(bf16[2,3,128,128]{3,2,1,0:T(8,128)(2,1)S(1)} %pad_maximum_fusion.3), channel_id=1, source_target_pairs={{0,1},{1,0},{2,3},{3,2},{4,5},{5,4},{6,7},{7,6},{8,9},{9,8},{10,11... | collective-permute-start | bytes 589832 | tf_op jit(solution)/shard_map/ppermute | solution.py:184
  27.9 0.1 pad_maximum_fusion.refs_0_
  28.0 0.1 collective-permute-done.9
  28.1 2.7 %collective-permute-done.10 = bf16[3,128,128]{2,1,0:T(8,128)(2,1)S(1)} collective-permute-done((bf16[3,128,128]{2,1,0:T(8,128)(2,1)S(1)}, bf16[3,128,128]{2,1,0:T(8,128)(2,1)S(1)}, u32[]{:S(2)}, u32[]{:S(2)}) %collective-permute-start.10) | collective-permute-done | bytes 98336 | tf_op jit(solution)/shard_map/ppermute | solution.py:184
  30.8 0.6 %collective-permute-start.11 = (bf16[2,3,128,128]{3,2,1,0:T(8,128)(2,1)S(1)}, bf16[2,3,128,128]{3,2,1,0:T(8,128)(2,1)S(1)}, u32[]{:S(2)}, u32[]{:S(2)}) collective-permute-start(bf16[2,3,128,128]{3,2,1,0:T(8,128)(2,1)S(1)} %pad_maximum_fusion.4), channel_id=1, source_target_pairs={{0,1},{1,0},{2,3},{3,2},{4,5},{5,4},{6,7},{7,6},{8,9},{9,8},{10,11... | collective-permute-start | bytes 589832 | tf_op jit(solution)/shard_map/ppermute | solution.py:184
  31.4 1.5 %collective-permute-start.5 = (bf16[2,3,128,128]{3,2,1,0:T(8,128)(2,1)S(1)}, bf16[2,3,128,128]{3,2,1,0:T(8,128)(2,1)S(1)}, u32[]{:S(2)}, u32[]{:S(2)}) collective-permute-start(bf16[2,3,128,128]{3,2,1,0:T(8,128)(2,1)S(1)} %pad_maximum_fusion.2), channel_id=1, source_target_pairs={{0,1},{1,0},{2,3},{3,2},{4,5},{5,4},{6,7},{7,6},{8,9},{9,8},{10,11... | collective-permute-start | bytes 589832 | tf_op jit(solution)/shard_map/ppermute | solution.py:184
  32.9 0.1 pad_maximum_fusion.1.refs_1_
  32.9 0.0 collective-permute-done
  32.9 0.1 collective-permute-start.15
  33.0 0.0 collective-permute-done.2
  33.0 0.5 collective-permute-start.14
  33.6 8.1 %collective-permute-done.5 = bf16[2,3,128,128]{3,2,1,0:T(8,128)(2,1)S(1)} collective-permute-done((bf16[2,3,128,128]{3,2,1,0:T(8,128)(2,1)S(1)}, bf16[2,3,128,128]{3,2,1,0:T(8,128)(2,1)S(1)}, u32[]{:S(2)}, u32[]{:S(2)}) %collective-permute-start.5) | collective-permute-done | bytes 196640 | tf_op jit(solution)/shard_map/ppermute | solution.py:184
  41.7 0.1 collective-permute-start.12
  41.8 0.0 collective-permute-done.8
  41.8 0.0 collective-permute-done.11
  41.9 0.6 collective-permute-start.13
  42.4 0.0 copy-done.7
  42.4 0.2 constant_dynamic-slice_fusion.amp
  42.7 0.0 collective-permute-done.15.refs_3_
  42.7 0.0 collective-permute-done.14.refs_2_
  42.7 0.0 copy-done.2
  42.7 0.0 copy-done.4
  42.7 6.4 %ladder_first.1.refs_4_ = f32[512,2048]{1,0:T(8,128)S(1)} custom-call(s32[8,16]{1,0:T(8,128)S(1)} %copy-done.4, s32[32]{0:T(128)S(1)} %copy-done.6, f32[2]{0:T(128)S(1)} %gather_fusion, f32[32,128]{1,0:T(8,128)S(1)} %copy-done.2, bf16[512,2048]{1,0:T(8,128)(2,1)S(1)} %constant_dynamic-slice_fusion.amp, bf16[4,3,128,128]{3,2,1,0:T(8,128)(2,1)S(1)} %pad_maximum_fusion.refs_0_, ...), custom_call_target="tpu_custom_call" | custom-call | flops 1610612736 | tf_op jit(solution)/shard_map/ladder_first/pallas_call | solution.py:145
  49.1 0.0 collective-permute-done.12.refs_2_
  49.1 0.0 collective-permute-done.13.refs_3_
  49.1 7.9 %ladder_last.1 = f32[512,2048]{1,0:T(8,128)} custom-call(s32[8,16]{1,0:T(8,128)S(1)} %copy-done.4, s32[32]{0:T(128)S(1)} %copy-done.6, f32[2]{0:T(128)S(1)} %gather_fusion, f32[32,128]{1,0:T(8,128)S(1)} %copy-done.2, bf16[512,2048]{1,0:T(8,128)(2,1)S(1)} %constant_dynamic-slice_fusion.amp, ...), custom_call_target="tpu_custom_call" | custom-call | flops 1610612736 | tf_op jit(solution)/shard_map/ladder_last/pallas_call | solution.py:145
  (18 shorter events, 0.2 us)
Async XLA Ops:
  0.0 13.7 %copy-start = (f32[4000]{0:T(1024)S(1)}, f32[4000]{0:T(1024)}, u32[]{:S(2)}) copy-start(f32[4000]{0:T(1024)} %param.12) | copy-start | bytes 48004
  0.0 0.9 %copy-start.1 = (bf16[2,3,128,128]{3,2,1,0:T(8,128)(2,1)S(1)}, bf16[2,3,128,128]{3,2,1,0:T(8,128)(2,1)}, u32[]{:S(2)}) copy-start(bf16[2,3,128,128]{3,2,1,0:T(8,128)(2,1)} %factors.1) | copy-start | bytes 589828
  0.9 0.7 %copy-start.3 = (s32[8,16]{1,0:T(8,128)S(1)}, s32[8,16]{1,0:T(8,128)}, u32[]{:S(2)}) copy-start(s32[8,16]{1,0:T(8,128)} %screening.5) | copy-start | bytes 1540
  1.6 0.7 %copy-start.5 = (s32[32]{0:T(128)S(1)}, s32[32]{0:T(128)}, u32[]{:S(2)}) copy-start(s32[32]{0:T(128)} %tile_slot.5) | copy-start | bytes 388
  3.7 29.2 %collective-permute-start = (bf16[1,3,128,128]{3,2,1,0:T(8,128)(2,1)S(1)}, bf16[1,3,128,128]{3,2,1,0:T(8,128)(2,1)S(1)}, u32[]{:S(2)}, u32[]{:S(2)}) collective-permute-start(bf16[1,3,128,128]{3,2,1,0:T(8,128)(2,1)S(1)} %bitcast.12), channel_id=1, source_target_pairs={{0,1},{1,0},{2,3},{3,2},{4,5},{5,4},{6,7},{7,6},{8,9},{9,8},{10,11... | collective-permute-start | bytes 294920 | tf_op jit(solution)/shard_map/ppermute | solution.py:184
  6.8 16.5 %collective-permute-start.1 = (bf16[3,128,128]{2,1,0:T(8,128)(2,1)S(1)}, bf16[3,128,128]{2,1,0:T(8,128)(2,1)S(1)}, u32[]{:S(2)}, u32[]{:S(2)}) collective-permute-start(bf16[3,128,128]{2,1,0:T(8,128)(2,1)S(1)} %get-tuple-element.14), channel_id=1, source_target_pairs={{0,4},{1,5},{2,6},{3,7},{4,0},{5,1},{6,2},{7,3},{8,12},{9,13},{10,... | collective-permute-start | bytes 294920 | tf_op jit(solution)/shard_map/ppermute | solution.py:184
  8.3 17.6 %collective-permute-start.3 = (bf16[3,128,128]{2,1,0:T(8,128)(2,1)S(1)}, bf16[3,128,128]{2,1,0:T(8,128)(2,1)S(1)}, u32[]{:S(2)}, u32[]{:S(2)}) collective-permute-start(bf16[3,128,128]{2,1,0:T(8,128)(2,1)S(1)} %get-tuple-element.15), channel_id=1, source_target_pairs={{0,8},{1,9},{2,10},{3,11},{4,12},{5,13},{6,14},{7,15},{8,0},{9,1},... | collective-permute-start | bytes 294920 | tf_op jit(solution)/shard_map/ppermute | solution.py:184
  9.9 9.8 %collective-permute-start.6 = (bf16[3,128,128]{2,1,0:T(8,128)(2,1)S(1)}, bf16[3,128,128]{2,1,0:T(8,128)(2,1)S(1)}, u32[]{:S(2)}, u32[]{:S(2)}) collective-permute-start(bf16[3,128,128]{2,1,0:T(8,128)(2,1)S(1)} %get-tuple-element.17), channel_id=1, source_target_pairs={{0,16},{1,17},{2,18},{3,19},{4,20},{5,21},{6,22},{7,23},{8,24},{9,... | collective-permute-start | bytes 294920 | tf_op jit(solution)/shard_map/ppermute | solution.py:184
  12.5 8.3 %collective-permute-start.7 = (bf16[3,128,128]{2,1,0:T(8,128)(2,1)S(1)}, bf16[3,128,128]{2,1,0:T(8,128)(2,1)S(1)}, u32[]{:S(2)}, u32[]{:S(2)}) collective-permute-start(bf16[3,128,128]{2,1,0:T(8,128)(2,1)S(1)} %get-tuple-element.18), channel_id=1, source_target_pairs={{0,20},{1,21},{2,22},{3,23},{4,16},{5,17},{6,18},{7,19},{8,28},{9,... | collective-permute-start | bytes 294920 | tf_op jit(solution)/shard_map/ppermute | solution.py:184
  14.3 28.1 %copy-start.7 = (bf16[1024,2048]{1,0:T(8,128)(2,1)S(1)}, bf16[1024,2048]{1,0:T(8,128)(2,1)}, u32[]{:S(2)}) copy-start(bf16[1024,2048]{1,0:T(8,128)(2,1)} %param.7) | copy-start | bytes 12582916
  19.6 6.7 %collective-permute-start.4 = (bf16[3,128,128]{2,1,0:T(8,128)(2,1)S(1)}, bf16[3,128,128]{2,1,0:T(8,128)(2,1)S(1)}, u32[]{:S(2)}, u32[]{:S(2)}) collective-permute-start(bf16[3,128,128]{2,1,0:T(8,128)(2,1)S(1)} %get-tuple-element.16), channel_id=1, source_target_pairs={{0,12},{1,13},{2,14},{3,15},{4,8},{5,9},{6,10},{7,11},{8,4},{9,5},... | collective-permute-start | bytes 294920 | tf_op jit(solution)/shard_map/ppermute | solution.py:184
  20.8 7.3 %collective-permute-start.9 = (bf16[3,128,128]{2,1,0:T(8,128)(2,1)S(1)}, bf16[3,128,128]{2,1,0:T(8,128)(2,1)S(1)}, u32[]{:S(2)}, u32[]{:S(2)}) collective-permute-start(bf16[3,128,128]{2,1,0:T(8,128)(2,1)S(1)} %get-tuple-element.19), channel_id=1, source_target_pairs={{0,24},{1,25},{2,26},{3,27},{4,28},{5,29},{6,30},{7,31},{8,16},{9,... | collective-permute-start | bytes 294920 | tf_op jit(solution)/shard_map/ppermute | solution.py:184
  23.2 19.4 %copy-start.2 = (f32[32,128]{1,0:T(8,128)S(1)}, f32[32,128]{1,0:T(8,128)}, u32[]{:S(2)}) copy-start(f32[32,128]{1,0:T(8,128)} %virt.3) | copy-start | bytes 49156
  23.2 19.4 %copy-start.4 = (s32[8,16]{1,0:T(8,128)S(1)}, s32[8,16]{1,0:T(8,128)}, u32[]{:S(2)}) copy-start(s32[8,16]{1,0:T(8,128)} %screening.5) | copy-start | bytes 1540
  23.2 19.5 %copy-start.6 = (s32[32]{0:T(128)S(1)}, s32[32]{0:T(128)}, u32[]{:S(2)}) copy-start(s32[32]{0:T(128)} %tile_slot.5) | copy-start | bytes 388
  23.3 7.5 %collective-permute-start.10 = (bf16[3,128,128]{2,1,0:T(8,128)(2,1)S(1)}, bf16[3,128,128]{2,1,0:T(8,128)(2,1)S(1)}, u32[]{:S(2)}, u32[]{:S(2)}) collective-permute-start(bf16[3,128,128]{2,1,0:T(8,128)(2,1)S(1)} %get-tuple-element.20), channel_id=1, source_target_pairs={{0,28},{1,29},{2,30},{3,31},{4,24},{5,25},{6,26},{7,27},{8,20},{9,... | collective-permute-start | bytes 294920 | tf_op jit(solution)/shard_map/ppermute | solution.py:184
  25.9 7.2 %collective-permute-start.2 = (bf16[1,3,128,128]{3,2,1,0:T(8,128)(2,1)S(1)}, bf16[1,3,128,128]{3,2,1,0:T(8,128)(2,1)S(1)}, u32[]{:S(2)}, u32[]{:S(2)}) collective-permute-start(bf16[1,3,128,128]{3,2,1,0:T(8,128)(2,1)S(1)} %bitcast.26), channel_id=1, source_target_pairs={{0,1},{1,0},{2,3},{3,2},{4,5},{5,4},{6,7},{7,6},{8,9},{9,8},{10,11... | collective-permute-start | bytes 294920 | tf_op jit(solution)/shard_map/ppermute | solution.py:184
  26.4 15.4 %collective-permute-start.8 = (bf16[2,3,128,128]{3,2,1,0:T(8,128)(2,1)S(1)}, bf16[2,3,128,128]{3,2,1,0:T(8,128)(2,1)S(1)}, u32[]{:S(2)}, u32[]{:S(2)}) collective-permute-start(bf16[2,3,128,128]{3,2,1,0:T(8,128)(2,1)S(1)} %pad_maximum_fusion.3), channel_id=1, source_target_pairs={{0,1},{1,0},{2,3},{3,2},{4,5},{5,4},{6,7},{7,6},{8,9},{9,8},{10,11... | collective-permute-start | bytes 589832 | tf_op jit(solution)/shard_map/ppermute | solution.py:184
  30.8 11.0 %collective-permute-start.11 = (bf16[2,3,128,128]{3,2,1,0:T(8,128)(2,1)S(1)}, bf16[2,3,128,128]{3,2,1,0:T(8,128)(2,1)S(1)}, u32[]{:S(2)}, u32[]{:S(2)}) collective-permute-start(bf16[2,3,128,128]{3,2,1,0:T(8,128)(2,1)S(1)} %pad_maximum_fusion.4), channel_id=1, source_target_pairs={{0,1},{1,0},{2,3},{3,2},{4,5},{5,4},{6,7},{7,6},{8,9},{9,8},{10,11... | collective-permute-start | bytes 589832 | tf_op jit(solution)/shard_map/ppermute | solution.py:184
  31.4 10.3 %collective-permute-start.5 = (bf16[2,3,128,128]{3,2,1,0:T(8,128)(2,1)S(1)}, bf16[2,3,128,128]{3,2,1,0:T(8,128)(2,1)S(1)}, u32[]{:S(2)}, u32[]{:S(2)}) collective-permute-start(bf16[2,3,128,128]{3,2,1,0:T(8,128)(2,1)S(1)} %pad_maximum_fusion.2), channel_id=1, source_target_pairs={{0,1},{1,0},{2,3},{3,2},{4,5},{5,4},{6,7},{7,6},{8,9},{9,8},{10,11... | collective-permute-start | bytes 589832 | tf_op jit(solution)/shard_map/ppermute | solution.py:184
  32.9 9.7 %collective-permute-start.15 = (bf16[4,3,128,128]{3,2,1,0:T(8,128)(2,1)S(1)}, bf16[4,3,128,128]{3,2,1,0:T(8,128)(2,1)S(1)}, u32[]{:S(2)}, u32[]{:S(2)}) collective-permute-start(bf16[4,3,128,128]{3,2,1,0:T(8,128)(2,1)S(1)} %pad_maximum_fusion.1.refs_1_), channel_id=1, source_target_pairs={{0,2},{1,3},{2,0},{3,1},{4,6},{5,7},{6,4},{7,5},{8,10},{9,11},{10,... | collective-permute-start | bytes 1179656 | tf_op jit(solution)/shard_map/ppermute | solution.py:184
  33.0 9.6 %collective-permute-start.14 = (bf16[4,3,128,128]{3,2,1,0:T(8,128)(2,1)S(1)}, bf16[4,3,128,128]{3,2,1,0:T(8,128)(2,1)S(1)}, u32[]{:S(2)}, u32[]{:S(2)}) collective-permute-start(bf16[4,3,128,128]{3,2,1,0:T(8,128)(2,1)S(1)} %pad_maximum_fusion.refs_0_), channel_id=1, source_target_pairs={{0,2},{1,3},{2,0},{3,1},{4,6},{5,7},{6,4},{7,5},{8,10},{9,11},{10,... | collective-permute-start | bytes 1179656 | tf_op jit(solution)/shard_map/ppermute | solution.py:184
  41.7 7.4 %collective-permute-start.12 = (bf16[4,3,128,128]{3,2,1,0:T(8,128)(2,1)S(1)}, bf16[4,3,128,128]{3,2,1,0:T(8,128)(2,1)S(1)}, u32[]{:S(2)}, u32[]{:S(2)}) collective-permute-start(bf16[4,3,128,128]{3,2,1,0:T(8,128)(2,1)S(1)} %constant_dynamic-update-slice_fusion.refs_0_), channel_id=1, source_target_pairs={{0,2},{1,3},{2,0},{3,1},{4,6},{5,7},{6,4},{7,5},{8,10},{9,11},{10,... | collective-permute-start | bytes 1179656 | tf_op jit(solution)/shard_map/ppermute | solution.py:184
  41.9 7.2 %collective-permute-start.13 = (bf16[4,3,128,128]{3,2,1,0:T(8,128)(2,1)S(1)}, bf16[4,3,128,128]{3,2,1,0:T(8,128)(2,1)S(1)}, u32[]{:S(2)}, u32[]{:S(2)}) collective-permute-start(bf16[4,3,128,128]{3,2,1,0:T(8,128)(2,1)S(1)} %constant_dynamic-update-slice_fusion.3.refs_1_), channel_id=1, source_target_pairs={{0,2},{1,3},{2,0},{3,1},{4,6},{5,7},{6,4},{7,5},{8,10},{9,11},{10,... | collective-permute-start | bytes 1179656 | tf_op jit(solution)/shard_map/ppermute | solution.py:184

commit v2 on v1

--- a/solution.py
+++ b/solution.py
@@ -14,37 +14,67 @@
 VMEM = pl.BlockSpec(memory_space=pltpu.VMEM)
 
 
-def pick_kernel(tile_dev, group, screening, tile_slot, factors, *outs):
-    count = screening.shape[1]
+def pick_kernel(tile_dev, group, screening, tile_slot, factors, *refs):
+    *outs, shown, slots, held, sems = refs
+    copies = [
+        pltpu.make_async_copy(screening, shown, sems.at[0]),
+        pltpu.make_async_copy(tile_slot, slots, sems.at[1]),
+        pltpu.make_async_copy(factors, held, sems.at[2]),
+    ]
+    for copy in copies:
+        copy.start()
     me = lax.axis_index("pair")
-    for shift, out in enumerate(outs):
+    copies[1].wait()
+    tiles = [jnp.int32(0)] * tile_dev
+    for t in range(tile_slot.shape[0]):
+        slot = slots[t]
+        tiles = [jnp.where(slot == me * tile_dev + n, t, x) for n, x in enumerate(tiles)]
+    copies[0].wait()
+    local = []
+    for shift in range(len(outs)):
         peer = (me // group) ^ shift
-        local = jnp.int32(0)
-        for t in range(count):
-            slot = tile_slot[screening[peer, t]]
-            local = jnp.where(slot // tile_dev == me, slot % tile_dev, local)
-        out[...] = factors[local]
+        found = jnp.int32(0)
+        for t in range(screening.shape[1]):
+            tile = shown[peer, t]
+            for n in range(1, tile_dev):
+                found = jnp.where(tile == tiles[n], n, found)
+        local.append(found)
+    copies[2].wait()
+    copies = [
+        pltpu.make_async_copy(held.at[found], out, sems.at[3 + n])
+        for n, (out, found) in enumerate(zip(outs, local))
+    ]
+    for copy in copies:
+        copy.start()
+    for copy in copies:
+        copy.wait()
 
 
 def pick(screening, tile_slot, factors, group, shifts):
     tile_dev, *tail = factors.shape
+    hbm = pl.BlockSpec(memory_space=pltpu.HBM)
     return pl.pallas_call(
         functools.partial(pick_kernel, tile_dev, group),
         out_shape=[jax.ShapeDtypeStruct(tail, factors.dtype)] * shifts,
-        in_specs=[SMEM, SMEM, VMEM],
-        out_specs=[VMEM] * shifts,
-        compiler_params=pltpu.CompilerParams(vmem_limit_bytes=8 * 2**20),
+        in_specs=[hbm, hbm, hbm],
+        out_specs=[ANY] * shifts,
+        scratch_shapes=[
+            pltpu.SMEM(screening.shape, jnp.int32),
+            pltpu.SMEM(tile_slot.shape, jnp.int32),
+            pltpu.VMEM(factors.shape, factors.dtype),
+            pltpu.SemaphoreType.DMA((3 + shifts,)),
+        ],
         name="pick",
     )(screening, tile_slot, factors)
 
 
 def ladder_kernel(dims, last, screening, tile_slot, occ, virt, amp, *refs):
-    tile_dev, group, row_tiles, shifts, tile, wide = dims
-    (near, far, near_other, far_other), refs = refs[:4], refs[4:]
+    tile_dev, group, row_tiles, shifts, tile = dims
+    bufs, refs = refs[:4], refs[4:]
     if last:
-        before, out, left, row_den, held, out_sem = refs
+        before, out, left, place, row_den, held, sems = refs
     else:
-        out, left = refs
+        out, left, place = refs
     me, cut = lax.axis_index("pair"), lax.axis_index("cuts")
     pair_id, core = me // group, me % group
     count, n_q = screening.shape[1], left.shape[1]
@@ -55,48 +85,34 @@
         slot = tile_slot[screening[pair_id, t]]
         owner = slot // tile_dev
         shift = (owner // group) ^ pair_id
-        same = owner % group == core
-        close = shift < half
-        for bufs, held_by in (((near, far), same), ((near_other, far_other), jnp.logical_not(same))):
-
-            @pl.when(held_by & close)
+        place[shift + (owner % group ^ core) * shifts] = t
+    for i in range(row_tiles):
+        slot = tile_slot[screening[pair_id, first + i]]
+        owner = slot // tile_dev
+        shift = (owner // group) ^ pair_id
+        which = shift // half + (owner % group ^ core) * 2
+        for n, buf in enumerate(bufs):
+
+            @pl.when(which == n)
             def _():
-                left[t] = bufs[0][shift]
-
-            @pl.when(held_by & jnp.logical_not(close))
-            def _():
-                left[t] = bufs[1][shift - half]
-
-    if last:
-        for i in range(row_tiles):
+                left[i] = buf[shift % half]
+
+        if last:
             row = virt[pl.ds(screening[pair_id, first + i], 1), :] - occ[0]
             row_den[i] = jnp.broadcast_to(row, (tile, tile)).T
 
-    def write(step, slot):
-        at = pl.ds(pl.multiple_of(step * wide, wide), wide)
-        return pltpu.make_async_copy(held.at[slot], out.at[:, at], out_sem.at[slot])
-
-    steps = out.shape[1] // wide
-
-    @pl.loop(0, steps)
-    def _(step):
-        slot = step % 2
-        base = pl.multiple_of(step * wide, wide)
-
-        if last:
-
-            @pl.when(step >= 2)
-            def _():
-                write(step - 2, slot).wait()
-
+    writes = []
+    for source in range(0, count, 2):
+        pair = [(n, bufs[n // half][n % half], place[n]) for n in (source, source + 1)]
+        offsets = [pl.multiple_of(at * tile, tile) for _, _, at in pair]
         halves = []
         for i in range(row_tiles):
-            lhs = left[first + i].reshape(n_q * tile, tile)
-            block = amp[i * tile : (i + 1) * tile, pl.ds(base, wide)]
+            rows = slice(i * tile, (i + 1) * tile)
+            block = jnp.concatenate([amp[rows, pl.ds(x, tile)] for x in offsets], axis=1)
+            lhs = left[i].reshape(n_q * tile, tile)
             half_done = jnp.dot(lhs, block, preferred_element_type=jnp.float32)
             halves.append(half_done.astype(jnp.bfloat16))
-        for j in range(wide // tile):
-            col = step * (wide // tile) + j
+        for j, (n, tiles, at) in enumerate(pair):
             cols = slice(j * tile, (j + 1) * tile)
             lhs = jnp.concatenate(
                 [
@@ -107,48 +123,53 @@
                 ],
                 axis=0,
             )
-            rhs = jnp.concatenate([left[col, q] for q in range(n_q)], axis=1)
+            rhs = jnp.concatenate([tiles[q] for q in range(n_q)], axis=1)
             acc = lax.dot_general(
                 lhs, rhs, (((1,), (1,)), ((), ())), preferred_element_type=jnp.float32
             )
-            at = pl.ds(pl.multiple_of(base + j * tile, tile), tile)
             if not last:
-                out[:, at] = acc
+                out[n] = acc
                 continue
-            acc = acc + before[:, at]
-            col_e = virt[pl.ds(screening[pair_id, col], 1), :] - occ[1]
+            acc = acc + before[n]
+            col_e = virt[pl.ds(screening[pair_id, at], 1), :] - occ[1]
             for i in range(row_tiles):
                 rows = slice(i * tile, (i + 1) * tile)
-                held[slot, rows, cols] = acc[rows] / (row_den[i] + col_e)
-        if last:
-            write(step, slot).start()
-
-    if last:
-        for step in range(max(0, steps - 2), steps):
-            write(step, step % 2).wait()
+                held[n, rows, :] = acc[rows] / (row_den[i] + col_e)
+            copy = pltpu.make_async_copy(held.at[n], out.at[:, pl.ds(offsets[j], tile)], sems.at[n])
+            copy.start()
+            writes.append(copy)
+    for copy in writes:
+        copy.wait()
 
 
 def ladder(screening, tile_slot, occ, virt, amp, tiles, dims, before=None):
-    _, _, row_tiles, _, tile, wide = dims
-    rows, columns = amp.shape
+    _, _, row_tiles, _, tile = dims
+    count, columns = screening.shape[1], amp.shape[1]
+    rows = row_tiles * tile
     last = before is not None
     n_q = tiles[0].shape[1]
-    scratch = [pltpu.VMEM((screening.shape[1], n_q, tile, tile), jnp.bfloat16)]
+    scratch = [
+        pltpu.VMEM((row_tiles, n_q, tile, tile), jnp.bfloat16),
+        pltpu.SMEM((count,), jnp.int32),
+    ]
     if last:
         scratch += [
             pltpu.VMEM((row_tiles, tile, tile), jnp.float32),
-            pltpu.VMEM((2, rows, wide), jnp.float32),
-            pltpu.SemaphoreType.DMA((2,)),
+            pltpu.VMEM((count, rows, tile), jnp.float32),
+            pltpu.SemaphoreType.DMA((count,)),
         ]
+        out = jax.ShapeDtypeStruct((rows, columns), jnp.float32)
+    else:
+        out = jax.ShapeDtypeStruct((count, rows, tile), jnp.float32)
     extra = [before] if last else []
     flops = 4 * n_q * rows * columns * tile
     return pl.pallas_call(
         functools.partial(ladder_kernel, dims, last),
-        out_shape=jax.ShapeDtypeStruct((rows, columns), jnp.float32),
+        out_shape=out,
         in_specs=[SMEM, SMEM, SMEM] + [VMEM] * (6 + len(extra)),
         out_specs=ANY if last else VMEM,
         scratch_shapes=scratch,
-        compiler_params=pltpu.CompilerParams(vmem_limit_bytes=(16 if last else 12) * 2**20),
+        compiler_params=pltpu.CompilerParams(vmem_limit_bytes=26 * 2**20),
         cost_estimate=pl.CostEstimate(flops=flops, bytes_accessed=0, transcendentals=0),
         name="ladder_last" if last else "ladder_first",
     )(screening, tile_slot, occ, virt, amp, *tiles, *extra)
@@ -200,7 +221,7 @@
     occ = occupied_energy[pair_orbitals[me // group]]
     rows = row_tiles * tile
     amp = lax.dynamic_slice_in_dim(amplitudes, lax.axis_index("cuts") * rows, rows, 0)
-    dims = (tile_dev, group, row_tiles, shifts, tile, 2 * tile)
+    dims = (tile_dev, group, row_tiles, shifts, tile)
     out = None
     for held in (got, crossed):
         near = jnp.stack(held[:half])

time: 57.2 us -> 52.4 us (0.916)
  Pallas kernels: 15.7 us -> 13.1 us
  local copies, waits for them, and re-layouts: 4.12 us -> 1.74 us
  other arithmetic: 0.18 us -> 1.07 us
    pallas_call x2, Pallas kernels: 14.3 us -> 11.1 us  [ladder(): pl.pallas_call(functools.partial(ladder_kernel, dims, last), out_shape=ou...]
    unnamed x19 -> x13, local copies, waits for them, and re-layouts: 2.34 us -> 0.06 us
    another operation x1, other arithmetic: 0.05 us -> 0.94 us  [direct(): near = jnp.stack(held[:half])]
  transfers between devices with their start and end apart: 16 -> 16, of which waited for: 5 -> 4; matrix products, arithmetic and copies ran while one was open for 4% -> 5% of each run, Pallas kernels for 11% -> 9%
where the time goes in v2:
time: 52.4 us; the launch traced here: 52.2 us
  starting transfers between devices  19.2 us (37%)
  waiting for transfers between devices  16.9 us (32%)
  Pallas kernels  13.1 us (25%)
  local copies, waits for them, and re-layouts  1.74 us (3%)
  other arithmetic  1.07 us (2%)
    ppermute x16, starting transfers between devices, send(): return lax.ppermute(x, BOTH, pairs)  19.2 us
    ppermute x16, waiting for transfers between devices, send(): return lax.ppermute(x, BOTH, pairs)  16.9 us
    pallas_call x2, Pallas kernels, ladder(): pl.pallas_call(functools.partial(ladder_kernel, dims, last), out_shape=ou...  11.1 us
    pallas_call x1, Pallas kernels, pick(): pl.pallas_call(functools.partial(pick_kernel, tile_dev, group), out_shape...  2.01 us
  transfers between devices with their start and end apart: 16, of which 4 were waited for; matrix products, arithmetic and copies ran while one was open for 5% of the time, Pallas kernels for 9%

profile of v2, /device:TPU:0, one launch (start us, length us, event | category | flops | bytes accessed | tf_op | source)
XLA Modules:
  0.0 52.2 jit_solution(5047797112284528615)
XLA Ops:
  0.0 0.0 copy-start
  0.0 2.0 %pick.1 = (bf16[3,128,128]{2,1,0:T(8,128)(2,1)}, bf16[3,128,128]{2,1,0:T(8,128)(2,1)}, bf16[3,128,128]{2,1,0:T(8,128)(2,1)}, bf16[3,128,128]{2,1,0:T(8,128)(2,1)...) custom-call(s32[8,16]{1,0:T(8,128)} %screening.5, ...), custom_call_target="tpu_custom_call" | custom-call | tf_op jit(solution)/shard_map/pick/pallas_call | solution.py:56
  2.0 3.1 %collective-permute-start = (bf16[1,3,128,128]{3,2,1,0:T(8,128)(2,1)}, bf16[1,3,128,128]{3,2,1,0:T(8,128)(2,1)S(1)}, u32[]{:S(2)}, u32[]{:S(2)}) collective-permute-start(bf16[1,3,128,128]{3,2,1,0:T(8,128)(2,1)} %bitcast.26), channel_id=1, source_target_pairs={{0,1},{1,0},{2,3},{3,2},{4,5},{5,4},{6,7},{7,6},{8,9},{9,8},{10,11... | collective-permute-start | bytes 294920 | tf_op jit(solution)/shard_map/ppermute | solution.py:205
  5.1 1.5 %collective-permute-start.1 = (bf16[3,128,128]{2,1,0:T(8,128)(2,1)}, bf16[3,128,128]{2,1,0:T(8,128)(2,1)S(1)}, u32[]{:S(2)}, u32[]{:S(2)}) collective-permute-start(bf16[3,128,128]{2,1,0:T(8,128)(2,1)} %get-tuple-element.14), channel_id=1, source_target_pairs={{0,4},{1,5},{2,6},{3,7},{4,0},{5,1},{6,2},{7,3},{8,12},{9,13},{10,... | collective-permute-start | bytes 294920 | tf_op jit(solution)/shard_map/ppermute | solution.py:205
  6.6 1.6 %collective-permute-start.3 = (bf16[3,128,128]{2,1,0:T(8,128)(2,1)}, bf16[3,128,128]{2,1,0:T(8,128)(2,1)S(1)}, u32[]{:S(2)}, u32[]{:S(2)}) collective-permute-start(bf16[3,128,128]{2,1,0:T(8,128)(2,1)} %get-tuple-element.15), channel_id=1, source_target_pairs={{0,8},{1,9},{2,10},{3,11},{4,12},{5,13},{6,14},{7,15},{8,0},{9,1},... | collective-permute-start | bytes 294920 | tf_op jit(solution)/shard_map/ppermute | solution.py:205
  8.1 2.6 %collective-permute-start.6 = (bf16[3,128,128]{2,1,0:T(8,128)(2,1)}, bf16[3,128,128]{2,1,0:T(8,128)(2,1)S(1)}, u32[]{:S(2)}, u32[]{:S(2)}) collective-permute-start(bf16[3,128,128]{2,1,0:T(8,128)(2,1)} %get-tuple-element.17), channel_id=1, source_target_pairs={{0,16},{1,17},{2,18},{3,19},{4,20},{5,21},{6,22},{7,23},{8,24},{9,... | collective-permute-start | bytes 294920 | tf_op jit(solution)/shard_map/ppermute | solution.py:205
  10.7 0.3 collective-permute-start.7
  11.0 0.9 %dynamic-slice_reduce_fusion = s32[2]{0:T(128)S(1)} fusion(s32[8,2]{0,1:T(2,128)} %param.11, s32[]{:T(128)S(6)} %select_n.22), kind=kLoop, calls=%fused_computation.13 | loop fusion | bytes 20 | tf_op jit(solution)/shard_map/dynamic_slice | solution.py:221
  11.9 0.0 copy-done
  11.9 0.6 %gather_fusion = f32[2]{0:T(128)S(1)} fusion(f32[4000]{0:T(1024)S(1)} %copy-done, s32[1024]{0:T(1024)S(1)} %pad_clamp_fusion), kind=kCustom, calls=%fused_computation | custom fusion | bytes 24 | tf_op jit(solution)/shard_map/gather | solution.py:221
  12.6 0.0 copy-start.4
  12.6 5.6 %collective-permute-done.6 = bf16[3,128,128]{2,1,0:T(8,128)(2,1)S(1)} collective-permute-done((bf16[3,128,128]{2,1,0:T(8,128)(2,1)}, bf16[3,128,128]{2,1,0:T(8,128)(2,1)S(1)}, u32[]{:S(2)}, u32[]{:S(2)}) %collective-permute-start.6) | collective-permute-done | bytes 98336 | tf_op jit(solution)/shard_map/ppermute | solution.py:205
  18.1 0.0 collective-permute-start.4
  18.1 1.2 %collective-permute-done.7 = bf16[3,128,128]{2,1,0:T(8,128)(2,1)S(1)} collective-permute-done((bf16[3,128,128]{2,1,0:T(8,128)(2,1)}, bf16[3,128,128]{2,1,0:T(8,128)(2,1)S(1)}, u32[]{:S(2)}, u32[]{:S(2)}) %collective-permute-start.7) | collective-permute-done | bytes 98336 | tf_op jit(solution)/shard_map/ppermute | solution.py:205
  19.3 2.4 %collective-permute-start.9 = (bf16[3,128,128]{2,1,0:T(8,128)(2,1)}, bf16[3,128,128]{2,1,0:T(8,128)(2,1)S(1)}, u32[]{:S(2)}, u32[]{:S(2)}) collective-permute-start(bf16[3,128,128]{2,1,0:T(8,128)(2,1)} %get-tuple-element.19), channel_id=1, source_target_pairs={{0,24},{1,25},{2,26},{3,27},{4,28},{5,29},{6,30},{7,31},{8,16},{9,... | collective-permute-start | bytes 294920 | tf_op jit(solution)/shard_map/ppermute | solution.py:205
  21.7 0.0 copy-start.1
  21.8 0.0 collective-permute-done.1
  21.8 2.4 %collective-permute-start.10 = (bf16[3,128,128]{2,1,0:T(8,128)(2,1)}, bf16[3,128,128]{2,1,0:T(8,128)(2,1)S(1)}, u32[]{:S(2)}, u32[]{:S(2)}) collective-permute-start(bf16[3,128,128]{2,1,0:T(8,128)(2,1)} %get-tuple-element.20), channel_id=1, source_target_pairs={{0,28},{1,29},{2,30},{3,31},{4,24},{5,25},{6,26},{7,27},{8,20},{9,... | collective-permute-start | bytes 294920 | tf_op jit(solution)/shard_map/ppermute | solution.py:205
  24.2 0.0 collective-permute-done.3
  24.2 0.5 collective-permute-start.2
  24.7 0.0 collective-permute-done.4
  24.7 1.5 %collective-permute-start.8 = (bf16[2,3,128,128]{3,2,1,0:T(8,128)(2,1)S(1)}, bf16[2,3,128,128]{3,2,1,0:T(8,128)(2,1)S(1)}, u32[]{:S(2)}, u32[]{:S(2)}) collective-permute-start(bf16[2,3,128,128]{3,2,1,0:T(8,128)(2,1)S(1)} %pad_maximum_fusion.3), channel_id=1, source_target_pairs={{0,1},{1,0},{2,3},{3,2},{4,5},{5,4},{6,7},{7,6},{8,9},{9,8},{10,11... | collective-permute-start | bytes 589832 | tf_op jit(solution)/shard_map/ppermute | solution.py:205
  26.2 0.9 %pad_maximum_fusion.refs_0_ = bf16[4,3,128,128]{3,2,1,0:T(8,128)(2,1)S(1)} fusion(bf16[1,3,128,128]{3,2,1,0:T(8,128)(2,1)S(1)} %bitcast.22, bf16[1,3,128,128]{3,2,1,0:T(8,128)(2,1)S(1)} %bitcast.16, bf16[1,3,128,128]{3,2,1,0:T(8,128)(2,1)S(1)} %bitcast.25, bf16[1,3,128,128]{3,2,1,0:T(8,128)(2,1)} %bitcast.27), kind=kLoop, calls=%fused_computation.1 | loop fusion | flops 589824 | bytes 786432 | tf_op jit(solution)/shard_map/stack | solution.py:227
  27.2 0.0 collective-permute-done.9
  27.2 2.3 %collective-permute-done.10 = bf16[3,128,128]{2,1,0:T(8,128)(2,1)S(1)} collective-permute-done((bf16[3,128,128]{2,1,0:T(8,128)(2,1)}, bf16[3,128,128]{2,1,0:T(8,128)(2,1)S(1)}, u32[]{:S(2)}, u32[]{:S(2)}) %collective-permute-start.10) | collective-permute-done | bytes 98336 | tf_op jit(solution)/shard_map/ppermute | solution.py:205
  29.5 0.6 %collective-permute-start.11 = (bf16[2,3,128,128]{3,2,1,0:T(8,128)(2,1)S(1)}, bf16[2,3,128,128]{3,2,1,0:T(8,128)(2,1)S(1)}, u32[]{:S(2)}, u32[]{:S(2)}) collective-permute-start(bf16[2,3,128,128]{3,2,1,0:T(8,128)(2,1)S(1)} %pad_maximum_fusion.4), channel_id=1, source_target_pairs={{0,1},{1,0},{2,3},{3,2},{4,5},{5,4},{6,7},{7,6},{8,9},{9,8},{10,11... | collective-permute-start | bytes 589832 | tf_op jit(solution)/shard_map/ppermute | solution.py:205
  30.1 1.5 %collective-permute-start.5 = (bf16[2,3,128,128]{3,2,1,0:T(8,128)(2,1)S(1)}, bf16[2,3,128,128]{3,2,1,0:T(8,128)(2,1)S(1)}, u32[]{:S(2)}, u32[]{:S(2)}) collective-permute-start(bf16[2,3,128,128]{3,2,1,0:T(8,128)(2,1)S(1)} %pad_maximum_fusion.2), channel_id=1, source_target_pairs={{0,1},{1,0},{2,3},{3,2},{4,5},{5,4},{6,7},{7,6},{8,9},{9,8},{10,11... | collective-permute-start | bytes 589832 | tf_op jit(solution)/shard_map/ppermute | solution.py:205
  31.6 0.1 pad_maximum_fusion.1.refs_1_
  31.6 0.0 collective-permute-done
  31.6 0.1 collective-permute-start.15
  31.7 0.0 collective-permute-done.2
  31.7 0.5 %collective-permute-start.14 = (bf16[4,3,128,128]{3,2,1,0:T(8,128)(2,1)S(1)}, bf16[4,3,128,128]{3,2,1,0:T(8,128)(2,1)S(1)}, u32[]{:S(2)}, u32[]{:S(2)}) collective-permute-start(bf16[4,3,128,128]{3,2,1,0:T(8,128)(2,1)S(1)} %pad_maximum_fusion.refs_0_), channel_id=1, source_target_pairs={{0,2},{1,3},{2,0},{3,1},{4,6},{5,7},{6,4},{7,5},{8,10},{9,11},{10,... | collective-permute-start | bytes 1179656 | tf_op jit(solution)/shard_map/ppermute | solution.py:205
  32.3 7.8 %collective-permute-done.5 = bf16[2,3,128,128]{3,2,1,0:T(8,128)(2,1)S(1)} collective-permute-done((bf16[2,3,128,128]{3,2,1,0:T(8,128)(2,1)S(1)}, bf16[2,3,128,128]{3,2,1,0:T(8,128)(2,1)S(1)}, u32[]{:S(2)}, u32[]{:S(2)}) %collective-permute-start.5) | collective-permute-done | bytes 196640 | tf_op jit(solution)/shard_map/ppermute | solution.py:205
  40.2 0.1 collective-permute-start.12
  40.3 0.0 collective-permute-done.8
  40.3 0.0 collective-permute-done.11
  40.3 0.6 %collective-permute-start.13 = (bf16[4,3,128,128]{3,2,1,0:T(8,128)(2,1)S(1)}, bf16[4,3,128,128]{3,2,1,0:T(8,128)(2,1)S(1)}, u32[]{:S(2)}, u32[]{:S(2)}) collective-permute-start(bf16[4,3,128,128]{3,2,1,0:T(8,128)(2,1)S(1)} %constant_dynamic-update-slice_fusion.3.refs_1_), channel_id=1, source_target_pairs={{0,2},{1,3},{2,0},{3,1},{4,6},{5,7},{6,4},{7,5},{8,10},{9,11},{10,... | collective-permute-start | bytes 1179656 | tf_op jit(solution)/shard_map/ppermute | solution.py:205
  40.9 0.0 copy-done.4
  40.9 0.1 constant_dynamic-slice_fusion.amp
  41.0 0.0 collective-permute-done.15.refs_3_
  41.0 0.0 collective-permute-done.14.refs_2_
  41.1 0.0 copy-done.1
  41.1 0.0 copy-done.2
  41.1 0.0 copy-done.3
  41.1 4.9 %ladder_first.1.refs_4_ = f32[16,512,128]{2,1,0:T(8,128)S(1)} custom-call(s32[8,16]{1,0:T(8,128)S(1)} %copy-done.2, s32[32]{0:T(128)S(1)} %copy-done.3, f32[2]{0:T(128)S(1)} %gather_fusion, f32[32,128]{1,0:T(8,128)S(1)} %copy-done.1, bf16[512,2048]{1,0:T(8,128)(2,1)S(1)} %constant_dynamic-slice_fusion.amp, ...), custom_call_target="tpu_custom_call" | custom-call | flops 1610612736 | tf_op jit(solution)/shard_map/ladder_first/pallas_call | solution.py:166
  46.0 0.0 collective-permute-done.12.refs_2_
  46.0 0.0 collective-permute-done.13.refs_3_
  46.1 6.1 %ladder_last.1 = f32[512,2048]{1,0:T(8,128)} custom-call(s32[8,16]{1,0:T(8,128)S(1)} %copy-done.2, s32[32]{0:T(128)S(1)} %copy-done.3, f32[2]{0:T(128)S(1)} %gather_fusion, f32[32,128]{1,0:T(8,128)S(1)} %copy-done.1, bf16[512,2048]{1,0:T(8,128)(2,1)S(1)} %constant_dynamic-slice_fusion.amp, ...), custom_call_target="tpu_custom_call" | custom-call | flops 1610612736 | tf_op jit(solution)/shard_map/ladder_last/pallas_call | solution.py:166
  (12 shorter events, 0.2 us)
Async XLA Ops:
  0.0 11.9 %copy-start = (f32[4000]{0:T(1024)S(1)}, f32[4000]{0:T(1024)}, u32[]{:S(2)}) copy-start(f32[4000]{0:T(1024)} %param.12) | copy-start | bytes 48004
  2.0 29.6 %collective-permute-start = (bf16[1,3,128,128]{3,2,1,0:T(8,128)(2,1)}, bf16[1,3,128,128]{3,2,1,0:T(8,128)(2,1)S(1)}, u32[]{:S(2)}, u32[]{:S(2)}) collective-permute-start(bf16[1,3,128,128]{3,2,1,0:T(8,128)(2,1)} %bitcast.26), channel_id=1, source_target_pairs={{0,1},{1,0},{2,3},{3,2},{4,5},{5,4},{6,7},{7,6},{8,9},{9,8},{10,11... | collective-permute-start | bytes 294920 | tf_op jit(solution)/shard_map/ppermute | solution.py:205
  5.1 16.7 %collective-permute-start.1 = (bf16[3,128,128]{2,1,0:T(8,128)(2,1)}, bf16[3,128,128]{2,1,0:T(8,128)(2,1)S(1)}, u32[]{:S(2)}, u32[]{:S(2)}) collective-permute-start(bf16[3,128,128]{2,1,0:T(8,128)(2,1)} %get-tuple-element.14), channel_id=1, source_target_pairs={{0,4},{1,5},{2,6},{3,7},{4,0},{5,1},{6,2},{7,3},{8,12},{9,13},{10,... | collective-permute-start | bytes 294920 | tf_op jit(solution)/shard_map/ppermute | solution.py:205
  6.6 17.6 %collective-permute-start.3 = (bf16[3,128,128]{2,1,0:T(8,128)(2,1)}, bf16[3,128,128]{2,1,0:T(8,128)(2,1)S(1)}, u32[]{:S(2)}, u32[]{:S(2)}) collective-permute-start(bf16[3,128,128]{2,1,0:T(8,128)(2,1)} %get-tuple-element.15), channel_id=1, source_target_pairs={{0,8},{1,9},{2,10},{3,11},{4,12},{5,13},{6,14},{7,15},{8,0},{9,1},... | collective-permute-start | bytes 294920 | tf_op jit(solution)/shard_map/ppermute | solution.py:205
  8.1 10.0 %collective-permute-start.6 = (bf16[3,128,128]{2,1,0:T(8,128)(2,1)}, bf16[3,128,128]{2,1,0:T(8,128)(2,1)S(1)}, u32[]{:S(2)}, u32[]{:S(2)}) collective-permute-start(bf16[3,128,128]{2,1,0:T(8,128)(2,1)} %get-tuple-element.17), channel_id=1, source_target_pairs={{0,16},{1,17},{2,18},{3,19},{4,20},{5,21},{6,22},{7,23},{8,24},{9,... | collective-permute-start | bytes 294920 | tf_op jit(solution)/shard_map/ppermute | solution.py:205
  10.7 8.6 %collective-permute-start.7 = (bf16[3,128,128]{2,1,0:T(8,128)(2,1)}, bf16[3,128,128]{2,1,0:T(8,128)(2,1)S(1)}, u32[]{:S(2)}, u32[]{:S(2)}) collective-permute-start(bf16[3,128,128]{2,1,0:T(8,128)(2,1)} %get-tuple-element.18), channel_id=1, source_target_pairs={{0,20},{1,21},{2,22},{3,23},{4,16},{5,17},{6,18},{7,19},{8,28},{9,... | collective-permute-start | bytes 294920 | tf_op jit(solution)/shard_map/ppermute | solution.py:205
  12.6 28.3 %copy-start.4 = (bf16[1024,2048]{1,0:T(8,128)(2,1)S(1)}, bf16[1024,2048]{1,0:T(8,128)(2,1)}, u32[]{:S(2)}) copy-start(bf16[1024,2048]{1,0:T(8,128)(2,1)} %param.7) | copy-start | bytes 12582916
  18.1 6.5 %collective-permute-start.4 = (bf16[3,128,128]{2,1,0:T(8,128)(2,1)}, bf16[3,128,128]{2,1,0:T(8,128)(2,1)S(1)}, u32[]{:S(2)}, u32[]{:S(2)}) collective-permute-start(bf16[3,128,128]{2,1,0:T(8,128)(2,1)} %get-tuple-element.16), channel_id=1, source_target_pairs={{0,12},{1,13},{2,14},{3,15},{4,8},{5,9},{6,10},{7,11},{8,4},{9,5},... | collective-permute-start | bytes 294920 | tf_op jit(solution)/shard_map/ppermute | solution.py:205
  19.3 7.8 %collective-permute-start.9 = (bf16[3,128,128]{2,1,0:T(8,128)(2,1)}, bf16[3,128,128]{2,1,0:T(8,128)(2,1)S(1)}, u32[]{:S(2)}, u32[]{:S(2)}) collective-permute-start(bf16[3,128,128]{2,1,0:T(8,128)(2,1)} %get-tuple-element.19), channel_id=1, source_target_pairs={{0,24},{1,25},{2,26},{3,27},{4,28},{5,29},{6,30},{7,31},{8,16},{9,... | collective-permute-start | bytes 294920 | tf_op jit(solution)/shard_map/ppermute | solution.py:205
  21.7 19.3 %copy-start.1 = (f32[32,128]{1,0:T(8,128)S(1)}, f32[32,128]{1,0:T(8,128)}, u32[]{:S(2)}) copy-start(f32[32,128]{1,0:T(8,128)} %virt.3) | copy-start | bytes 49156
  21.7 19.3 %copy-start.2 = (s32[8,16]{1,0:T(8,128)S(1)}, s32[8,16]{1,0:T(8,128)}, u32[]{:S(2)}) copy-start(s32[8,16]{1,0:T(8,128)} %screening.5) | copy-start | bytes 1540
  21.7 19.4 %copy-start.3 = (s32[32]{0:T(128)S(1)}, s32[32]{0:T(128)}, u32[]{:S(2)}) copy-start(s32[32]{0:T(128)} %tile_slot.5) | copy-start | bytes 388
  21.8 7.7 %collective-permute-start.10 = (bf16[3,128,128]{2,1,0:T(8,128)(2,1)}, bf16[3,128,128]{2,1,0:T(8,128)(2,1)S(1)}, u32[]{:S(2)}, u32[]{:S(2)}) collective-permute-start(bf16[3,128,128]{2,1,0:T(8,128)(2,1)} %get-tuple-element.20), channel_id=1, source_target_pairs={{0,28},{1,29},{2,30},{3,31},{4,24},{5,25},{6,26},{7,27},{8,20},{9,... | collective-permute-start | bytes 294920 | tf_op jit(solution)/shard_map/ppermute | solution.py:205
  24.2 7.6 %collective-permute-start.2 = (bf16[1,3,128,128]{3,2,1,0:T(8,128)(2,1)S(1)}, bf16[1,3,128,128]{3,2,1,0:T(8,128)(2,1)S(1)}, u32[]{:S(2)}, u32[]{:S(2)}) collective-permute-start(bf16[1,3,128,128]{3,2,1,0:T(8,128)(2,1)S(1)} %bitcast.24), channel_id=1, source_target_pairs={{0,1},{1,0},{2,3},{3,2},{4,5},{5,4},{6,7},{7,6},{8,9},{9,8},{10,11... | collective-permute-start | bytes 294920 | tf_op jit(solution)/shard_map/ppermute | solution.py:205
  24.7 15.6 %collective-permute-start.8 = (bf16[2,3,128,128]{3,2,1,0:T(8,128)(2,1)S(1)}, bf16[2,3,128,128]{3,2,1,0:T(8,128)(2,1)S(1)}, u32[]{:S(2)}, u32[]{:S(2)}) collective-permute-start(bf16[2,3,128,128]{3,2,1,0:T(8,128)(2,1)S(1)} %pad_maximum_fusion.3), channel_id=1, source_target_pairs={{0,1},{1,0},{2,3},{3,2},{4,5},{5,4},{6,7},{7,6},{8,9},{9,8},{10,11... | collective-permute-start | bytes 589832 | tf_op jit(solution)/shard_map/ppermute | solution.py:205
  29.5 10.8 %collective-permute-start.11 = (bf16[2,3,128,128]{3,2,1,0:T(8,128)(2,1)S(1)}, bf16[2,3,128,128]{3,2,1,0:T(8,128)(2,1)S(1)}, u32[]{:S(2)}, u32[]{:S(2)}) collective-permute-start(bf16[2,3,128,128]{3,2,1,0:T(8,128)(2,1)S(1)} %pad_maximum_fusion.4), channel_id=1, source_target_pairs={{0,1},{1,0},{2,3},{3,2},{4,5},{5,4},{6,7},{7,6},{8,9},{9,8},{10,11... | collective-permute-start | bytes 589832 | tf_op jit(solution)/shard_map/ppermute | solution.py:205
  30.1 10.1 %collective-permute-start.5 = (bf16[2,3,128,128]{3,2,1,0:T(8,128)(2,1)S(1)}, bf16[2,3,128,128]{3,2,1,0:T(8,128)(2,1)S(1)}, u32[]{:S(2)}, u32[]{:S(2)}) collective-permute-start(bf16[2,3,128,128]{3,2,1,0:T(8,128)(2,1)S(1)} %pad_maximum_fusion.2), channel_id=1, source_target_pairs={{0,1},{1,0},{2,3},{3,2},{4,5},{5,4},{6,7},{7,6},{8,9},{9,8},{10,11... | collective-permute-start | bytes 589832 | tf_op jit(solution)/shard_map/ppermute | solution.py:205
  31.6 9.4 %collective-permute-start.15 = (bf16[4,3,128,128]{3,2,1,0:T(8,128)(2,1)S(1)}, bf16[4,3,128,128]{3,2,1,0:T(8,128)(2,1)S(1)}, u32[]{:S(2)}, u32[]{:S(2)}) collective-permute-start(bf16[4,3,128,128]{3,2,1,0:T(8,128)(2,1)S(1)} %pad_maximum_fusion.1.refs_1_), channel_id=1, source_target_pairs={{0,2},{1,3},{2,0},{3,1},{4,6},{5,7},{6,4},{7,5},{8,10},{9,11},{10,... | collective-permute-start | bytes 1179656 | tf_op jit(solution)/shard_map/ppermute | solution.py:205
  31.7 9.3 %collective-permute-start.14 = (bf16[4,3,128,128]{3,2,1,0:T(8,128)(2,1)S(1)}, bf16[4,3,128,128]{3,2,1,0:T(8,128)(2,1)S(1)}, u32[]{:S(2)}, u32[]{:S(2)}) collective-permute-start(bf16[4,3,128,128]{3,2,1,0:T(8,128)(2,1)S(1)} %pad_maximum_fusion.refs_0_), channel_id=1, source_target_pairs={{0,2},{1,3},{2,0},{3,1},{4,6},{5,7},{6,4},{7,5},{8,10},{9,11},{10,... | collective-permute-start | bytes 1179656 | tf_op jit(solution)/shard_map/ppermute | solution.py:205
  40.2 5.9 %collective-permute-start.12 = (bf16[4,3,128,128]{3,2,1,0:T(8,128)(2,1)S(1)}, bf16[4,3,128,128]{3,2,1,0:T(8,128)(2,1)S(1)}, u32[]{:S(2)}, u32[]{:S(2)}) collective-permute-start(bf16[4,3,128,128]{3,2,1,0:T(8,128)(2,1)S(1)} %constant_dynamic-update-slice_fusion.refs_0_), channel_id=1, source_target_pairs={{0,2},{1,3},{2,0},{3,1},{4,6},{5,7},{6,4},{7,5},{8,10},{9,11},{10,... | collective-permute-start | bytes 1179656 | tf_op jit(solution)/shard_map/ppermute | solution.py:205
  40.3 5.7 %collective-permute-start.13 = (bf16[4,3,128,128]{3,2,1,0:T(8,128)(2,1)S(1)}, bf16[4,3,128,128]{3,2,1,0:T(8,128)(2,1)S(1)}, u32[]{:S(2)}, u32[]{:S(2)}) collective-permute-start(bf16[4,3,128,128]{3,2,1,0:T(8,128)(2,1)S(1)} %constant_dynamic-update-slice_fusion.3.refs_1_), channel_id=1, source_target_pairs={{0,2},{1,3},{2,0},{3,1},{4,6},{5,7},{6,4},{7,5},{8,10},{9,11},{10,... | collective-permute-start | bytes 1179656 | tf_op jit(solution)/shard_map/ppermute | solution.py:205

commit v3 on v2

--- a/solution.py
+++ b/solution.py
@@ -112,21 +112,29 @@
             lhs = left[i].reshape(n_q * tile, tile)
             half_done = jnp.dot(lhs, block, preferred_element_type=jnp.float32)
             halves.append(half_done.astype(jnp.bfloat16))
-        for j, (n, tiles, at) in enumerate(pair):
-            cols = slice(j * tile, (j + 1) * tile)
-            lhs = jnp.concatenate(
-                [
-                    jnp.concatenate(
-                        [h[q * tile : (q + 1) * tile, cols] for q in range(n_q)], axis=1
-                    )
-                    for h in halves
-                ],
-                axis=0,
-            )
-            rhs = jnp.concatenate([tiles[q] for q in range(n_q)], axis=1)
-            acc = lax.dot_general(
-                lhs, rhs, (((1,), (1,)), ((), ())), preferred_element_type=jnp.float32
-            )
+        lhs = jnp.concatenate(
+            [
+                jnp.concatenate([h[q * tile : (q + 1) * tile] for q in range(n_q)], axis=1)
+                for h in halves
+            ],
+            axis=0,
+        )
+        zero = jnp.zeros((tile, tile), jnp.bfloat16)
+        rhs = jnp.concatenate(
+            [
+                jnp.concatenate(
+                    [x for q in range(n_q) for x in ((tiles[q], zero), (zero, tiles[q]))[j]],
+                    axis=1,
+                )
+                for j, (_, tiles, _) in enumerate(pair)
+            ],
+            axis=0,
+        )
+        both = lax.dot_general(
+            lhs, rhs, (((1,), (1,)), ((), ())), preferred_element_type=jnp.float32
+        )
+        for j, (n, _, at) in enumerate(pair):
+            acc = both[:, j * tile : (j + 1) * tile]
             if not last:
                 out[n] = acc
                 continue
@@ -176,12 +184,10 @@
 
 
 def crossings(shifts):
-    near = [[s, s + 1] for s in range(2, shifts // 2, 2)]
-    far = [[s, s + 1] for s in range(shifts // 2, shifts, 2)]
-    groups = [[0], [1]]
-    while near or far:
-        groups += [x.pop(0) for x in (far, near) if x and (x is near or len(x) > 1 or not near)]
-    return groups
+    half = shifts // 2
+    early = [[s] for s in (0, 1, half, half + 1)]
+    near = [[s, s + 1] for s in range(2, half, 2)]
+    return early + near + [[s] for s in range(half + 2, shifts)]
 
 
 def direct(
@@ -214,10 +220,12 @@
     ]
     crossed = [None] * shifts
     for members in crossings(shifts):
-        x = jnp.stack([got[s] for s in members])
+        x = got[members[0]]
+        if len(members) > 1:
+            x = jnp.stack([got[s] for s in members])
         x = send(x, lambda p, c: (p, c ^ 1))
         for n, s in enumerate(members):
-            crossed[s] = x[n]
+            crossed[s] = x[n] if len(members) > 1 else x
     occ = occupied_energy[pair_orbitals[me // group]]
     rows = row_tiles * tile
     amp = lax.dynamic_slice_in_dim(amplitudes, lax.axis_index("cuts") * rows, rows, 0)

time: 52.4 us -> 50.9 us (0.971)
  waiting for transfers between devices: 16.9 us -> 11.2 us
  starting transfers between devices: 19.2 us -> 21.8 us
  local copies, waits for them, and re-layouts: 1.74 us -> 3.35 us
    ppermute x16 -> x18, waiting for transfers between devices: 16.9 us -> 11.2 us  [send(): return lax.ppermute(x, BOTH, pairs)]
    ppermute x16 -> x18, starting transfers between devices: 19.2 us -> 21.8 us  [send(): return lax.ppermute(x, BOTH, pairs)]
    dynamic_slice x1, local copies, waits for them, and re-layouts: 0.14 us -> 1.83 us  [direct(): lax.dynamic_slice_in_dim(amplitudes, lax.axis_index('cuts') * rows, rows, 0)]
  transfers between devices with their start and end apart: 16 -> 18, of which waited for: 4 -> 6; matrix products, arithmetic and copies ran while one was open for 5% -> 9% of each run, Pallas kernels for 9% -> 10%
where the time goes in v3:
time: 50.9 us; the launch traced here: 50.7 us
  starting transfers between devices  21.8 us (43%)
  Pallas kernels  13.1 us (26%)
  waiting for transfers between devices  11.2 us (22%)
  local copies, waits for them, and re-layouts  3.35 us (7%)
  other arithmetic  1.12 us (2%)
    ppermute x18, starting transfers between devices, send(): return lax.ppermute(x, BOTH, pairs)  21.8 us
    ppermute x18, waiting for transfers between devices, send(): return lax.ppermute(x, BOTH, pairs)  11.2 us
    pallas_call x2, Pallas kernels, ladder(): pl.pallas_call(functools.partial(ladder_kernel, dims, last), out_shape=ou...  11.1 us
    pallas_call x1, Pallas kernels, pick(): pl.pallas_call(functools.partial(pick_kernel, tile_dev, group), out_shape...  2.01 us
    dynamic_slice x1, local copies, waits for them, and re-layouts, direct(): lax.dynamic_slice_in_dim(amplitudes, lax.axis_index('cuts') * rows, rows, 0)  1.83 us
  transfers between devices with their start and end apart: 18, of which 6 were waited for; matrix products, arithmetic and copies ran while one was open for 9% of the time, Pallas kernels for 10%

profile of v3, /device:TPU:0, one launch (start us, length us, event | category | flops | bytes accessed | tf_op | source)
XLA Modules:
  0.0 50.7 jit_solution(13814486016841042462)
XLA Ops:
  0.0 2.0 %pick.1 = (bf16[3,128,128]{2,1,0:T(8,128)(2,1)}, bf16[3,128,128]{2,1,0:T(8,128)(2,1)}, bf16[3,128,128]{2,1,0:T(8,128)(2,1)}, bf16[3,128,128]{2,1,0:T(8,128)(2,1)...) custom-call(s32[8,16]{1,0:T(8,128)} %screening.5, ...), custom_call_target="tpu_custom_call" | custom-call | tf_op jit(solution)/shard_map/pick/pallas_call | solution.py:56
  2.0 0.0 copy-start.1
  2.0 0.0 copy-start.2
  2.0 0.0 copy-start.3
  2.1 3.0 %collective-permute-start.1 = (bf16[3,128,128]{2,1,0:T(8,128)(2,1)}, bf16[3,128,128]{2,1,0:T(8,128)(2,1)S(1)}, u32[]{:S(2)}, u32[]{:S(2)}) collective-permute-start(bf16[3,128,128]{2,1,0:T(8,128)(2,1)} %get-tuple-element.14), channel_id=1, source_target_pairs={{0,4},{1,5},{2,6},{3,7},{4,0},{5,1},{6,2},{7,3},{8,12},{9,13},{10,... | collective-permute-start | bytes 294920 | tf_op jit(solution)/shard_map/ppermute | solution.py:211
  5.1 1.6 %collective-permute-start.3 = (bf16[3,128,128]{2,1,0:T(8,128)(2,1)}, bf16[3,128,128]{2,1,0:T(8,128)(2,1)S(1)}, u32[]{:S(2)}, u32[]{:S(2)}) collective-permute-start(bf16[3,128,128]{2,1,0:T(8,128)(2,1)} %get-tuple-element.15), channel_id=1, source_target_pairs={{0,8},{1,9},{2,10},{3,11},{4,12},{5,13},{6,14},{7,15},{8,0},{9,1},... | collective-permute-start | bytes 294920 | tf_op jit(solution)/shard_map/ppermute | solution.py:211
  6.7 0.0 collective-permute-start.4
  6.7 3.0 %collective-permute-start.6 = (bf16[3,128,128]{2,1,0:T(8,128)(2,1)}, bf16[3,128,128]{2,1,0:T(8,128)(2,1)S(1)}, u32[]{:S(2)}, u32[]{:S(2)}) collective-permute-start(bf16[3,128,128]{2,1,0:T(8,128)(2,1)} %get-tuple-element.17), channel_id=1, source_target_pairs={{0,16},{1,17},{2,18},{3,19},{4,20},{5,21},{6,22},{7,23},{8,24},{9,... | collective-permute-start | bytes 294920 | tf_op jit(solution)/shard_map/ppermute | solution.py:211
  9.7 1.3 %collective-permute-start.8 = (bf16[3,128,128]{2,1,0:T(8,128)(2,1)}, bf16[3,128,128]{2,1,0:T(8,128)(2,1)S(1)}, u32[]{:S(2)}, u32[]{:S(2)}) collective-permute-start(bf16[3,128,128]{2,1,0:T(8,128)(2,1)} %get-tuple-element.18), channel_id=1, source_target_pairs={{0,20},{1,21},{2,22},{3,23},{4,16},{5,17},{6,18},{7,19},{8,28},{9,... | collective-permute-start | bytes 294920 | tf_op jit(solution)/shard_map/ppermute | solution.py:211
  10.9 0.9 %dynamic-slice_reduce_fusion = s32[2]{0:T(128)S(1)} fusion(s32[8,2]{0,1:T(2,128)} %param.11, s32[]{:T(128)S(6)} %select_n.22), kind=kLoop, calls=%fused_computation.8 | loop fusion | bytes 20 | tf_op jit(solution)/shard_map/dynamic_slice | solution.py:229
  11.8 0.6 %gather_fusion = f32[2]{0:T(128)S(1)} fusion(f32[4000]{0:T(1024)S(1)} %copy-done, s32[1024]{0:T(1024)S(1)} %pad_clamp_fusion), kind=kCustom, calls=%fused_computation | custom fusion | bytes 24 | tf_op jit(solution)/shard_map/gather | solution.py:229
  12.5 0.5 collective-permute-done.3
  12.9 3.2 %collective-permute-start.10 = (bf16[3,128,128]{2,1,0:T(8,128)(2,1)}, bf16[3,128,128]{2,1,0:T(8,128)(2,1)S(1)}, u32[]{:S(2)}, u32[]{:S(2)}) collective-permute-start(bf16[3,128,128]{2,1,0:T(8,128)(2,1)} %get-tuple-element.19), channel_id=1, source_target_pairs={{0,24},{1,25},{2,26},{3,27},{4,28},{5,29},{6,30},{7,31},{8,16},{9,... | collective-permute-start | bytes 294920 | tf_op jit(solution)/shard_map/ppermute | solution.py:211
  16.1 0.0 collective-permute-done.4
  16.1 1.8 %collective-permute-start.12 = (bf16[3,128,128]{2,1,0:T(8,128)(2,1)}, bf16[3,128,128]{2,1,0:T(8,128)(2,1)S(1)}, u32[]{:S(2)}, u32[]{:S(2)}) collective-permute-start(bf16[3,128,128]{2,1,0:T(8,128)(2,1)} %get-tuple-element.20), channel_id=1, source_target_pairs={{0,28},{1,29},{2,30},{3,31},{4,24},{5,25},{6,26},{7,27},{8,20},{9,... | collective-permute-start | bytes 294920 | tf_op jit(solution)/shard_map/ppermute | solution.py:211
  17.9 0.0 collective-permute-done.1
  18.0 1.6 %collective-permute-start.5 = (bf16[2,3,128,128]{3,2,1,0:T(8,128)(2,1)S(1)}, bf16[2,3,128,128]{3,2,1,0:T(8,128)(2,1)S(1)}, u32[]{:S(2)}, u32[]{:S(2)}) collective-permute-start(bf16[2,3,128,128]{3,2,1,0:T(8,128)(2,1)S(1)} %pad_maximum_fusion.4), channel_id=1, source_target_pairs={{0,1},{1,0},{2,3},{3,2},{4,5},{5,4},{6,7},{7,6},{8,9},{9,8},{10,11... | collective-permute-start | bytes 589832 | tf_op jit(solution)/shard_map/ppermute | solution.py:211
  19.5 0.0 collective-permute-done.6
  19.5 0.5 collective-permute-start.7
  20.0 5.0 %collective-permute-done.8 = bf16[3,128,128]{2,1,0:T(8,128)(2,1)S(1)} collective-permute-done((bf16[3,128,128]{2,1,0:T(8,128)(2,1)}, bf16[3,128,128]{2,1,0:T(8,128)(2,1)S(1)}, u32[]{:S(2)}, u32[]{:S(2)}) %collective-permute-start.8) | collective-permute-done | bytes 98336 | tf_op jit(solution)/shard_map/ppermute | solution.py:211
  25.0 1.5 %collective-permute-start.9 = (bf16[3,128,128]{2,1,0:T(8,128)(2,1)S(1)}, bf16[3,128,128]{2,1,0:T(8,128)(2,1)S(1)}, u32[]{:S(2)}, u32[]{:S(2)}) collective-permute-start(bf16[3,128,128]{2,1,0:T(8,128)(2,1)S(1)} %collective-permute-done.8), channel_id=1, source_target_pairs={{0,1},{1,0},{2,3},{3,2},{4,5},{5,4},{6,7},{7,6},{8,9},{9,8},{10,11... | collective-permute-start | bytes 294920 | tf_op jit(solution)/shard_map/ppermute | solution.py:211
  26.6 0.0 collective-permute-done.10
  26.6 0.5 collective-permute-start.11
  27.1 0.9 %pad_maximum_fusion.2.refs_0_ = bf16[4,3,128,128]{3,2,1,0:T(8,128)(2,1)S(1)} fusion(bf16[1,3,128,128]{3,2,1,0:T(8,128)(2,1)S(1)} %bitcast.21, bf16[1,3,128,128]{3,2,1,0:T(8,128)(2,1)S(1)} %bitcast.19, bf16[1,3,128,128]{3,2,1,0:T(8,128)(2,1)S(1)} %bitcast.22, bf16[1,3,128,128]{3,2,1,0:T(8,128)(2,1)} %bitcast.23), kind=kLoop, calls=%fused_computation.3 | loop fusion | flops 589824 | bytes 786432 | tf_op jit(solution)/shard_map/stack | solution.py:235
  28.0 0.0 collective-permute-done.12
  28.0 1.6 %collective-permute-start.13 = (bf16[3,128,128]{2,1,0:T(8,128)(2,1)S(1)}, bf16[3,128,128]{2,1,0:T(8,128)(2,1)S(1)}, u32[]{:S(2)}, u32[]{:S(2)}) collective-permute-start(bf16[3,128,128]{2,1,0:T(8,128)(2,1)S(1)} %collective-permute-done.12), channel_id=1, source_target_pairs={{0,1},{1,0},{2,3},{3,2},{4,5},{5,4},{6,7},{7,6},{8,9},{9,8},{10,11... | collective-permute-start | bytes 294920 | tf_op jit(solution)/shard_map/ppermute | solution.py:211
  29.6 0.1 pad_maximum_fusion.3.refs_1_
  29.7 0.0 collective-permute-done.7
  29.7 0.6 %collective-permute-start = (bf16[3,128,128]{2,1,0:T(8,128)(2,1)}, bf16[3,128,128]{2,1,0:T(8,128)(2,1)S(1)}, u32[]{:S(2)}, u32[]{:S(2)}) collective-permute-start(bf16[3,128,128]{2,1,0:T(8,128)(2,1)} %get-tuple-element.13), channel_id=1, source_target_pairs={{0,1},{1,0},{2,3},{3,2},{4,5},{5,4},{6,7},{7,6},{8,9},{9,8},{10,11... | collective-permute-start | bytes 294920 | tf_op jit(solution)/shard_map/ppermute | solution.py:211
  30.2 0.0 collective-permute-done.9
  30.3 0.0 collective-permute-start.16
  30.3 1.6 %collective-permute-done.11 = bf16[3,128,128]{2,1,0:T(8,128)(2,1)S(1)} collective-permute-done((bf16[3,128,128]{2,1,0:T(8,128)(2,1)S(1)}, bf16[3,128,128]{2,1,0:T(8,128)(2,1)S(1)}, u32[]{:S(2)}, u32[]{:S(2)}) %collective-permute-start.11) | collective-permute-done | bytes 98336 | tf_op jit(solution)/shard_map/ppermute | solution.py:211
  31.9 0.0 collective-permute-start.17
  31.9 1.0 %collective-permute-done.13 = bf16[3,128,128]{2,1,0:T(8,128)(2,1)S(1)} collective-permute-done((bf16[3,128,128]{2,1,0:T(8,128)(2,1)S(1)}, bf16[3,128,128]{2,1,0:T(8,128)(2,1)S(1)}, u32[]{:S(2)}, u32[]{:S(2)}) %collective-permute-start.13) | collective-permute-done | bytes 98336 | tf_op jit(solution)/shard_map/ppermute | solution.py:211
  32.9 1.5 %collective-permute-start.2 = (bf16[3,128,128]{2,1,0:T(8,128)(2,1)S(1)}, bf16[3,128,128]{2,1,0:T(8,128)(2,1)S(1)}, u32[]{:S(2)}, u32[]{:S(2)}) collective-permute-start(bf16[3,128,128]{2,1,0:T(8,128)(2,1)S(1)} %collective-permute-done.1), channel_id=1, source_target_pairs={{0,1},{1,0},{2,3},{3,2},{4,5},{5,4},{6,7},{7,6},{8,9},{9,8},{10,11... | collective-permute-start | bytes 294920 | tf_op jit(solution)/shard_map/ppermute | solution.py:211
  34.5 0.1 pad_maximum_fusion.1.refs_1_
  34.5 0.1 collective-permute-done
  34.6 0.0 collective-permute-start.15
  34.6 3.0 %collective-permute-done.2 = bf16[3,128,128]{2,1,0:T(8,128)(2,1)S(1)} collective-permute-done((bf16[3,128,128]{2,1,0:T(8,128)(2,1)S(1)}, bf16[3,128,128]{2,1,0:T(8,128)(2,1)S(1)}, u32[]{:S(2)}, u32[]{:S(2)}) %collective-permute-start.2) | collective-permute-done | bytes 98336 | tf_op jit(solution)/shard_map/ppermute | solution.py:211
  37.5 0.0 collective-permute-done.5
  37.6 0.1 collective-permute-start.14
  37.7 1.8 %constant_dynamic-slice_fusion.amp = bf16[512,2048]{1,0:T(8,128)(2,1)S(1)} fusion(bf16[1024,2048]{1,0:T(8,128)(2,1)} %param.7, s32[]{:T(128)S(6)} %select_n.24), kind=kLoop, calls=%fused_computation.10 | loop fusion | bytes 4194308 | tf_op jit(solution)/shard_map/dynamic_slice | solution.py:231
  39.5 0.0 collective-permute-done.16.refs_2_
  39.5 0.0 collective-permute-done.17.refs_3_
  39.6 4.9 %ladder_first.1.refs_4_ = f32[16,512,128]{2,1,0:T(8,128)S(1)} custom-call(s32[8,16]{1,0:T(8,128)S(1)} %copy-done.2, s32[32]{0:T(128)S(1)} %copy-done.3, f32[2]{0:T(128)S(1)} %gather_fusion, f32[32,128]{1,0:T(8,128)S(1)} %copy-done.1, bf16[512,2048]{1,0:T(8,128)(2,1)S(1)} %constant_dynamic-slice_fusion.amp, ...), custom_call_target="tpu_custom_call" | custom-call | flops 1610612736 | tf_op jit(solution)/shard_map/ladder_first/pallas_call | solution.py:174
  44.4 0.0 collective-permute-done.15.refs_3_
  44.5 0.0 collective-permute-done.14.refs_2_
  44.5 6.2 %ladder_last.1 = f32[512,2048]{1,0:T(8,128)} custom-call(s32[8,16]{1,0:T(8,128)S(1)} %copy-done.2, s32[32]{0:T(128)S(1)} %copy-done.3, f32[2]{0:T(128)S(1)} %gather_fusion, f32[32,128]{1,0:T(8,128)S(1)} %copy-done.1, bf16[512,2048]{1,0:T(8,128)(2,1)S(1)} %constant_dynamic-slice_fusion.amp, bf16[4,3,128,128]{3,2,1,0:T(8,128)(2,1)S(1)} %pad_maximum_fusion.refs_0_, ...), custom_call_target="tpu_custom_call" | custom-call | flops 1610612736 | tf_op jit(solution)/shard_map/ladder_last/pallas_call | solution.py:174
  (9 shorter events, 0.1 us)
Async XLA Ops:
  0.0 11.8 %copy-start = (f32[4000]{0:T(1024)S(1)}, f32[4000]{0:T(1024)}, u32[]{:S(2)}) copy-start(f32[4000]{0:T(1024)} %param.12) | copy-start | bytes 48004
  2.0 37.5 %copy-start.1 = (f32[32,128]{1,0:T(8,128)S(1)}, f32[32,128]{1,0:T(8,128)}, u32[]{:S(2)}) copy-start(f32[32,128]{1,0:T(8,128)} %virt.3) | copy-start | bytes 49156
  2.0 37.5 %copy-start.2 = (s32[8,16]{1,0:T(8,128)S(1)}, s32[8,16]{1,0:T(8,128)}, u32[]{:S(2)}) copy-start(s32[8,16]{1,0:T(8,128)} %screening.5) | copy-start | bytes 1540
  2.0 37.5 %copy-start.3 = (s32[32]{0:T(128)S(1)}, s32[32]{0:T(128)}, u32[]{:S(2)}) copy-start(s32[32]{0:T(128)} %tile_slot.5) | copy-start | bytes 388
  2.1 15.9 %collective-permute-start.1 = (bf16[3,128,128]{2,1,0:T(8,128)(2,1)}, bf16[3,128,128]{2,1,0:T(8,128)(2,1)S(1)}, u32[]{:S(2)}, u32[]{:S(2)}) collective-permute-start(bf16[3,128,128]{2,1,0:T(8,128)(2,1)} %get-tuple-element.14), channel_id=1, source_target_pairs={{0,4},{1,5},{2,6},{3,7},{4,0},{5,1},{6,2},{7,3},{8,12},{9,13},{10,... | collective-permute-start | bytes 294920 | tf_op jit(solution)/shard_map/ppermute | solution.py:211
  5.1 7.8 %collective-permute-start.3 = (bf16[3,128,128]{2,1,0:T(8,128)(2,1)}, bf16[3,128,128]{2,1,0:T(8,128)(2,1)S(1)}, u32[]{:S(2)}, u32[]{:S(2)}) collective-permute-start(bf16[3,128,128]{2,1,0:T(8,128)(2,1)} %get-tuple-element.15), channel_id=1, source_target_pairs={{0,8},{1,9},{2,10},{3,11},{4,12},{5,13},{6,14},{7,15},{8,0},{9,1},... | collective-permute-start | bytes 294920 | tf_op jit(solution)/shard_map/ppermute | solution.py:211
  6.7 9.4 %collective-permute-start.4 = (bf16[3,128,128]{2,1,0:T(8,128)(2,1)}, bf16[3,128,128]{2,1,0:T(8,128)(2,1)S(1)}, u32[]{:S(2)}, u32[]{:S(2)}) collective-permute-start(bf16[3,128,128]{2,1,0:T(8,128)(2,1)} %get-tuple-element.16), channel_id=1, source_target_pairs={{0,12},{1,13},{2,14},{3,15},{4,8},{5,9},{6,10},{7,11},{8,4},{9,5},... | collective-permute-start | bytes 294920 | tf_op jit(solution)/shard_map/ppermute | solution.py:211
  6.7 12.9 %collective-permute-start.6 = (bf16[3,128,128]{2,1,0:T(8,128)(2,1)}, bf16[3,128,128]{2,1,0:T(8,128)(2,1)S(1)}, u32[]{:S(2)}, u32[]{:S(2)}) collective-permute-start(bf16[3,128,128]{2,1,0:T(8,128)(2,1)} %get-tuple-element.17), channel_id=1, source_target_pairs={{0,16},{1,17},{2,18},{3,19},{4,20},{5,21},{6,22},{7,23},{8,24},{9,... | collective-permute-start | bytes 294920 | tf_op jit(solution)/shard_map/ppermute | solution.py:211
  9.7 15.4 %collective-permute-start.8 = (bf16[3,128,128]{2,1,0:T(8,128)(2,1)}, bf16[3,128,128]{2,1,0:T(8,128)(2,1)S(1)}, u32[]{:S(2)}, u32[]{:S(2)}) collective-permute-start(bf16[3,128,128]{2,1,0:T(8,128)(2,1)} %get-tuple-element.18), channel_id=1, source_target_pairs={{0,20},{1,21},{2,22},{3,23},{4,16},{5,17},{6,18},{7,19},{8,28},{9,... | collective-permute-start | bytes 294920 | tf_op jit(solution)/shard_map/ppermute | solution.py:211
  12.9 13.6 %collective-permute-start.10 = (bf16[3,128,128]{2,1,0:T(8,128)(2,1)}, bf16[3,128,128]{2,1,0:T(8,128)(2,1)S(1)}, u32[]{:S(2)}, u32[]{:S(2)}) collective-permute-start(bf16[3,128,128]{2,1,0:T(8,128)(2,1)} %get-tuple-element.19), channel_id=1, source_target_pairs={{0,24},{1,25},{2,26},{3,27},{4,28},{5,29},{6,30},{7,31},{8,16},{9,... | collective-permute-start | bytes 294920 | tf_op jit(solution)/shard_map/ppermute | solution.py:211
  16.1 11.9 %collective-permute-start.12 = (bf16[3,128,128]{2,1,0:T(8,128)(2,1)}, bf16[3,128,128]{2,1,0:T(8,128)(2,1)S(1)}, u32[]{:S(2)}, u32[]{:S(2)}) collective-permute-start(bf16[3,128,128]{2,1,0:T(8,128)(2,1)} %get-tuple-element.20), channel_id=1, source_target_pairs={{0,28},{1,29},{2,30},{3,31},{4,24},{5,25},{6,26},{7,27},{8,20},{9,... | collective-permute-start | bytes 294920 | tf_op jit(solution)/shard_map/ppermute | solution.py:211
  18.0 19.6 %collective-permute-start.5 = (bf16[2,3,128,128]{3,2,1,0:T(8,128)(2,1)S(1)}, bf16[2,3,128,128]{3,2,1,0:T(8,128)(2,1)S(1)}, u32[]{:S(2)}, u32[]{:S(2)}) collective-permute-start(bf16[2,3,128,128]{3,2,1,0:T(8,128)(2,1)S(1)} %pad_maximum_fusion.4), channel_id=1, source_target_pairs={{0,1},{1,0},{2,3},{3,2},{4,5},{5,4},{6,7},{7,6},{8,9},{9,8},{10,11... | collective-permute-start | bytes 589832 | tf_op jit(solution)/shard_map/ppermute | solution.py:211
  19.5 10.1 %collective-permute-start.7 = (bf16[3,128,128]{2,1,0:T(8,128)(2,1)S(1)}, bf16[3,128,128]{2,1,0:T(8,128)(2,1)S(1)}, u32[]{:S(2)}, u32[]{:S(2)}) collective-permute-start(bf16[3,128,128]{2,1,0:T(8,128)(2,1)S(1)} %collective-permute-done.6), channel_id=1, source_target_pairs={{0,1},{1,0},{2,3},{3,2},{4,5},{5,4},{6,7},{7,6},{8,9},{9,8},{10,11... | collective-permute-start | bytes 294920 | tf_op jit(solution)/shard_map/ppermute | solution.py:211
  25.0 5.3 %collective-permute-start.9 = (bf16[3,128,128]{2,1,0:T(8,128)(2,1)S(1)}, bf16[3,128,128]{2,1,0:T(8,128)(2,1)S(1)}, u32[]{:S(2)}, u32[]{:S(2)}) collective-permute-start(bf16[3,128,128]{2,1,0:T(8,128)(2,1)S(1)} %collective-permute-done.8), channel_id=1, source_target_pairs={{0,1},{1,0},{2,3},{3,2},{4,5},{5,4},{6,7},{7,6},{8,9},{9,8},{10,11... | collective-permute-start | bytes 294920 | tf_op jit(solution)/shard_map/ppermute | solution.py:211
  26.6 5.3 %collective-permute-start.11 = (bf16[3,128,128]{2,1,0:T(8,128)(2,1)S(1)}, bf16[3,128,128]{2,1,0:T(8,128)(2,1)S(1)}, u32[]{:S(2)}, u32[]{:S(2)}) collective-permute-start(bf16[3,128,128]{2,1,0:T(8,128)(2,1)S(1)} %collective-permute-done.10), channel_id=1, source_target_pairs={{0,1},{1,0},{2,3},{3,2},{4,5},{5,4},{6,7},{7,6},{8,9},{9,8},{10,11... | collective-permute-start | bytes 294920 | tf_op jit(solution)/shard_map/ppermute | solution.py:211
  28.0 4.9 %collective-permute-start.13 = (bf16[3,128,128]{2,1,0:T(8,128)(2,1)S(1)}, bf16[3,128,128]{2,1,0:T(8,128)(2,1)S(1)}, u32[]{:S(2)}, u32[]{:S(2)}) collective-permute-start(bf16[3,128,128]{2,1,0:T(8,128)(2,1)S(1)} %collective-permute-done.12), channel_id=1, source_target_pairs={{0,1},{1,0},{2,3},{3,2},{4,5},{5,4},{6,7},{7,6},{8,9},{9,8},{10,11... | collective-permute-start | bytes 294920 | tf_op jit(solution)/shard_map/ppermute | solution.py:211
  29.7 4.9 %collective-permute-start = (bf16[3,128,128]{2,1,0:T(8,128)(2,1)}, bf16[3,128,128]{2,1,0:T(8,128)(2,1)S(1)}, u32[]{:S(2)}, u32[]{:S(2)}) collective-permute-start(bf16[3,128,128]{2,1,0:T(8,128)(2,1)} %get-tuple-element.13), channel_id=1, source_target_pairs={{0,1},{1,0},{2,3},{3,2},{4,5},{5,4},{6,7},{7,6},{8,9},{9,8},{10,11... | collective-permute-start | bytes 294920 | tf_op jit(solution)/shard_map/ppermute | solution.py:211
  30.3 9.2 %collective-permute-start.16 = (bf16[4,3,128,128]{3,2,1,0:T(8,128)(2,1)S(1)}, bf16[4,3,128,128]{3,2,1,0:T(8,128)(2,1)S(1)}, u32[]{:S(2)}, u32[]{:S(2)}) collective-permute-start(bf16[4,3,128,128]{3,2,1,0:T(8,128)(2,1)S(1)} %pad_maximum_fusion.2.refs_0_), channel_id=1, source_target_pairs={{0,2},{1,3},{2,0},{3,1},{4,6},{5,7},{6,4},{7,5},{8,10},{9,11},{10,... | collective-permute-start | bytes 1179656 | tf_op jit(solution)/shard_map/ppermute | solution.py:211
  31.9 7.7 %collective-permute-start.17 = (bf16[4,3,128,128]{3,2,1,0:T(8,128)(2,1)S(1)}, bf16[4,3,128,128]{3,2,1,0:T(8,128)(2,1)S(1)}, u32[]{:S(2)}, u32[]{:S(2)}) collective-permute-start(bf16[4,3,128,128]{3,2,1,0:T(8,128)(2,1)S(1)} %pad_maximum_fusion.3.refs_1_), channel_id=1, source_target_pairs={{0,2},{1,3},{2,0},{3,1},{4,6},{5,7},{6,4},{7,5},{8,10},{9,11},{10,... | collective-permute-start | bytes 1179656 | tf_op jit(solution)/shard_map/ppermute | solution.py:211
  32.9 4.6 %collective-permute-start.2 = (bf16[3,128,128]{2,1,0:T(8,128)(2,1)S(1)}, bf16[3,128,128]{2,1,0:T(8,128)(2,1)S(1)}, u32[]{:S(2)}, u32[]{:S(2)}) collective-permute-start(bf16[3,128,128]{2,1,0:T(8,128)(2,1)S(1)} %collective-permute-done.1), channel_id=1, source_target_pairs={{0,1},{1,0},{2,3},{3,2},{4,5},{5,4},{6,7},{7,6},{8,9},{9,8},{10,11... | collective-permute-start | bytes 294920 | tf_op jit(solution)/shard_map/ppermute | solution.py:211
  34.6 9.9 %collective-permute-start.15 = (bf16[4,3,128,128]{3,2,1,0:T(8,128)(2,1)S(1)}, bf16[4,3,128,128]{3,2,1,0:T(8,128)(2,1)S(1)}, u32[]{:S(2)}, u32[]{:S(2)}) collective-permute-start(bf16[4,3,128,128]{3,2,1,0:T(8,128)(2,1)S(1)} %pad_maximum_fusion.1.refs_1_), channel_id=1, source_target_pairs={{0,2},{1,3},{2,0},{3,1},{4,6},{5,7},{6,4},{7,5},{8,10},{9,11},{10,... | collective-permute-start | bytes 1179656 | tf_op jit(solution)/shard_map/ppermute | solution.py:211
  37.6 6.9 %collective-permute-start.14 = (bf16[4,3,128,128]{3,2,1,0:T(8,128)(2,1)S(1)}, bf16[4,3,128,128]{3,2,1,0:T(8,128)(2,1)S(1)}, u32[]{:S(2)}, u32[]{:S(2)}) collective-permute-start(bf16[4,3,128,128]{3,2,1,0:T(8,128)(2,1)S(1)} %pad_maximum_fusion.refs_0_), channel_id=1, source_target_pairs={{0,2},{1,3},{2,0},{3,1},{4,6},{5,7},{6,4},{7,5},{8,10},{9,11},{10,... | collective-permute-start | bytes 1179656 | tf_op jit(solution)/shard_map/ppermute | solution.py:211

commit v4 on v3

--- a/solution.py
+++ b/solution.py
@@ -68,119 +68,174 @@
     )(screening, tile_slot, factors)
 
 
-def ladder_kernel(dims, last, screening, tile_slot, occ, virt, amp, *refs):
+def plan_kernel(dims, screening, tile_slot, occ, virt, table, row_den, col_e):
     tile_dev, group, row_tiles, shifts, tile = dims
-    bufs, refs = refs[:4], refs[4:]
-    if last:
-        before, out, left, place, row_den, held, sems = refs
-    else:
-        out, left, place = refs
     me, cut = lax.axis_index("pair"), lax.axis_index("cuts")
     pair_id, core = me // group, me % group
-    count, n_q = screening.shape[1], left.shape[1]
+    count = screening.shape[1]
     first = core * (count // group) + cut * row_tiles
-    half = shifts // 2
-
-    for t in range(count):
+
+    def source(t):
         slot = tile_slot[screening[pair_id, t]]
         owner = slot // tile_dev
         shift = (owner // group) ^ pair_id
-        place[shift + (owner % group ^ core) * shifts] = t
+        return shift + (owner % group ^ core) * shifts
+
+    for t in range(count):
+        n = source(t)
+        table[n] = t
+        col_e[pl.ds(n, 1), :] = virt[pl.ds(screening[pair_id, t], 1), :] - occ[1]
     for i in range(row_tiles):
-        slot = tile_slot[screening[pair_id, first + i]]
-        owner = slot // tile_dev
-        shift = (owner // group) ^ pair_id
-        which = shift // half + (owner % group ^ core) * 2
-        for n, buf in enumerate(bufs):
-
-            @pl.when(which == n)
-            def _():
-                left[i] = buf[shift % half]
-
-        if last:
-            row = virt[pl.ds(screening[pair_id, first + i], 1), :] - occ[0]
-            row_den[i] = jnp.broadcast_to(row, (tile, tile)).T
-
-    writes = []
-    for source in range(0, count, 2):
-        pair = [(n, bufs[n // half][n % half], place[n]) for n in (source, source + 1)]
-        offsets = [pl.multiple_of(at * tile, tile) for _, _, at in pair]
-        halves = []
-        for i in range(row_tiles):
-            rows = slice(i * tile, (i + 1) * tile)
-            block = jnp.concatenate([amp[rows, pl.ds(x, tile)] for x in offsets], axis=1)
-            lhs = left[i].reshape(n_q * tile, tile)
-            half_done = jnp.dot(lhs, block, preferred_element_type=jnp.float32)
-            halves.append(half_done.astype(jnp.bfloat16))
-        lhs = jnp.concatenate(
+        table[count + i] = source(first + i)
+        row = virt[pl.ds(screening[pair_id, first + i], 1), :] - occ[0]
+        row_den[i] = jnp.broadcast_to(row, (tile, tile)).T
+
+
+def plan(screening, tile_slot, occ, virt, dims):
+    _, _, row_tiles, _, tile = dims
+    count = screening.shape[1]
+    return pl.pallas_call(
+        functools.partial(plan_kernel, dims),
+        out_shape=[
+            jax.ShapeDtypeStruct((count + row_tiles,), jnp.int32),
+            jax.ShapeDtypeStruct((row_tiles, tile, tile), jnp.float32),
+            jax.ShapeDtypeStruct((count, tile), jnp.float32),
+        ],
+        in_specs=[SMEM, SMEM, SMEM, VMEM],
+        out_specs=[SMEM, VMEM, VMEM],
+        compiler_params=pltpu.CompilerParams(vmem_limit_bytes=4 * 2**20),
+        name="plan",
+    )(screening, tile_slot, occ, virt)
+
+
+def columns_of(bufs):
+    return [(buf, n) for buf in bufs for n in range(buf.shape[0])]
+
+
+def right_product(base, dims, table, amp, bufs, out):
+    _, _, row_tiles, shifts, tile = dims
+    sources = columns_of(bufs)
+    half = len(sources) // 2
+    zero = jnp.zeros((tile, tile), jnp.bfloat16)
+    for m in range(0, len(sources), 2):
+        pair, block = [], []
+        for n in (m, m + 1):
+            buf, k = sources[n]
+            pair.append(buf[k])
+            at = table[base + n % half + n // half * shifts]
+            block.append(amp[:, pl.ds(pl.multiple_of(at * tile, tile), tile)])
+        n_q = pair[0].shape[0]
+        rhs = jnp.concatenate(
             [
-                jnp.concatenate([h[q * tile : (q + 1) * tile] for q in range(n_q)], axis=1)
-                for h in halves
+                jnp.concatenate(((x[q], zero), (zero, x[q]))[j], axis=1)
+                for q in range(n_q)
+                for j, x in enumerate(pair)
             ],
             axis=0,
         )
-        zero = jnp.zeros((tile, tile), jnp.bfloat16)
-        rhs = jnp.concatenate(
-            [
-                jnp.concatenate(
-                    [x for q in range(n_q) for x in ((tiles[q], zero), (zero, tiles[q]))[j]],
-                    axis=1,
+        done = lax.dot_general(
+            jnp.concatenate(block, axis=1),
+            rhs,
+            (((1,), (1,)), ((), ())),
+            preferred_element_type=jnp.float32,
+        ).astype(jnp.bfloat16)
+        for i in range(row_tiles):
+            for q in range(n_q):
+                out[i, q, :, m * tile : (m + 2) * tile] = done[
+                    i * tile : (i + 1) * tile, q * 2 * tile : (q + 1) * 2 * tile
+                ]
+
+
+def right_kernel(base, dims, table, amp, *refs):
+    *bufs, out = refs
+    right_product(base, dims, table, amp, bufs, out)
+
+
+def product_shape(dims, bufs):
+    _, _, row_tiles, shifts, tile = dims
+    return (row_tiles, bufs[0].shape[1], tile, shifts * tile)
+
+
+def right(base, dims, table, amp, bufs):
+    shape = product_shape(dims, bufs)
+    flops = 2 * amp.shape[0] * shape[1] * shape[3] * shape[2]
+    return pl.pallas_call(
+        functools.partial(right_kernel, base, dims),
+        out_shape=jax.ShapeDtypeStruct(shape, jnp.bfloat16),
+        in_specs=[SMEM] + [VMEM] * (1 + len(bufs)),
+        out_specs=VMEM,
+        compiler_params=pltpu.CompilerParams(vmem_limit_bytes=10 * 2**20),
+        cost_estimate=pl.CostEstimate(flops=flops, bytes_accessed=0, transcendentals=0),
+        name="right",
+    )(table, amp, *bufs)
+
+
+def left_kernel(dims, sizes, table, row_den, col_e, amp, *refs):
+    _, _, row_tiles, shifts, tile = dims
+    own, cross, refs = refs[:sizes], refs[sizes : 2 * sizes], refs[2 * sizes :]
+    near_own, far_own, near_cross, out, far_cross, left, held, sems = refs
+    half = shifts // 2
+    n_q = own[0].shape[1]
+    bounds = [0]
+    for buf in own:
+        bounds.append(bounds[-1] + buf.shape[0])
+    for i in range(row_tiles):
+        source = table[2 * shifts + i]
+        shift, other = source % shifts, source // shifts
+        rank = jnp.where(shift < half, 0, shifts) + other * half + shift % half
+        for n in range(sizes):
+
+            @pl.when((rank >= bounds[n]) & (rank < bounds[n + 1]))
+            def _():
+                for q in range(n_q):
+                    left[i, :, q * tile : (q + 1) * tile] = own[n][rank - bounds[n], q]
+                    at = (n_q + q) * tile
+                    left[i, :, at : at + tile] = cross[n][rank - bounds[n], q]
+
+    far = [buf for n, buf in enumerate(cross) if bounds[n] >= shifts]
+    right_product(half, dims, table, amp, far, far_cross)
+    writes = []
+    for part, pieces in enumerate(((near_own, near_cross), (far_own, far_cross))):
+        for m in range(0, shifts, 2):
+            cols = slice(m * tile, (m + 2) * tile)
+            ids = [part * half + n % half + n // half * shifts for n in (m, m + 1)]
+            for i in range(row_tiles):
+                rhs = jnp.concatenate(
+                    [x[i, q, :, cols] for x in pieces for q in range(n_q)], axis=0
                 )
-                for j, (_, tiles, _) in enumerate(pair)
-            ],
-            axis=0,
-        )
-        both = lax.dot_general(
-            lhs, rhs, (((1,), (1,)), ((), ())), preferred_element_type=jnp.float32
-        )
-        for j, (n, _, at) in enumerate(pair):
-            acc = both[:, j * tile : (j + 1) * tile]
-            if not last:
-                out[n] = acc
-                continue
-            acc = acc + before[n]
-            col_e = virt[pl.ds(screening[pair_id, at], 1), :] - occ[1]
-            for i in range(row_tiles):
-                rows = slice(i * tile, (i + 1) * tile)
-                held[n, rows, :] = acc[rows] / (row_den[i] + col_e)
-            copy = pltpu.make_async_copy(held.at[n], out.at[:, pl.ds(offsets[j], tile)], sems.at[n])
-            copy.start()
-            writes.append(copy)
+                acc = jnp.dot(left[i], rhs, preferred_element_type=jnp.float32)
+                for j, n in enumerate(ids):
+                    den = row_den[i] + col_e[n : n + 1, :]
+                    held[n, i * tile : (i + 1) * tile, :] = (
+                        acc[:, j * tile : (j + 1) * tile] / den
+                    )
+            for n in ids:
+                at = pl.ds(pl.multiple_of(table[n] * tile, tile), tile)
+                copy = pltpu.make_async_copy(held.at[n], out.at[:, at], sems.at[n])
+                copy.start()
+                writes.append(copy)
     for copy in writes:
         copy.wait()
 
 
-def ladder(screening, tile_slot, occ, virt, amp, tiles, dims, before=None):
-    _, _, row_tiles, _, tile = dims
-    count, columns = screening.shape[1], amp.shape[1]
-    rows = row_tiles * tile
-    last = before is not None
-    n_q = tiles[0].shape[1]
-    scratch = [
-        pltpu.VMEM((row_tiles, n_q, tile, tile), jnp.bfloat16),
-        pltpu.SMEM((count,), jnp.int32),
-    ]
-    if last:
-        scratch += [
-            pltpu.VMEM((row_tiles, tile, tile), jnp.float32),
+def left_product(dims, table, row_den, col_e, amp, own, cross, done):
+    _, _, row_tiles, shifts, tile = dims
+    rows, columns = amp.shape
+    count, n_q = 2 * shifts, own[0].shape[1]
+    return pl.pallas_call(
+        functools.partial(left_kernel, dims, len(own)),
+        out_shape=jax.ShapeDtypeStruct((rows, columns), jnp.float32),
+        in_specs=[SMEM] + [VMEM] * (3 + 2 * len(own) + len(done)),
+        out_specs=ANY,
+        scratch_shapes=[
+            pltpu.VMEM(product_shape(dims, own), jnp.bfloat16),
+            pltpu.VMEM((row_tiles, tile, 2 * n_q * tile), jnp.bfloat16),
             pltpu.VMEM((count, rows, tile), jnp.float32),
             pltpu.SemaphoreType.DMA((count,)),
-        ]
-        out = jax.ShapeDtypeStruct((rows, columns), jnp.float32)
-    else:
-        out = jax.ShapeDtypeStruct((count, rows, tile), jnp.float32)
-    extra = [before] if last else []
-    flops = 4 * n_q * rows * columns * tile
-    return pl.pallas_call(
-        functools.partial(ladder_kernel, dims, last),
-        out_shape=out,
-        in_specs=[SMEM, SMEM, SMEM] + [VMEM] * (6 + len(extra)),
-        out_specs=ANY if last else VMEM,
-        scratch_shapes=scratch,
-        compiler_params=pltpu.CompilerParams(vmem_limit_bytes=26 * 2**20),
-        cost_estimate=pl.CostEstimate(flops=flops, bytes_accessed=0, transcendentals=0),
-        name="ladder_last" if last else "ladder_first",
-    )(screening, tile_slot, occ, virt, amp, *tiles, *extra)
+        ],
+        compiler_params=pltpu.CompilerParams(vmem_limit_bytes=24 * 2**20),
+        name="left",
+    )(table, row_den, col_e, amp, *own, *cross, *done)
 
 
 def crossings(shifts):
@@ -230,13 +285,20 @@
     rows = row_tiles * tile
     amp = lax.dynamic_slice_in_dim(amplitudes, lax.axis_index("cuts") * rows, rows, 0)
     dims = (tile_dev, group, row_tiles, shifts, tile)
-    out = None
-    for held in (got, crossed):
-        near = jnp.stack(held[:half])
-        far = jnp.stack(held[half:])
-        tiles = [near, far, over(near), over(far)]
-        out = ladder(screening, tile_slot, occ, virtual_energy, amp, tiles, dims, out)
-    return out
+    table, row_den, col_e = plan(screening, tile_slot, occ, virtual_energy, dims)
+    quarter = half + half // 2
+    sides, done = [], []
+    for n, held in enumerate((got, crossed)):
+        mine, other = [], []
+        for lo, hi in ((0, half), (half, quarter), (quarter, shifts)):
+            mine.append(jnp.stack(held[lo:hi]))
+            other.append(over(mine[-1]))
+        near, far = [mine[0], other[0]], mine[1:] + other[1:]
+        sides.append(near + far)
+        for m, (base, bufs) in enumerate(((0, near), (half, far))):
+            if (n, m) != (1, 1):
+                done.append(right(base, dims, table, amp, bufs))
+    return left_product(dims, table, row_den, col_e, amp, *sides, done)
 
 
 def general(

time: 50.9 us -> 61.4 us (1.21)
  the two profiles are of different devices: /device:TPU:0 before, /device:TPU:21 now
where the time goes in v4:
time: 61.4 us; the launch traced here: 61 us
  waiting for transfers between devices  20.6 us (34%)
  starting transfers between devices  19.1 us (31%)
  Pallas kernels  15.4 us (25%)
  local copies, waits for them, and re-layouts  3.28 us (5%)
  other arithmetic  2.43 us (4%)
    ppermute x20, waiting for transfers between devices, send(): return lax.ppermute(x, BOTH, pairs)  20.6 us
    ppermute x20, starting transfers between devices, send(): return lax.ppermute(x, BOTH, pairs)  19.1 us
    pallas_call x3, Pallas kernels, right(): pl.pallas_call(functools.partial(right_kernel, base, dims), out_shape=jax...  6.03 us
    pallas_call x1, Pallas kernels, left_product(): pl.pallas_call(functools.partial(left_kernel, dims, len(own)), out_shape=...  5.9 us
    another operation x6, other arithmetic, direct(): mine.append(jnp.stack(held[lo:hi]))  2.4 us
    pallas_call x1, Pallas kernels, pick(): pl.pallas_call(functools.partial(pick_kernel, tile_dev, group), out_shape...  2.01 us
    dynamic_slice x1, local copies, waits for them, and re-layouts, direct(): lax.dynamic_slice_in_dim(amplitudes, lax.axis_index('cuts') * rows, rows, 0)  1.75 us
    pallas_call x1, Pallas kernels, plan(): pl.pallas_call(functools.partial(plan_kernel, dims), out_shape=[jax.Shape...  1.5 us
  transfers between devices with their start and end apart: 20, of which 5 were waited for; matrix products, arithmetic and copies ran while one was open for 9% of the time, Pallas kernels for 12%

profile of v4, /device:TPU:21, one launch (start us, length us, event | category | flops | bytes accessed | tf_op | source)
XLA Modules:
  0.0 61.0 jit_solution(7300777480766504567)
XLA Ops:
  0.0 2.0 %pick.1 = (bf16[3,128,128]{2,1,0:T(8,128)(2,1)}, bf16[3,128,128]{2,1,0:T(8,128)(2,1)}, bf16[3,128,128]{2,1,0:T(8,128)(2,1)}, bf16[3,128,128]{2,1,0:T(8,128)(2,1)...) custom-call(s32[8,16]{1,0:T(8,128)} %screening.3, ...), custom_call_target="tpu_custom_call" | custom-call | tf_op jit(solution)/shard_map/pick/pallas_call | solution.py:56
  2.0 0.0 copy-start.4
  2.1 1.3 %collective-permute-start = (bf16[3,128,128]{2,1,0:T(8,128)(2,1)}, bf16[3,128,128]{2,1,0:T(8,128)(2,1)S(1)}, u32[]{:S(2)}, u32[]{:S(2)}) collective-permute-start(bf16[3,128,128]{2,1,0:T(8,128)(2,1)} %get-tuple-element.20), channel_id=1, source_target_pairs={{0,4},{1,5},{2,6},{3,7},{4,0},{5,1},{6,2},{7,3},{8,12},{9,13},{10,... | collective-permute-start | bytes 294920 | tf_op jit(solution)/shard_map/ppermute | solution.py:266
  3.3 1.3 %collective-permute-start.1 = (bf16[3,128,128]{2,1,0:T(8,128)(2,1)}, bf16[3,128,128]{2,1,0:T(8,128)(2,1)S(1)}, u32[]{:S(2)}, u32[]{:S(2)}) collective-permute-start(bf16[3,128,128]{2,1,0:T(8,128)(2,1)} %get-tuple-element.21), channel_id=1, source_target_pairs={{0,8},{1,9},{2,10},{3,11},{4,12},{5,13},{6,14},{7,15},{8,0},{9,1},... | collective-permute-start | bytes 294920 | tf_op jit(solution)/shard_map/ppermute | solution.py:266
  4.6 0.1 collective-permute-start.2
  4.8 0.1 collective-permute-start.4
  4.8 3.2 %collective-permute-start.5 = (bf16[3,128,128]{2,1,0:T(8,128)(2,1)}, bf16[3,128,128]{2,1,0:T(8,128)(2,1)S(1)}, u32[]{:S(2)}, u32[]{:S(2)}) collective-permute-start(bf16[3,128,128]{2,1,0:T(8,128)(2,1)} %get-tuple-element.24), channel_id=1, source_target_pairs={{0,20},{1,21},{2,22},{3,23},{4,16},{5,17},{6,18},{7,19},{8,28},{9,... | collective-permute-start | bytes 294920 | tf_op jit(solution)/shard_map/ppermute | solution.py:266
  8.1 0.9 %dynamic-slice_reduce_fusion = s32[2]{0:T(128)S(1)} fusion(s32[8,2]{0,1:T(2,128)} %param.11, s32[]{:T(128)S(6)} %select_n.22), kind=kLoop, calls=%fused_computation.10 | loop fusion | bytes 20 | tf_op jit(solution)/shard_map/dynamic_slice | solution.py:284
  8.9 0.0 copy-start.2
  8.9 0.0 copy-start.3
  9.0 1.7 %constant_dynamic-slice_fusion.amp = bf16[512,2048]{1,0:T(8,128)(2,1)S(1)} fusion(bf16[1024,2048]{1,0:T(8,128)(2,1)} %param.7, s32[]{:T(128)S(6)} %select_n.24), kind=kLoop, calls=%fused_computation.12 | loop fusion | bytes 4194308 | tf_op jit(solution)/shard_map/dynamic_slice | solution.py:286
  10.7 0.2 collective-permute-start.6
  11.0 0.0 collective-permute-done.2
  11.0 1.3 %collective-permute-start.7 = (bf16[3,128,128]{2,1,0:T(8,128)(2,1)S(1)}, bf16[3,128,128]{2,1,0:T(8,128)(2,1)S(1)}, u32[]{:S(2)}, u32[]{:S(2)}) collective-permute-start(bf16[3,128,128]{2,1,0:T(8,128)(2,1)S(1)} %copy-done.6), channel_id=1, source_target_pairs={{0,28},{1,29},{2,30},{3,31},{4,24},{5,25},{6,26},{7,27},{8,20},{9,... | collective-permute-start | bytes 294920 | tf_op jit(solution)/shard_map/ppermute | solution.py:266
  12.3 9.8 %collective-permute-done.6 = bf16[3,128,128]{2,1,0:T(8,128)(2,1)S(1)} collective-permute-done((bf16[3,128,128]{2,1,0:T(8,128)(2,1)S(1)}, bf16[3,128,128]{2,1,0:T(8,128)(2,1)S(1)}, u32[]{:S(2)}, u32[]{:S(2)}) %collective-permute-start.6) | collective-permute-done | bytes 98336 | tf_op jit(solution)/shard_map/ppermute | solution.py:266
  22.0 0.2 collective-permute-start.10
  22.3 3.3 %collective-permute-done.7 = bf16[3,128,128]{2,1,0:T(8,128)(2,1)S(1)} collective-permute-done((bf16[3,128,128]{2,1,0:T(8,128)(2,1)S(1)}, bf16[3,128,128]{2,1,0:T(8,128)(2,1)S(1)}, u32[]{:S(2)}, u32[]{:S(2)}) %collective-permute-start.7) | collective-permute-done | bytes 98336 | tf_op jit(solution)/shard_map/ppermute | solution.py:266
  25.5 0.2 collective-permute-start.12
  25.8 1.6 %collective-permute-start.9 = (bf16[2,3,128,128]{3,2,1,0:T(8,128)(2,1)S(1)}, bf16[2,3,128,128]{3,2,1,0:T(8,128)(2,1)S(1)}, u32[]{:S(2)}, u32[]{:S(2)}) collective-permute-start(bf16[2,3,128,128]{3,2,1,0:T(8,128)(2,1)S(1)} %pad_maximum_fusion.3.refs_1_.refs_3_), channel_id=1, source_target_pairs={{0,2},{1,3},{2,0},{3,1},{4,6},{5,7},{6,4},{7,5},{8,10},{9,11},{10,... | collective-permute-start | bytes 589832 | tf_op jit(solution)/shard_map/ppermute | solution.py:266
  27.4 0.1 pad_maximum_fusion.refs_0_
  27.5 0.1 collective-permute-start.3
  27.6 0.0 collective-permute-done.5
  27.6 0.0 copy-start.5
  27.6 1.3 %collective-permute-start.11 = (bf16[3,128,128]{2,1,0:T(8,128)(2,1)S(1)}, bf16[3,128,128]{2,1,0:T(8,128)(2,1)S(1)}, u32[]{:S(2)}, u32[]{:S(2)}) collective-permute-start(bf16[3,128,128]{2,1,0:T(8,128)(2,1)S(1)} %collective-permute-done), channel_id=1, source_target_pairs={{0,1},{1,0},{2,3},{3,2},{4,5},{5,4},{6,7},{7,6},{8,9},{9,8},{10,11... | collective-permute-start | bytes 294920 | tf_op jit(solution)/shard_map/ppermute | solution.py:266
  28.9 0.9 %pad_maximum_fusion.2.refs_0_.refs_2_ = bf16[2,3,128,128]{3,2,1,0:T(8,128)(2,1)S(1)} fusion(bf16[1,3,128,128]{3,2,1,0:T(8,128)(2,1)S(1)} %bitcast.26, bf16[1,3,128,128]{3,2,1,0:T(8,128)(2,1)} %bitcast.5), kind=kLoop, calls=%fused_computation.3 | loop fusion | flops 98304 | bytes 393216 | tf_op jit(solution)/shard_map/stack | solution.py:294
  29.8 0.0 collective-permute-done.10
  29.8 0.3 collective-permute-start.14
  30.1 4.4 %collective-permute-done.11 = bf16[3,128,128]{2,1,0:T(8,128)(2,1)S(1)} collective-permute-done((bf16[3,128,128]{2,1,0:T(8,128)(2,1)S(1)}, bf16[3,128,128]{2,1,0:T(8,128)(2,1)S(1)}, u32[]{:S(2)}, u32[]{:S(2)}) %collective-permute-start.11) | collective-permute-done | bytes 98336 | tf_op jit(solution)/shard_map/ppermute | solution.py:266
  34.6 0.2 collective-permute-start.16
  34.8 1.2 %collective-permute-start.17 = (bf16[3,128,128]{2,1,0:T(8,128)(2,1)S(1)}, bf16[3,128,128]{2,1,0:T(8,128)(2,1)S(1)}, u32[]{:S(2)}, u32[]{:S(2)}) collective-permute-start(bf16[3,128,128]{2,1,0:T(8,128)(2,1)S(1)} %collective-permute-done.7), channel_id=1, source_target_pairs={{0,1},{1,0},{2,3},{3,2},{4,5},{5,4},{6,7},{7,6},{8,9},{9,8},{10,11... | collective-permute-start | bytes 294920 | tf_op jit(solution)/shard_map/ppermute | solution.py:266
  36.1 2.2 %collective-permute-done.16 = bf16[3,128,128]{2,1,0:T(8,128)(2,1)S(1)} collective-permute-done((bf16[3,128,128]{2,1,0:T(8,128)(2,1)S(1)}, bf16[3,128,128]{2,1,0:T(8,128)(2,1)S(1)}, u32[]{:S(2)}, u32[]{:S(2)}) %collective-permute-start.16) | collective-permute-done | bytes 98336 | tf_op jit(solution)/shard_map/ppermute | solution.py:266
  38.3 0.2 collective-permute-start.15
  38.5 0.8 %collective-permute-done.17 = bf16[3,128,128]{2,1,0:T(8,128)(2,1)S(1)} collective-permute-done((bf16[3,128,128]{2,1,0:T(8,128)(2,1)S(1)}, bf16[3,128,128]{2,1,0:T(8,128)(2,1)S(1)}, u32[]{:S(2)}, u32[]{:S(2)}) %collective-permute-start.17) | collective-permute-done | bytes 98336 | tf_op jit(solution)/shard_map/ppermute | solution.py:266
  39.4 3.8 %collective-permute-start.13 = (bf16[4,3,128,128]{3,2,1,0:T(8,128)(2,1)S(1)}, bf16[4,3,128,128]{3,2,1,0:T(8,128)(2,1)}, u32[]{:S(2)}, u32[]{:S(2)}) collective-permute-start(bf16[4,3,128,128]{3,2,1,0:T(8,128)(2,1)S(1)} %pad_maximum_fusion.1.refs_0_.refs_6_), channel_id=1, source_target_pairs={{0,2},{1,3},{2,0},{3,1},{4,6},{5,7},{6,4},{7,5},{8,10},{9,11},{10,... | collective-permute-start | bytes 1179656 | tf_op jit(solution)/shard_map/ppermute | solution.py:266
  43.1 0.7 %pad_maximum_fusion.6.refs_9_ = bf16[2,3,128,128]{3,2,1,0:T(8,128)(2,1)} fusion(bf16[1,3,128,128]{3,2,1,0:T(8,128)(2,1)S(1)} %bitcast.32, bf16[1,3,128,128]{3,2,1,0:T(8,128)(2,1)S(1)} %bitcast.30), kind=kLoop, calls=%fused_computation.7 | loop fusion | flops 98304 | bytes 393216 | tf_op jit(solution)/shard_map/stack | solution.py:294
  43.8 0.0 collective-permute-start.8
  43.8 0.0 collective-permute-done.15
  43.8 2.3 %collective-permute-start.19 = (bf16[2,3,128,128]{3,2,1,0:T(8,128)(2,1)}, bf16[2,3,128,128]{3,2,1,0:T(8,128)(2,1)}, u32[]{:S(2)}, u32[]{:S(2)}) collective-permute-start(bf16[2,3,128,128]{3,2,1,0:T(8,128)(2,1)} %pad_maximum_fusion.6.refs_9_), channel_id=1, source_target_pairs={{0,2},{1,3},{2,0},{3,1},{4,6},{5,7},{6,4},{7,5},{8,10},{9,11},{10,... | collective-permute-start | bytes 589832 | tf_op jit(solution)/shard_map/ppermute | solution.py:266
  46.2 0.7 %pad_maximum_fusion.5.refs_8_ = bf16[2,3,128,128]{3,2,1,0:T(8,128)(2,1)} fusion(bf16[1,3,128,128]{3,2,1,0:T(8,128)(2,1)S(1)} %bitcast.31, bf16[1,3,128,128]{3,2,1,0:T(8,128)(2,1)S(1)} %bitcast.29), kind=kLoop, calls=%fused_computation.6 | loop fusion | flops 98304 | bytes 393216 | tf_op jit(solution)/shard_map/stack | solution.py:294
  46.9 0.0 collective-permute-done.9.refs_3_.refs_5_
  46.9 0.0 collective-permute-start.18
  46.9 0.6 %gather_fusion = f32[2]{0:T(128)S(1)} fusion(f32[4000]{0:T(1024)S(1)} %copy-done, s32[1024]{0:T(1024)S(1)} %pad_clamp_fusion), kind=kCustom, calls=%fused_computation | custom fusion | bytes 24 | tf_op jit(solution)/shard_map/gather | solution.py:284
  47.5 1.5 %plan.1 = (s32[20]{0:T(128)S(1)}, f32[4,128,128]{2,1,0:T(8,128)S(1)}, f32[16,128]{1,0:T(8,128)S(1)}) custom-call(s32[8,16]{1,0:T(8,128)S(1)} %copy-done.2, s32[32]{0:T(128)S(1)} %copy-done.3, f32[2]{0:T(128)S(1)} %gather_fusion, f32[32,128]{1,0:T(8,128)S(1)} %copy-done.1), custom_call_target="tpu_custom_call" | custom-call | tf_op jit(solution)/shard_map/plan/pallas_call | solution.py:97
  49.0 0.0 collective-permute-done.8.refs_2_.refs_4_
  49.0 2.0 %right.4.refs_13_ = bf16[4,3,128,1024]{3,2,1,0:T(8,128)(2,1)S(1)} custom-call(s32[20]{0:T(128)S(1)} %get-tuple-element.16.table, bf16[512,2048]{1,0:T(8,128)(2,1)S(1)} %constant_dynamic-slice_fusion.amp, bf16[2,3,128,128]{3,2,1,0:T(8,128)(2,1)S(1)} %pad_maximum_fusion.2.refs_0_.refs_2_, bf16[2,3,128,128]{3,2,1,0:T(8,128)(2,1)S(1)} %pad_maximum_fusion.3.refs_1_.refs_3_, ...), custom_call_target="tpu_custom_call" | custom-call | flops 402653184 | tf_op jit(solution)/shard_map/right/pallas_call | solution.py:162
  51.0 2.0 %right.3.refs_12_ = bf16[4,3,128,1024]{3,2,1,0:T(8,128)(2,1)S(1)} custom-call(s32[20]{0:T(128)S(1)} %get-tuple-element.16.table, bf16[512,2048]{1,0:T(8,128)(2,1)S(1)} %constant_dynamic-slice_fusion.amp, bf16[4,3,128,128]{3,2,1,0:T(8,128)(2,1)S(1)} %pad_maximum_fusion.refs_0_, bf16[4,3,128,128]{3,2,1,0:T(8,128)(2,1)} %collective-permute-done.3.refs_1_), custom_call_target="tpu_custom_call" | custom-call | flops 402653184 | tf_op jit(solution)/shard_map/right/pallas_call | solution.py:162
  53.1 2.0 %right.5.refs_14_ = bf16[4,3,128,1024]{3,2,1,0:T(8,128)(2,1)S(1)} custom-call(s32[20]{0:T(128)S(1)} %get-tuple-element.16.table, bf16[512,2048]{1,0:T(8,128)(2,1)S(1)} %constant_dynamic-slice_fusion.amp, bf16[4,3,128,128]{3,2,1,0:T(8,128)(2,1)S(1)} %pad_maximum_fusion.1.refs_0_.refs_6_, bf16[4,3,128,128]{3,2,1,0:T(8,128)(2,1)} %collective-permute-done.13.refs_1_.refs_7_), custom_call_target="tpu_custom_call" | custom-call | flops 402653184 | tf_op jit(solution)/shard_map/right/pallas_call | solution.py:162
  55.1 5.9 %left.1 = f32[512,2048]{1,0:T(8,128)} custom-call(s32[20]{0:T(128)S(1)} %get-tuple-element.16.table, f32[4,128,128]{2,1,0:T(8,128)S(1)} %get-tuple-element.17.row_den, f32[16,128]{1,0:T(8,128)S(1)} %get-tuple-element.18.col_e, bf16[512,2048]{1,0:T(8,128)(2,1)S(1)} %constant_dynamic-slice_fusion.amp, bf16[4,3,128,128]{3,2,1,0:T(8,128)(2,1)S(1)} %pad_maximum_fusion.refs_0_, ...), custom_call_target="tpu_custom_call" | custom-call | tf_op jit(solution)/shard_map/left/pallas_call | solution.py:225
  (26 shorter events, 0.1 us)
Async XLA Ops:
  0.0 46.9 %copy-start = (f32[4000]{0:T(1024)S(1)}, f32[4000]{0:T(1024)}, u32[]{:S(2)}) copy-start(f32[4000]{0:T(1024)} %param.12) | copy-start | bytes 48004
  2.0 8.7 %copy-start.7 = (bf16[3,128,128]{2,1,0:T(8,128)(2,1)S(1)}, bf16[3,128,128]{2,1,0:T(8,128)(2,1)}, u32[]{:S(2)}) copy-start(bf16[3,128,128]{2,1,0:T(8,128)(2,1)} %get-tuple-element.25) | copy-start | bytes 294916
  2.0 8.9 %copy-start.6 = (bf16[3,128,128]{2,1,0:T(8,128)(2,1)S(1)}, bf16[3,128,128]{2,1,0:T(8,128)(2,1)}, u32[]{:S(2)}) copy-start(bf16[3,128,128]{2,1,0:T(8,128)(2,1)} %get-tuple-element.26) | copy-start | bytes 294916
  2.0 20.0 %copy-start.4 = (bf16[3,128,128]{2,1,0:T(8,128)(2,1)S(1)}, bf16[3,128,128]{2,1,0:T(8,128)(2,1)}, u32[]{:S(2)}) copy-start(bf16[3,128,128]{2,1,0:T(8,128)(2,1)} %get-tuple-element.19) | copy-start | bytes 294916
  2.1 23.7 %collective-permute-start = (bf16[3,128,128]{2,1,0:T(8,128)(2,1)}, bf16[3,128,128]{2,1,0:T(8,128)(2,1)S(1)}, u32[]{:S(2)}, u32[]{:S(2)}) collective-permute-start(bf16[3,128,128]{2,1,0:T(8,128)(2,1)} %get-tuple-element.20), channel_id=1, source_target_pairs={{0,4},{1,5},{2,6},{3,7},{4,0},{5,1},{6,2},{7,3},{8,12},{9,13},{10,... | collective-permute-start | bytes 294920 | tf_op jit(solution)/shard_map/ppermute | solution.py:266
  3.3 7.4 %collective-permute-start.1 = (bf16[3,128,128]{2,1,0:T(8,128)(2,1)}, bf16[3,128,128]{2,1,0:T(8,128)(2,1)S(1)}, u32[]{:S(2)}, u32[]{:S(2)}) collective-permute-start(bf16[3,128,128]{2,1,0:T(8,128)(2,1)} %get-tuple-element.21), channel_id=1, source_target_pairs={{0,8},{1,9},{2,10},{3,11},{4,12},{5,13},{6,14},{7,15},{8,0},{9,1},... | collective-permute-start | bytes 294920 | tf_op jit(solution)/shard_map/ppermute | solution.py:266
  4.6 6.3 %collective-permute-start.2 = (bf16[3,128,128]{2,1,0:T(8,128)(2,1)}, bf16[3,128,128]{2,1,0:T(8,128)(2,1)S(1)}, u32[]{:S(2)}, u32[]{:S(2)}) collective-permute-start(bf16[3,128,128]{2,1,0:T(8,128)(2,1)} %get-tuple-element.22), channel_id=1, source_target_pairs={{0,12},{1,13},{2,14},{3,15},{4,8},{5,9},{6,10},{7,11},{8,4},{9,5},... | collective-permute-start | bytes 294920 | tf_op jit(solution)/shard_map/ppermute | solution.py:266
  4.8 22.7 %collective-permute-start.4 = (bf16[3,128,128]{2,1,0:T(8,128)(2,1)}, bf16[3,128,128]{2,1,0:T(8,128)(2,1)}, u32[]{:S(2)}, u32[]{:S(2)}) collective-permute-start(bf16[3,128,128]{2,1,0:T(8,128)(2,1)} %get-tuple-element.23), channel_id=1, source_target_pairs={{0,16},{1,17},{2,18},{3,19},{4,20},{5,21},{6,22},{7,23},{8,24},{9,... | collective-permute-start | bytes 294920 | tf_op jit(solution)/shard_map/ppermute | solution.py:266
  4.8 22.8 %collective-permute-start.5 = (bf16[3,128,128]{2,1,0:T(8,128)(2,1)}, bf16[3,128,128]{2,1,0:T(8,128)(2,1)S(1)}, u32[]{:S(2)}, u32[]{:S(2)}) collective-permute-start(bf16[3,128,128]{2,1,0:T(8,128)(2,1)} %get-tuple-element.24), channel_id=1, source_target_pairs={{0,20},{1,21},{2,22},{3,23},{4,16},{5,17},{6,18},{7,19},{8,28},{9,... | collective-permute-start | bytes 294920 | tf_op jit(solution)/shard_map/ppermute | solution.py:266
  8.9 38.6 %copy-start.1 = (f32[32,128]{1,0:T(8,128)S(1)}, f32[32,128]{1,0:T(8,128)}, u32[]{:S(2)}) copy-start(f32[32,128]{1,0:T(8,128)} %virt.1) | copy-start | bytes 49156
  8.9 38.6 %copy-start.2 = (s32[8,16]{1,0:T(8,128)S(1)}, s32[8,16]{1,0:T(8,128)}, u32[]{:S(2)}) copy-start(s32[8,16]{1,0:T(8,128)} %screening.3) | copy-start | bytes 1540
  8.9 38.6 %copy-start.3 = (s32[32]{0:T(128)S(1)}, s32[32]{0:T(128)}, u32[]{:S(2)}) copy-start(s32[32]{0:T(128)} %tile_slot.3) | copy-start | bytes 388
  10.7 11.3 %collective-permute-start.6 = (bf16[3,128,128]{2,1,0:T(8,128)(2,1)S(1)}, bf16[3,128,128]{2,1,0:T(8,128)(2,1)S(1)}, u32[]{:S(2)}, u32[]{:S(2)}) collective-permute-start(bf16[3,128,128]{2,1,0:T(8,128)(2,1)S(1)} %copy-done.7), channel_id=1, source_target_pairs={{0,24},{1,25},{2,26},{3,27},{4,28},{5,29},{6,30},{7,31},{8,16},{9,... | collective-permute-start | bytes 294920 | tf_op jit(solution)/shard_map/ppermute | solution.py:266
  11.0 14.6 %collective-permute-start.7 = (bf16[3,128,128]{2,1,0:T(8,128)(2,1)S(1)}, bf16[3,128,128]{2,1,0:T(8,128)(2,1)S(1)}, u32[]{:S(2)}, u32[]{:S(2)}) collective-permute-start(bf16[3,128,128]{2,1,0:T(8,128)(2,1)S(1)} %copy-done.6), channel_id=1, source_target_pairs={{0,28},{1,29},{2,30},{3,31},{4,24},{5,25},{6,26},{7,27},{8,20},{9,... | collective-permute-start | bytes 294920 | tf_op jit(solution)/shard_map/ppermute | solution.py:266
  22.0 7.8 %collective-permute-start.10 = (bf16[3,128,128]{2,1,0:T(8,128)(2,1)S(1)}, bf16[3,128,128]{2,1,0:T(8,128)(2,1)S(1)}, u32[]{:S(2)}, u32[]{:S(2)}) collective-permute-start(bf16[3,128,128]{2,1,0:T(8,128)(2,1)S(1)} %copy-done.4), channel_id=1, source_target_pairs={{0,1},{1,0},{2,3},{3,2},{4,5},{5,4},{6,7},{7,6},{8,9},{9,8},{10,11... | collective-permute-start | bytes 294920 | tf_op jit(solution)/shard_map/ppermute | solution.py:266
  25.5 9.3 %collective-permute-start.12 = (bf16[2,3,128,128]{3,2,1,0:T(8,128)(2,1)S(1)}, bf16[2,3,128,128]{3,2,1,0:T(8,128)(2,1)S(1)}, u32[]{:S(2)}, u32[]{:S(2)}) collective-permute-start(bf16[2,3,128,128]{3,2,1,0:T(8,128)(2,1)S(1)} %pad_maximum_fusion.4), channel_id=1, source_target_pairs={{0,1},{1,0},{2,3},{3,2},{4,5},{5,4},{6,7},{7,6},{8,9},{9,8},{10,11... | collective-permute-start | bytes 589832 | tf_op jit(solution)/shard_map/ppermute | solution.py:266
  25.8 21.1 %collective-permute-start.9 = (bf16[2,3,128,128]{3,2,1,0:T(8,128)(2,1)S(1)}, bf16[2,3,128,128]{3,2,1,0:T(8,128)(2,1)S(1)}, u32[]{:S(2)}, u32[]{:S(2)}) collective-permute-start(bf16[2,3,128,128]{3,2,1,0:T(8,128)(2,1)S(1)} %pad_maximum_fusion.3.refs_1_.refs_3_), channel_id=1, source_target_pairs={{0,2},{1,3},{2,0},{3,1},{4,6},{5,7},{6,4},{7,5},{8,10},{9,11},{10,... | collective-permute-start | bytes 589832 | tf_op jit(solution)/shard_map/ppermute | solution.py:266
  27.5 23.5 %collective-permute-start.3 = (bf16[4,3,128,128]{3,2,1,0:T(8,128)(2,1)S(1)}, bf16[4,3,128,128]{3,2,1,0:T(8,128)(2,1)}, u32[]{:S(2)}, u32[]{:S(2)}) collective-permute-start(bf16[4,3,128,128]{3,2,1,0:T(8,128)(2,1)S(1)} %pad_maximum_fusion.refs_0_), channel_id=1, source_target_pairs={{0,2},{1,3},{2,0},{3,1},{4,6},{5,7},{6,4},{7,5},{8,10},{9,11},{10,... | collective-permute-start | bytes 1179656 | tf_op jit(solution)/shard_map/ppermute | solution.py:266
  27.6 8.4 %copy-start.5 = (bf16[3,128,128]{2,1,0:T(8,128)(2,1)}, bf16[3,128,128]{2,1,0:T(8,128)(2,1)S(1)}, u32[]{:S(2)}) copy-start(bf16[3,128,128]{2,1,0:T(8,128)(2,1)S(1)} %collective-permute-done.5) | copy-start | bytes 294916
  27.6 7.0 %collective-permute-start.11 = (bf16[3,128,128]{2,1,0:T(8,128)(2,1)S(1)}, bf16[3,128,128]{2,1,0:T(8,128)(2,1)S(1)}, u32[]{:S(2)}, u32[]{:S(2)}) collective-permute-start(bf16[3,128,128]{2,1,0:T(8,128)(2,1)S(1)} %collective-permute-done), channel_id=1, source_target_pairs={{0,1},{1,0},{2,3},{3,2},{4,5},{5,4},{6,7},{7,6},{8,9},{9,8},{10,11... | collective-permute-start | bytes 294920 | tf_op jit(solution)/shard_map/ppermute | solution.py:266
  29.8 14.0 %collective-permute-start.14 = (bf16[3,128,128]{2,1,0:T(8,128)(2,1)}, bf16[3,128,128]{2,1,0:T(8,128)(2,1)S(1)}, u32[]{:S(2)}, u32[]{:S(2)}) collective-permute-start(bf16[3,128,128]{2,1,0:T(8,128)(2,1)} %collective-permute-done.4), channel_id=1, source_target_pairs={{0,1},{1,0},{2,3},{3,2},{4,5},{5,4},{6,7},{7,6},{8,9},{9,8},{10,11... | collective-permute-start | bytes 294920 | tf_op jit(solution)/shard_map/ppermute | solution.py:266
  34.6 3.7 %collective-permute-start.16 = (bf16[3,128,128]{2,1,0:T(8,128)(2,1)S(1)}, bf16[3,128,128]{2,1,0:T(8,128)(2,1)S(1)}, u32[]{:S(2)}, u32[]{:S(2)}) collective-permute-start(bf16[3,128,128]{2,1,0:T(8,128)(2,1)S(1)} %collective-permute-done.6), channel_id=1, source_target_pairs={{0,1},{1,0},{2,3},{3,2},{4,5},{5,4},{6,7},{7,6},{8,9},{9,8},{10,11... | collective-permute-start | bytes 294920 | tf_op jit(solution)/shard_map/ppermute | solution.py:266
  34.8 4.6 %collective-permute-start.17 = (bf16[3,128,128]{2,1,0:T(8,128)(2,1)S(1)}, bf16[3,128,128]{2,1,0:T(8,128)(2,1)S(1)}, u32[]{:S(2)}, u32[]{:S(2)}) collective-permute-start(bf16[3,128,128]{2,1,0:T(8,128)(2,1)S(1)} %collective-permute-done.7), channel_id=1, source_target_pairs={{0,1},{1,0},{2,3},{3,2},{4,5},{5,4},{6,7},{7,6},{8,9},{9,8},{10,11... | collective-permute-start | bytes 294920 | tf_op jit(solution)/shard_map/ppermute | solution.py:266
  38.3 5.5 %collective-permute-start.15 = (bf16[3,128,128]{2,1,0:T(8,128)(2,1)}, bf16[3,128,128]{2,1,0:T(8,128)(2,1)S(1)}, u32[]{:S(2)}, u32[]{:S(2)}) collective-permute-start(bf16[3,128,128]{2,1,0:T(8,128)(2,1)} %copy-done.5), channel_id=1, source_target_pairs={{0,1},{1,0},{2,3},{3,2},{4,5},{5,4},{6,7},{7,6},{8,9},{9,8},{10,11... | collective-permute-start | bytes 294920 | tf_op jit(solution)/shard_map/ppermute | solution.py:266
  39.4 13.7 %collective-permute-start.13 = (bf16[4,3,128,128]{3,2,1,0:T(8,128)(2,1)S(1)}, bf16[4,3,128,128]{3,2,1,0:T(8,128)(2,1)}, u32[]{:S(2)}, u32[]{:S(2)}) collective-permute-start(bf16[4,3,128,128]{3,2,1,0:T(8,128)(2,1)S(1)} %pad_maximum_fusion.1.refs_0_.refs_6_), channel_id=1, source_target_pairs={{0,2},{1,3},{2,0},{3,1},{4,6},{5,7},{6,4},{7,5},{8,10},{9,11},{10,... | collective-permute-start | bytes 1179656 | tf_op jit(solution)/shard_map/ppermute | solution.py:266
  43.8 5.2 %collective-permute-start.8 = (bf16[2,3,128,128]{3,2,1,0:T(8,128)(2,1)S(1)}, bf16[2,3,128,128]{3,2,1,0:T(8,128)(2,1)}, u32[]{:S(2)}, u32[]{:S(2)}) collective-permute-start(bf16[2,3,128,128]{3,2,1,0:T(8,128)(2,1)S(1)} %pad_maximum_fusion.2.refs_0_.refs_2_), channel_id=1, source_target_pairs={{0,2},{1,3},{2,0},{3,1},{4,6},{5,7},{6,4},{7,5},{8,10},{9,11},{10,... | collective-permute-start | bytes 589832 | tf_op jit(solution)/shard_map/ppermute | solution.py:266
  43.8 11.3 %collective-permute-start.19 = (bf16[2,3,128,128]{3,2,1,0:T(8,128)(2,1)}, bf16[2,3,128,128]{3,2,1,0:T(8,128)(2,1)}, u32[]{:S(2)}, u32[]{:S(2)}) collective-permute-start(bf16[2,3,128,128]{3,2,1,0:T(8,128)(2,1)} %pad_maximum_fusion.6.refs_9_), channel_id=1, source_target_pairs={{0,2},{1,3},{2,0},{3,1},{4,6},{5,7},{6,4},{7,5},{8,10},{9,11},{10,... | collective-permute-start | bytes 589832 | tf_op jit(solution)/shard_map/ppermute | solution.py:266
  46.9 8.3 %collective-permute-start.18 = (bf16[2,3,128,128]{3,2,1,0:T(8,128)(2,1)}, bf16[2,3,128,128]{3,2,1,0:T(8,128)(2,1)}, u32[]{:S(2)}, u32[]{:S(2)}) collective-permute-start(bf16[2,3,128,128]{3,2,1,0:T(8,128)(2,1)} %pad_maximum_fusion.5.refs_8_), channel_id=1, source_target_pairs={{0,2},{1,3},{2,0},{3,1},{4,6},{5,7},{6,4},{7,5},{8,10},{9,11},{10,... | collective-permute-start | bytes 589832 | tf_op jit(solution)/shard_map/ppermute | solution.py:266

commit v5 on v4

--- a/solution.py
+++ b/solution.py
@@ -68,12 +68,23 @@
     )(screening, tile_slot, factors)
 
 
-def plan_kernel(dims, screening, tile_slot, occ, virt, table, row_den, col_e):
+def plan_kernel(dims, screening, tile_slot, orbitals, occupied, virtual, *refs):
     tile_dev, group, row_tiles, shifts, tile = dims
+    table, row_den, col_e, *held, sems = refs
+    given = (screening, tile_slot, orbitals, occupied, virtual)
+    copies = [
+        pltpu.make_async_copy(x, y, sems.at[n]) for n, (x, y) in enumerate(zip(given, held))
+    ]
+    for copy in copies:
+        copy.start()
+    for copy in copies:
+        copy.wait()
+    screening, tile_slot, orbitals, occupied, virt = held
     me, cut = lax.axis_index("pair"), lax.axis_index("cuts")
     pair_id, core = me // group, me % group
     count = screening.shape[1]
     first = core * (count // group) + cut * row_tiles
+    occ = [occupied[orbitals[n, pair_id]] for n in range(2)]
 
     def source(t):
         slot = tile_slot[screening[pair_id, t]]
@@ -91,7 +102,7 @@
         row_den[i] = jnp.broadcast_to(row, (tile, tile)).T
 
 
-def plan(screening, tile_slot, occ, virt, dims):
+def plan(screening, tile_slot, orbitals, occupied, virtual, dims):
     _, _, row_tiles, _, tile = dims
     count = screening.shape[1]
     return pl.pallas_call(
@@ -101,11 +112,18 @@
             jax.ShapeDtypeStruct((row_tiles, tile, tile), jnp.float32),
             jax.ShapeDtypeStruct((count, tile), jnp.float32),
         ],
-        in_specs=[SMEM, SMEM, SMEM, VMEM],
+        in_specs=[pl.BlockSpec(memory_space=pltpu.HBM)] * 5,
         out_specs=[SMEM, VMEM, VMEM],
-        compiler_params=pltpu.CompilerParams(vmem_limit_bytes=4 * 2**20),
+        scratch_shapes=[
+            pltpu.SMEM(screening.shape, jnp.int32),
+            pltpu.SMEM(tile_slot.shape, jnp.int32),
+            pltpu.SMEM(orbitals.shape, jnp.int32),
+            pltpu.SMEM(occupied.shape, jnp.float32),
+            pltpu.VMEM(virtual.shape, jnp.float32),
+            pltpu.SemaphoreType.DMA((5,)),
+        ],
         name="plan",
-    )(screening, tile_slot, occ, virt)
+    )(screening, tile_slot, orbitals, occupied, virtual)
 
 
 def columns_of(bufs):
@@ -254,7 +272,6 @@
     shifts = n_pair // group
     half = shifts // 2
     row_tiles = amplitudes.shape[0] // tile // n_cut
-    me = lax.axis_index("pair")
 
     def send(x, move):
         pairs = [
@@ -281,11 +298,12 @@
         x = send(x, lambda p, c: (p, c ^ 1))
         for n, s in enumerate(members):
             crossed[s] = x[n] if len(members) > 1 else x
-    occ = occupied_energy[pair_orbitals[me // group]]
     rows = row_tiles * tile
     amp = lax.dynamic_slice_in_dim(amplitudes, lax.axis_index("cuts") * rows, rows, 0)
     dims = (tile_dev, group, row_tiles, shifts, tile)
-    table, row_den, col_e = plan(screening, tile_slot, occ, virtual_energy, dims)
+    table, row_den, col_e = plan(
+        screening, tile_slot, pair_orbitals.T, occupied_energy, virtual_energy, dims
+    )
     quarter = half + half // 2
     sides, done = [], []
     for n, held in enumerate((got, crossed)):

time: 61.4 us -> 65.9 us (1.073)
  the two profiles are of different devices: /device:TPU:21 before, /device:TPU:17 now
where the time goes in v5:
time: 65.9 us; the launch traced here: 65.6 us
  starting transfers between devices  23.1 us (35%)
  waiting for transfers between devices  21.5 us (33%)
  Pallas kernels  15.9 us (24%)
  other arithmetic  2.44 us (4%)
  local copies, waits for them, and re-layouts  2.4 us (4%)
    ppermute x20, starting transfers between devices, send(): return lax.ppermute(x, BOTH, pairs)  23.1 us
    ppermute x20, waiting for transfers between devices, send(): return lax.ppermute(x, BOTH, pairs)  21.5 us
    pallas_call x3, Pallas kernels, right(): pl.pallas_call(functools.partial(right_kernel, base, dims), out_shape=jax...  6.05 us
    pallas_call x1, Pallas kernels, left_product(): pl.pallas_call(functools.partial(left_kernel, dims, len(own)), out_shape=...  5.94 us
    another operation x6, other arithmetic, direct(): mine.append(jnp.stack(held[lo:hi]))  2.42 us
    pallas_call x1, Pallas kernels, plan(): pl.pallas_call(functools.partial(plan_kernel, dims), out_shape=[jax.Shape...  2.05 us
    pallas_call x1, Pallas kernels, pick(): pl.pallas_call(functools.partial(pick_kernel, tile_dev, group), out_shape...  1.88 us
    dynamic_slice x1, local copies, waits for them, and re-layouts, direct(): lax.dynamic_slice_in_dim(amplitudes, lax.axis_index('cuts') * rows, rows, 0)  1.73 us
  transfers between devices with their start and end apart: 20, of which 5 were waited for; matrix products, arithmetic and copies ran while one was open for 6% of the time, Pallas kernels for 12%

profile of v5, /device:TPU:17, one launch (start us, length us, event | category | flops | bytes accessed | tf_op | source)
XLA Modules:
  0.0 65.6 jit_solution(831883113373151885)
XLA Ops:
  0.0 1.9 %pick.1 = (bf16[3,128,128]{2,1,0:T(8,128)(2,1)}, bf16[3,128,128]{2,1,0:T(8,128)(2,1)}, bf16[3,128,128]{2,1,0:T(8,128)(2,1)}, bf16[3,128,128]{2,1,0:T(8,128)(2,1)...) custom-call(s32[8,16]{1,0:T(8,128)} %screening.3, ...), custom_call_target="tpu_custom_call" | custom-call | tf_op jit(solution)/shard_map/pick/pallas_call | solution.py:56
  1.9 1.4 %collective-permute-start.1 = (bf16[3,128,128]{2,1,0:T(8,128)(2,1)}, bf16[3,128,128]{2,1,0:T(8,128)(2,1)S(1)}, u32[]{:S(2)}, u32[]{:S(2)}) collective-permute-start(bf16[3,128,128]{2,1,0:T(8,128)(2,1)} %get-tuple-element.21), channel_id=1, source_target_pairs={{0,8},{1,9},{2,10},{3,11},{4,12},{5,13},{6,14},{7,15},{8,0},{9,1},... | collective-permute-start | bytes 294920 | tf_op jit(solution)/shard_map/ppermute | solution.py:283
  3.2 1.1 %collective-permute-start.2 = (bf16[3,128,128]{2,1,0:T(8,128)(2,1)}, bf16[3,128,128]{2,1,0:T(8,128)(2,1)S(1)}, u32[]{:S(2)}, u32[]{:S(2)}) collective-permute-start(bf16[3,128,128]{2,1,0:T(8,128)(2,1)} %get-tuple-element.22), channel_id=1, source_target_pairs={{0,12},{1,13},{2,14},{3,15},{4,8},{5,9},{6,10},{7,11},{8,4},{9,5},... | collective-permute-start | bytes 294920 | tf_op jit(solution)/shard_map/ppermute | solution.py:283
  4.3 0.3 collective-permute-start
  4.6 0.0 collective-permute-start.4
  4.6 3.3 %collective-permute-start.5 = (bf16[3,128,128]{2,1,0:T(8,128)(2,1)}, bf16[3,128,128]{2,1,0:T(8,128)(2,1)S(1)}, u32[]{:S(2)}, u32[]{:S(2)}) collective-permute-start(bf16[3,128,128]{2,1,0:T(8,128)(2,1)} %get-tuple-element.24), channel_id=1, source_target_pairs={{0,20},{1,21},{2,22},{3,23},{4,16},{5,17},{6,18},{7,19},{8,28},{9,... | collective-permute-start | bytes 294920 | tf_op jit(solution)/shard_map/ppermute | solution.py:283
  7.9 0.0 collective-permute-done.1
  7.9 0.2 collective-permute-start.6
  8.1 1.1 %collective-permute-done.2 = bf16[3,128,128]{2,1,0:T(8,128)(2,1)S(1)} collective-permute-done((bf16[3,128,128]{2,1,0:T(8,128)(2,1)}, bf16[3,128,128]{2,1,0:T(8,128)(2,1)S(1)}, u32[]{:S(2)}, u32[]{:S(2)}) %collective-permute-start.2) | collective-permute-done | bytes 98336 | tf_op jit(solution)/shard_map/ppermute | solution.py:283
  9.2 0.2 collective-permute-start.7
  9.4 13.2 %collective-permute-done.6 = bf16[3,128,128]{2,1,0:T(8,128)(2,1)S(1)} collective-permute-done((bf16[3,128,128]{2,1,0:T(8,128)(2,1)}, bf16[3,128,128]{2,1,0:T(8,128)(2,1)S(1)}, u32[]{:S(2)}, u32[]{:S(2)}) %collective-permute-start.6) | collective-permute-done | bytes 98336 | tf_op jit(solution)/shard_map/ppermute | solution.py:283
  22.6 1.2 %collective-permute-start.10 = (bf16[3,128,128]{2,1,0:T(8,128)(2,1)}, bf16[3,128,128]{2,1,0:T(8,128)(2,1)S(1)}, u32[]{:S(2)}, u32[]{:S(2)}) collective-permute-start(bf16[3,128,128]{2,1,0:T(8,128)(2,1)} %get-tuple-element.19), channel_id=1, source_target_pairs={{0,1},{1,0},{2,3},{3,2},{4,5},{5,4},{6,7},{7,6},{8,9},{9,8},{10,11... | collective-permute-start | bytes 294920 | tf_op jit(solution)/shard_map/ppermute | solution.py:283
  23.8 1.8 %collective-permute-done.7 = bf16[3,128,128]{2,1,0:T(8,128)(2,1)S(1)} collective-permute-done((bf16[3,128,128]{2,1,0:T(8,128)(2,1)}, bf16[3,128,128]{2,1,0:T(8,128)(2,1)S(1)}, u32[]{:S(2)}, u32[]{:S(2)}) %collective-permute-start.7) | collective-permute-done | bytes 98336 | tf_op jit(solution)/shard_map/ppermute | solution.py:283
  25.7 1.2 %collective-permute-start.12 = (bf16[2,3,128,128]{3,2,1,0:T(8,128)(2,1)S(1)}, bf16[2,3,128,128]{3,2,1,0:T(8,128)(2,1)S(1)}, u32[]{:S(2)}, u32[]{:S(2)}) collective-permute-start(bf16[2,3,128,128]{3,2,1,0:T(8,128)(2,1)S(1)} %pad_maximum_fusion.4), channel_id=1, source_target_pairs={{0,1},{1,0},{2,3},{3,2},{4,5},{5,4},{6,7},{7,6},{8,9},{9,8},{10,11... | collective-permute-start | bytes 589832 | tf_op jit(solution)/shard_map/ppermute | solution.py:283
  26.9 1.3 %collective-permute-start.9 = (bf16[2,3,128,128]{3,2,1,0:T(8,128)(2,1)S(1)}, bf16[2,3,128,128]{3,2,1,0:T(8,128)(2,1)S(1)}, u32[]{:S(2)}, u32[]{:S(2)}) collective-permute-start(bf16[2,3,128,128]{3,2,1,0:T(8,128)(2,1)S(1)} %pad_maximum_fusion.3.refs_1_.refs_3_), channel_id=1, source_target_pairs={{0,2},{1,3},{2,0},{3,1},{4,6},{5,7},{6,4},{7,5},{8,10},{9,11},{10,... | collective-permute-start | bytes 589832 | tf_op jit(solution)/shard_map/ppermute | solution.py:283
  28.3 0.9 %pad_maximum_fusion.refs_0_ = bf16[4,3,128,128]{3,2,1,0:T(8,128)(2,1)S(1)} fusion(bf16[1,3,128,128]{3,2,1,0:T(8,128)(2,1)S(1)} %bitcast.18, bf16[1,3,128,128]{3,2,1,0:T(8,128)(2,1)S(1)} %bitcast.16, bf16[1,3,128,128]{3,2,1,0:T(8,128)(2,1)S(1)} %bitcast.20, bf16[1,3,128,128]{3,2,1,0:T(8,128)(2,1)} %bitcast.19), kind=kLoop, calls=%fused_computation | loop fusion | flops 589824 | bytes 786432 | tf_op jit(solution)/shard_map/stack | solution.py:312
  29.2 0.0 collective-permute-done.4
  29.2 0.3 collective-permute-start.16
  29.5 1.2 %collective-permute-start.17 = (bf16[3,128,128]{2,1,0:T(8,128)(2,1)S(1)}, bf16[3,128,128]{2,1,0:T(8,128)(2,1)S(1)}, u32[]{:S(2)}, u32[]{:S(2)}) collective-permute-start(bf16[3,128,128]{2,1,0:T(8,128)(2,1)S(1)} %collective-permute-done.7), channel_id=1, source_target_pairs={{0,1},{1,0},{2,3},{3,2},{4,5},{5,4},{6,7},{7,6},{8,9},{9,8},{10,11... | collective-permute-start | bytes 294920 | tf_op jit(solution)/shard_map/ppermute | solution.py:283
  30.8 3.3 %collective-permute-done.16 = bf16[3,128,128]{2,1,0:T(8,128)(2,1)S(1)} collective-permute-done((bf16[3,128,128]{2,1,0:T(8,128)(2,1)S(1)}, bf16[3,128,128]{2,1,0:T(8,128)(2,1)S(1)}, u32[]{:S(2)}, u32[]{:S(2)}) %collective-permute-start.16) | collective-permute-done | bytes 98336 | tf_op jit(solution)/shard_map/ppermute | solution.py:283
  34.1 2.2 %collective-permute-start.8 = (bf16[2,3,128,128]{3,2,1,0:T(8,128)(2,1)S(1)}, bf16[2,3,128,128]{3,2,1,0:T(8,128)(2,1)}, u32[]{:S(2)}, u32[]{:S(2)}) collective-permute-start(bf16[2,3,128,128]{3,2,1,0:T(8,128)(2,1)S(1)} %pad_maximum_fusion.2.refs_0_.refs_2_), channel_id=1, source_target_pairs={{0,2},{1,3},{2,0},{3,1},{4,6},{5,7},{6,4},{7,5},{8,10},{9,11},{10,... | collective-permute-start | bytes 589832 | tf_op jit(solution)/shard_map/ppermute | solution.py:283
  36.3 1.4 %collective-permute-start.11 = (bf16[3,128,128]{2,1,0:T(8,128)(2,1)S(1)}, bf16[3,128,128]{2,1,0:T(8,128)(2,1)S(1)}, u32[]{:S(2)}, u32[]{:S(2)}) collective-permute-start(bf16[3,128,128]{2,1,0:T(8,128)(2,1)S(1)} %collective-permute-done), channel_id=1, source_target_pairs={{0,1},{1,0},{2,3},{3,2},{4,5},{5,4},{6,7},{7,6},{8,9},{9,8},{10,11... | collective-permute-start | bytes 294920 | tf_op jit(solution)/shard_map/ppermute | solution.py:283
  37.7 0.7 %pad_maximum_fusion.6.refs_9_ = bf16[2,3,128,128]{3,2,1,0:T(8,128)(2,1)} fusion(bf16[1,3,128,128]{3,2,1,0:T(8,128)(2,1)S(1)} %bitcast.30, bf16[1,3,128,128]{3,2,1,0:T(8,128)(2,1)S(1)} %bitcast.28), kind=kLoop, calls=%fused_computation.6 | loop fusion | flops 98304 | bytes 393216 | tf_op jit(solution)/shard_map/stack | solution.py:312
  38.4 0.0 collective-permute-done.10
  38.4 1.3 %collective-permute-start.3 = (bf16[4,3,128,128]{3,2,1,0:T(8,128)(2,1)S(1)}, bf16[4,3,128,128]{3,2,1,0:T(8,128)(2,1)}, u32[]{:S(2)}, u32[]{:S(2)}) collective-permute-start(bf16[4,3,128,128]{3,2,1,0:T(8,128)(2,1)S(1)} %pad_maximum_fusion.refs_0_), channel_id=1, source_target_pairs={{0,2},{1,3},{2,0},{3,1},{4,6},{5,7},{6,4},{7,5},{8,10},{9,11},{10,... | collective-permute-start | bytes 1179656 | tf_op jit(solution)/shard_map/ppermute | solution.py:283
  39.7 0.0 collective-permute-done.11
  39.8 1.4 %collective-permute-start.14 = (bf16[3,128,128]{2,1,0:T(8,128)(2,1)S(1)}, bf16[3,128,128]{2,1,0:T(8,128)(2,1)S(1)}, u32[]{:S(2)}, u32[]{:S(2)}) collective-permute-start(bf16[3,128,128]{2,1,0:T(8,128)(2,1)S(1)} %collective-permute-done.4), channel_id=1, source_target_pairs={{0,1},{1,0},{2,3},{3,2},{4,5},{5,4},{6,7},{7,6},{8,9},{9,8},{10,11... | collective-permute-start | bytes 294920 | tf_op jit(solution)/shard_map/ppermute | solution.py:283
  41.2 0.0 collective-permute-done.12
  41.2 0.1 collective-permute-start.15
  41.3 2.0 %collective-permute-done.14 = bf16[3,128,128]{2,1,0:T(8,128)(2,1)S(1)} collective-permute-done((bf16[3,128,128]{2,1,0:T(8,128)(2,1)S(1)}, bf16[3,128,128]{2,1,0:T(8,128)(2,1)S(1)}, u32[]{:S(2)}, u32[]{:S(2)}) %collective-permute-start.14) | collective-permute-done | bytes 98336 | tf_op jit(solution)/shard_map/ppermute | solution.py:283
  43.2 3.5 %collective-permute-start.19 = (bf16[2,3,128,128]{3,2,1,0:T(8,128)(2,1)}, bf16[2,3,128,128]{3,2,1,0:T(8,128)(2,1)}, u32[]{:S(2)}, u32[]{:S(2)}) collective-permute-start(bf16[2,3,128,128]{3,2,1,0:T(8,128)(2,1)} %pad_maximum_fusion.6.refs_9_), channel_id=1, source_target_pairs={{0,2},{1,3},{2,0},{3,1},{4,6},{5,7},{6,4},{7,5},{8,10},{9,11},{10,... | collective-permute-start | bytes 589832 | tf_op jit(solution)/shard_map/ppermute | solution.py:283
  46.7 0.0 collective-permute-done.15
  46.7 1.5 %collective-permute-start.13 = (bf16[4,3,128,128]{3,2,1,0:T(8,128)(2,1)S(1)}, bf16[4,3,128,128]{3,2,1,0:T(8,128)(2,1)}, u32[]{:S(2)}, u32[]{:S(2)}) collective-permute-start(bf16[4,3,128,128]{3,2,1,0:T(8,128)(2,1)S(1)} %pad_maximum_fusion.1.refs_0_.refs_6_), channel_id=1, source_target_pairs={{0,2},{1,3},{2,0},{3,1},{4,6},{5,7},{6,4},{7,5},{8,10},{9,11},{10,... | collective-permute-start | bytes 1179656 | tf_op jit(solution)/shard_map/ppermute | solution.py:283
  48.3 0.7 %pad_maximum_fusion.5.refs_8_ = bf16[2,3,128,128]{3,2,1,0:T(8,128)(2,1)} fusion(bf16[1,3,128,128]{3,2,1,0:T(8,128)(2,1)S(1)} %bitcast.29, bf16[1,3,128,128]{3,2,1,0:T(8,128)(2,1)S(1)} %bitcast.27), kind=kLoop, calls=%fused_computation.5 | loop fusion | flops 98304 | bytes 393216 | tf_op jit(solution)/shard_map/stack | solution.py:312
  49.0 0.0 collective-permute-done.9.refs_3_.refs_5_
  49.0 0.0 collective-permute-start.18
  49.0 1.7 %constant_dynamic-slice_fusion.amp = bf16[512,2048]{1,0:T(8,128)(2,1)S(1)} fusion(bf16[1024,2048]{1,0:T(8,128)(2,1)} %param.7, s32[]{:T(128)S(6)} %select_n.3), kind=kLoop, calls=%fused_computation.7 | loop fusion | bytes 4194308 | tf_op jit(solution)/shard_map/dynamic_slice | solution.py:302
  50.7 2.1 %plan.1 = (s32[20]{0:T(128)}, f32[4,128,128]{2,1,0:T(8,128)}, f32[16,128]{1,0:T(8,128)}) custom-call(s32[8,16]{1,0:T(8,128)} %screening.3, s32[32]{0:T(128)} %tile_slot.3, s32[2,8]{1,0:T(2,128)} %bitcast.31, f32[4000]{0:T(1024)} %occupied.1, f32[32,128]{1,0:T(8,128)} %virtual.1), custom_call_target="tpu_custom_call" | custom-call | tf_op jit(solution)/shard_map/plan/pallas_call | solution.py:108
  52.8 0.0 collective-permute-done.8.refs_2_.refs_4_
  52.8 0.7 copy-done.1
  53.4 2.0 %right.4.refs_13_ = bf16[4,3,128,1024]{3,2,1,0:T(8,128)(2,1)S(1)} custom-call(s32[20]{0:T(128)S(1)} %copy-done.1, bf16[512,2048]{1,0:T(8,128)(2,1)S(1)} %constant_dynamic-slice_fusion.amp, bf16[2,3,128,128]{3,2,1,0:T(8,128)(2,1)S(1)} %pad_maximum_fusion.2.refs_0_.refs_2_, bf16[2,3,128,128]{3,2,1,0:T(8,128)(2,1)S(1)} %pad_maximum_fusion.3.refs_1_.refs_3_, ...), custom_call_target="tpu_custom_call" | custom-call | flops 402653184 | tf_op jit(solution)/shard_map/right/pallas_call | solution.py:180
  55.4 0.0 collective-permute-done.3.refs_1_
  55.4 2.0 %right.3.refs_12_ = bf16[4,3,128,1024]{3,2,1,0:T(8,128)(2,1)S(1)} custom-call(s32[20]{0:T(128)S(1)} %copy-done.1, bf16[512,2048]{1,0:T(8,128)(2,1)S(1)} %constant_dynamic-slice_fusion.amp, bf16[4,3,128,128]{3,2,1,0:T(8,128)(2,1)S(1)} %pad_maximum_fusion.refs_0_, bf16[4,3,128,128]{3,2,1,0:T(8,128)(2,1)} %collective-permute-done.3.refs_1_), custom_call_target="tpu_custom_call" | custom-call | flops 402653184 | tf_op jit(solution)/shard_map/right/pallas_call | solution.py:180
  57.5 0.0 copy-start
  57.5 0.0 collective-permute-done.13.refs_1_.refs_7_
  57.5 2.1 %right.5.refs_14_ = bf16[4,3,128,1024]{3,2,1,0:T(8,128)(2,1)S(1)} custom-call(s32[20]{0:T(128)S(1)} %copy-done.1, bf16[512,2048]{1,0:T(8,128)(2,1)S(1)} %constant_dynamic-slice_fusion.amp, bf16[4,3,128,128]{3,2,1,0:T(8,128)(2,1)S(1)} %pad_maximum_fusion.1.refs_0_.refs_6_, bf16[4,3,128,128]{3,2,1,0:T(8,128)(2,1)} %collective-permute-done.13.refs_1_.refs_7_), custom_call_target="tpu_custom_call" | custom-call | flops 402653184 | tf_op jit(solution)/shard_map/right/pallas_call | solution.py:180
  59.6 0.0 collective-permute-done.18.refs_10_
  59.6 5.9 %left.1 = f32[512,2048]{1,0:T(8,128)} custom-call(s32[20]{0:T(128)S(1)} %copy-done.2, f32[4,128,128]{2,1,0:T(8,128)S(1)} %copy-done, f32[16,128]{1,0:T(8,128)S(1)} %copy-done.3, bf16[512,2048]{1,0:T(8,128)(2,1)S(1)} %constant_dynamic-slice_fusion.amp, bf16[4,3,128,128]{3,2,1,0:T(8,128)(2,1)S(1)} %pad_maximum_fusion.refs_0_, ...), custom_call_target="tpu_custom_call" | custom-call | tf_op jit(solution)/shard_map/left/pallas_call | solution.py:243
  (14 shorter events, 0.1 us)
Async XLA Ops:
  1.9 6.0 %collective-permute-start.1 = (bf16[3,128,128]{2,1,0:T(8,128)(2,1)}, bf16[3,128,128]{2,1,0:T(8,128)(2,1)S(1)}, u32[]{:S(2)}, u32[]{:S(2)}) collective-permute-start(bf16[3,128,128]{2,1,0:T(8,128)(2,1)} %get-tuple-element.21), channel_id=1, source_target_pairs={{0,8},{1,9},{2,10},{3,11},{4,12},{5,13},{6,14},{7,15},{8,0},{9,1},... | collective-permute-start | bytes 294920 | tf_op jit(solution)/shard_map/ppermute | solution.py:283
  3.2 5.9 %collective-permute-start.2 = (bf16[3,128,128]{2,1,0:T(8,128)(2,1)}, bf16[3,128,128]{2,1,0:T(8,128)(2,1)S(1)}, u32[]{:S(2)}, u32[]{:S(2)}) collective-permute-start(bf16[3,128,128]{2,1,0:T(8,128)(2,1)} %get-tuple-element.22), channel_id=1, source_target_pairs={{0,12},{1,13},{2,14},{3,15},{4,8},{5,9},{6,10},{7,11},{8,4},{9,5},... | collective-permute-start | bytes 294920 | tf_op jit(solution)/shard_map/ppermute | solution.py:283
  4.3 22.6 %collective-permute-start = (bf16[3,128,128]{2,1,0:T(8,128)(2,1)}, bf16[3,128,128]{2,1,0:T(8,128)(2,1)S(1)}, u32[]{:S(2)}, u32[]{:S(2)}) collective-permute-start(bf16[3,128,128]{2,1,0:T(8,128)(2,1)} %get-tuple-element.20), channel_id=1, source_target_pairs={{0,4},{1,5},{2,6},{3,7},{4,0},{5,1},{6,2},{7,3},{8,12},{9,13},{10,... | collective-permute-start | bytes 294920 | tf_op jit(solution)/shard_map/ppermute | solution.py:283
  4.6 24.6 %collective-permute-start.4 = (bf16[3,128,128]{2,1,0:T(8,128)(2,1)}, bf16[3,128,128]{2,1,0:T(8,128)(2,1)S(1)}, u32[]{:S(2)}, u32[]{:S(2)}) collective-permute-start(bf16[3,128,128]{2,1,0:T(8,128)(2,1)} %get-tuple-element.23), channel_id=1, source_target_pairs={{0,16},{1,17},{2,18},{3,19},{4,20},{5,21},{6,22},{7,23},{8,24},{9,... | collective-permute-start | bytes 294920 | tf_op jit(solution)/shard_map/ppermute | solution.py:283
  4.6 24.9 %collective-permute-start.5 = (bf16[3,128,128]{2,1,0:T(8,128)(2,1)}, bf16[3,128,128]{2,1,0:T(8,128)(2,1)S(1)}, u32[]{:S(2)}, u32[]{:S(2)}) collective-permute-start(bf16[3,128,128]{2,1,0:T(8,128)(2,1)} %get-tuple-element.24), channel_id=1, source_target_pairs={{0,20},{1,21},{2,22},{3,23},{4,16},{5,17},{6,18},{7,19},{8,28},{9,... | collective-permute-start | bytes 294920 | tf_op jit(solution)/shard_map/ppermute | solution.py:283
  7.9 14.7 %collective-permute-start.6 = (bf16[3,128,128]{2,1,0:T(8,128)(2,1)}, bf16[3,128,128]{2,1,0:T(8,128)(2,1)S(1)}, u32[]{:S(2)}, u32[]{:S(2)}) collective-permute-start(bf16[3,128,128]{2,1,0:T(8,128)(2,1)} %get-tuple-element.25), channel_id=1, source_target_pairs={{0,24},{1,25},{2,26},{3,27},{4,28},{5,29},{6,30},{7,31},{8,16},{9,... | collective-permute-start | bytes 294920 | tf_op jit(solution)/shard_map/ppermute | solution.py:283
  9.2 16.5 %collective-permute-start.7 = (bf16[3,128,128]{2,1,0:T(8,128)(2,1)}, bf16[3,128,128]{2,1,0:T(8,128)(2,1)S(1)}, u32[]{:S(2)}, u32[]{:S(2)}) collective-permute-start(bf16[3,128,128]{2,1,0:T(8,128)(2,1)} %get-tuple-element.26), channel_id=1, source_target_pairs={{0,28},{1,29},{2,30},{3,31},{4,24},{5,25},{6,26},{7,27},{8,20},{9,... | collective-permute-start | bytes 294920 | tf_op jit(solution)/shard_map/ppermute | solution.py:283
  22.6 15.8 %collective-permute-start.10 = (bf16[3,128,128]{2,1,0:T(8,128)(2,1)}, bf16[3,128,128]{2,1,0:T(8,128)(2,1)S(1)}, u32[]{:S(2)}, u32[]{:S(2)}) collective-permute-start(bf16[3,128,128]{2,1,0:T(8,128)(2,1)} %get-tuple-element.19), channel_id=1, source_target_pairs={{0,1},{1,0},{2,3},{3,2},{4,5},{5,4},{6,7},{7,6},{8,9},{9,8},{10,11... | collective-permute-start | bytes 294920 | tf_op jit(solution)/shard_map/ppermute | solution.py:283
  25.7 15.5 %collective-permute-start.12 = (bf16[2,3,128,128]{3,2,1,0:T(8,128)(2,1)S(1)}, bf16[2,3,128,128]{3,2,1,0:T(8,128)(2,1)S(1)}, u32[]{:S(2)}, u32[]{:S(2)}) collective-permute-start(bf16[2,3,128,128]{3,2,1,0:T(8,128)(2,1)S(1)} %pad_maximum_fusion.4), channel_id=1, source_target_pairs={{0,1},{1,0},{2,3},{3,2},{4,5},{5,4},{6,7},{7,6},{8,9},{9,8},{10,11... | collective-permute-start | bytes 589832 | tf_op jit(solution)/shard_map/ppermute | solution.py:283
  26.9 22.0 %collective-permute-start.9 = (bf16[2,3,128,128]{3,2,1,0:T(8,128)(2,1)S(1)}, bf16[2,3,128,128]{3,2,1,0:T(8,128)(2,1)S(1)}, u32[]{:S(2)}, u32[]{:S(2)}) collective-permute-start(bf16[2,3,128,128]{3,2,1,0:T(8,128)(2,1)S(1)} %pad_maximum_fusion.3.refs_1_.refs_3_), channel_id=1, source_target_pairs={{0,2},{1,3},{2,0},{3,1},{4,6},{5,7},{6,4},{7,5},{8,10},{9,11},{10,... | collective-permute-start | bytes 589832 | tf_op jit(solution)/shard_map/ppermute | solution.py:283
  29.2 4.9 %collective-permute-start.16 = (bf16[3,128,128]{2,1,0:T(8,128)(2,1)S(1)}, bf16[3,128,128]{2,1,0:T(8,128)(2,1)S(1)}, u32[]{:S(2)}, u32[]{:S(2)}) collective-permute-start(bf16[3,128,128]{2,1,0:T(8,128)(2,1)S(1)} %collective-permute-done.6), channel_id=1, source_target_pairs={{0,1},{1,0},{2,3},{3,2},{4,5},{5,4},{6,7},{7,6},{8,9},{9,8},{10,11... | collective-permute-start | bytes 294920 | tf_op jit(solution)/shard_map/ppermute | solution.py:283
  29.5 6.8 %collective-permute-start.17 = (bf16[3,128,128]{2,1,0:T(8,128)(2,1)S(1)}, bf16[3,128,128]{2,1,0:T(8,128)(2,1)S(1)}, u32[]{:S(2)}, u32[]{:S(2)}) collective-permute-start(bf16[3,128,128]{2,1,0:T(8,128)(2,1)S(1)} %collective-permute-done.7), channel_id=1, source_target_pairs={{0,1},{1,0},{2,3},{3,2},{4,5},{5,4},{6,7},{7,6},{8,9},{9,8},{10,11... | collective-permute-start | bytes 294920 | tf_op jit(solution)/shard_map/ppermute | solution.py:283
  34.1 18.7 %collective-permute-start.8 = (bf16[2,3,128,128]{3,2,1,0:T(8,128)(2,1)S(1)}, bf16[2,3,128,128]{3,2,1,0:T(8,128)(2,1)}, u32[]{:S(2)}, u32[]{:S(2)}) collective-permute-start(bf16[2,3,128,128]{3,2,1,0:T(8,128)(2,1)S(1)} %pad_maximum_fusion.2.refs_0_.refs_2_), channel_id=1, source_target_pairs={{0,2},{1,3},{2,0},{3,1},{4,6},{5,7},{6,4},{7,5},{8,10},{9,11},{10,... | collective-permute-start | bytes 589832 | tf_op jit(solution)/shard_map/ppermute | solution.py:283
  36.3 3.5 %collective-permute-start.11 = (bf16[3,128,128]{2,1,0:T(8,128)(2,1)S(1)}, bf16[3,128,128]{2,1,0:T(8,128)(2,1)S(1)}, u32[]{:S(2)}, u32[]{:S(2)}) collective-permute-start(bf16[3,128,128]{2,1,0:T(8,128)(2,1)S(1)} %collective-permute-done), channel_id=1, source_target_pairs={{0,1},{1,0},{2,3},{3,2},{4,5},{5,4},{6,7},{7,6},{8,9},{9,8},{10,11... | collective-permute-start | bytes 294920 | tf_op jit(solution)/shard_map/ppermute | solution.py:283
  38.4 17.0 %collective-permute-start.3 = (bf16[4,3,128,128]{3,2,1,0:T(8,128)(2,1)S(1)}, bf16[4,3,128,128]{3,2,1,0:T(8,128)(2,1)}, u32[]{:S(2)}, u32[]{:S(2)}) collective-permute-start(bf16[4,3,128,128]{3,2,1,0:T(8,128)(2,1)S(1)} %pad_maximum_fusion.refs_0_), channel_id=1, source_target_pairs={{0,2},{1,3},{2,0},{3,1},{4,6},{5,7},{6,4},{7,5},{8,10},{9,11},{10,... | collective-permute-start | bytes 1179656 | tf_op jit(solution)/shard_map/ppermute | solution.py:283
  39.8 3.5 %collective-permute-start.14 = (bf16[3,128,128]{2,1,0:T(8,128)(2,1)S(1)}, bf16[3,128,128]{2,1,0:T(8,128)(2,1)S(1)}, u32[]{:S(2)}, u32[]{:S(2)}) collective-permute-start(bf16[3,128,128]{2,1,0:T(8,128)(2,1)S(1)} %collective-permute-done.4), channel_id=1, source_target_pairs={{0,1},{1,0},{2,3},{3,2},{4,5},{5,4},{6,7},{7,6},{8,9},{9,8},{10,11... | collective-permute-start | bytes 294920 | tf_op jit(solution)/shard_map/ppermute | solution.py:283
  41.2 5.6 %collective-permute-start.15 = (bf16[3,128,128]{2,1,0:T(8,128)(2,1)S(1)}, bf16[3,128,128]{2,1,0:T(8,128)(2,1)S(1)}, u32[]{:S(2)}, u32[]{:S(2)}) collective-permute-start(bf16[3,128,128]{2,1,0:T(8,128)(2,1)S(1)} %collective-permute-done.5), channel_id=1, source_target_pairs={{0,1},{1,0},{2,3},{3,2},{4,5},{5,4},{6,7},{7,6},{8,9},{9,8},{10,11... | collective-permute-start | bytes 294920 | tf_op jit(solution)/shard_map/ppermute | solution.py:283
  43.2 16.3 %collective-permute-start.19 = (bf16[2,3,128,128]{3,2,1,0:T(8,128)(2,1)}, bf16[2,3,128,128]{3,2,1,0:T(8,128)(2,1)}, u32[]{:S(2)}, u32[]{:S(2)}) collective-permute-start(bf16[2,3,128,128]{3,2,1,0:T(8,128)(2,1)} %pad_maximum_fusion.6.refs_9_), channel_id=1, source_target_pairs={{0,2},{1,3},{2,0},{3,1},{4,6},{5,7},{6,4},{7,5},{8,10},{9,11},{10,... | collective-permute-start | bytes 589832 | tf_op jit(solution)/shard_map/ppermute | solution.py:283
  46.7 10.7 %collective-permute-start.13 = (bf16[4,3,128,128]{3,2,1,0:T(8,128)(2,1)S(1)}, bf16[4,3,128,128]{3,2,1,0:T(8,128)(2,1)}, u32[]{:S(2)}, u32[]{:S(2)}) collective-permute-start(bf16[4,3,128,128]{3,2,1,0:T(8,128)(2,1)S(1)} %pad_maximum_fusion.1.refs_0_.refs_6_), channel_id=1, source_target_pairs={{0,2},{1,3},{2,0},{3,1},{4,6},{5,7},{6,4},{7,5},{8,10},{9,11},{10,... | collective-permute-start | bytes 1179656 | tf_op jit(solution)/shard_map/ppermute | solution.py:283
  49.0 10.6 %collective-permute-start.18 = (bf16[2,3,128,128]{3,2,1,0:T(8,128)(2,1)}, bf16[2,3,128,128]{3,2,1,0:T(8,128)(2,1)}, u32[]{:S(2)}, u32[]{:S(2)}) collective-permute-start(bf16[2,3,128,128]{3,2,1,0:T(8,128)(2,1)} %pad_maximum_fusion.5.refs_8_), channel_id=1, source_target_pairs={{0,2},{1,3},{2,0},{3,1},{4,6},{5,7},{6,4},{7,5},{8,10},{9,11},{10,... | collective-permute-start | bytes 589832 | tf_op jit(solution)/shard_map/ppermute | solution.py:283
  52.8 0.7 %copy-start.1 = (s32[20]{0:T(128)S(1)}, s32[20]{0:T(128)}, u32[]{:S(2)}) copy-start(s32[20]{0:T(128)} %get-tuple-element.16.table) | copy-start | bytes 244
  57.5 2.1 %copy-start = (f32[4,128,128]{2,1,0:T(8,128)S(1)}, f32[4,128,128]{2,1,0:T(8,128)}, u32[]{:S(2)}) copy-start(f32[4,128,128]{2,1,0:T(8,128)} %get-tuple-element.17.row_den) | copy-start | bytes 786436
  57.5 2.1 %copy-start.2 = (s32[20]{0:T(128)S(1)}, s32[20]{0:T(128)}, u32[]{:S(2)}) copy-start(s32[20]{0:T(128)} %get-tuple-element.16.table) | copy-start | bytes 244
  57.5 2.1 %copy-start.3 = (f32[16,128]{1,0:T(8,128)S(1)}, f32[16,128]{1,0:T(8,128)}, u32[]{:S(2)}) copy-start(f32[16,128]{1,0:T(8,128)} %get-tuple-element.18.col_e) | copy-start | bytes 24580

commit v6 on v5

--- a/solution.py
+++ b/solution.py
@@ -256,13 +256,6 @@
     )(table, row_den, col_e, amp, *own, *cross, *done)
 
 
-def crossings(shifts):
-    half = shifts // 2
-    early = [[s] for s in (0, 1, half, half + 1)]
-    near = [[s, s + 1] for s in range(2, half, 2)]
-    return early + near + [[s] for s in range(half + 2, shifts)]
-
-
 def direct(
     amplitudes, factors, screening, tile_slot, pair_orbitals, occupied_energy, virtual_energy
 ):
@@ -290,14 +283,7 @@
         send(picked[s], lambda p, c: (p ^ (s * group), c))
         for s in range(1, shifts)
     ]
-    crossed = [None] * shifts
-    for members in crossings(shifts):
-        x = got[members[0]]
-        if len(members) > 1:
-            x = jnp.stack([got[s] for s in members])
-        x = send(x, lambda p, c: (p, c ^ 1))
-        for n, s in enumerate(members):
-            crossed[s] = x[n] if len(members) > 1 else x
+    crossed = [send(got[s], lambda p, c: (p, c ^ 1)) for s in range(shifts)]
     rows = row_tiles * tile
     amp = lax.dynamic_slice_in_dim(amplitudes, lax.axis_index("cuts") * rows, rows, 0)
     dims = (tile_dev, group, row_tiles, shifts, tile)

time: 65.9 us -> 58.9 us (0.89)
  the two profiles are of different devices: /device:TPU:17 before, /device:TPU:0 now
where the time goes in v6:
time: 58.9 us; the launch traced here: 58.5 us
  starting transfers between devices  28.6 us (49%)
  Pallas kernels  15.9 us (27%)
  waiting for transfers between devices  8.89 us (15%)
  other arithmetic  2.44 us (4%)
  local copies, waits for them, and re-layouts  2.4 us (4%)
    ppermute x21, starting transfers between devices, send(): return lax.ppermute(x, BOTH, pairs)  28.6 us
    ppermute x21, waiting for transfers between devices, send(): return lax.ppermute(x, BOTH, pairs)  8.89 us
    pallas_call x3, Pallas kernels, right(): pl.pallas_call(functools.partial(right_kernel, base, dims), out_shape=jax...  6.05 us
    pallas_call x1, Pallas kernels, left_product(): pl.pallas_call(functools.partial(left_kernel, dims, len(own)), out_shape=...  5.94 us
    another operation x6, other arithmetic, direct(): mine.append(jnp.stack(held[lo:hi]))  2.44 us
    pallas_call x1, Pallas kernels, plan(): pl.pallas_call(functools.partial(plan_kernel, dims), out_shape=[jax.Shape...  2.05 us
    pallas_call x1, Pallas kernels, pick(): pl.pallas_call(functools.partial(pick_kernel, tile_dev, group), out_shape...  1.9 us
    dynamic_slice x1, local copies, waits for them, and re-layouts, direct(): lax.dynamic_slice_in_dim(amplitudes, lax.axis_index('cuts') * rows, rows, 0)  1.73 us
  transfers between devices with their start and end apart: 21, of which 6 were waited for; matrix products, arithmetic and copies ran while one was open for 7% of the time, Pallas kernels for 14%

profile of v6, /device:TPU:0, one launch (start us, length us, event | category | flops | bytes accessed | tf_op | source)
XLA Modules:
  0.0 58.5 jit_solution(9017244005123858849)
XLA Ops:
  0.0 1.9 %pick.1 = (bf16[3,128,128]{2,1,0:T(8,128)(2,1)}, bf16[3,128,128]{2,1,0:T(8,128)(2,1)}, bf16[3,128,128]{2,1,0:T(8,128)(2,1)}, bf16[3,128,128]{2,1,0:T(8,128)(2,1)...) custom-call(s32[8,16]{1,0:T(8,128)} %screening.3, ...), custom_call_target="tpu_custom_call" | custom-call | tf_op jit(solution)/shard_map/pick/pallas_call | solution.py:56
  1.9 5.1 %collective-permute-start.6 = (bf16[3,128,128]{2,1,0:T(8,128)(2,1)}, bf16[3,128,128]{2,1,0:T(8,128)(2,1)S(1)}, u32[]{:S(2)}, u32[]{:S(2)}) collective-permute-start(bf16[3,128,128]{2,1,0:T(8,128)(2,1)} %get-tuple-element.25), channel_id=1, source_target_pairs={{0,24},{1,25},{2,26},{3,27},{4,28},{5,29},{6,30},{7,31},{8,16},{9,... | collective-permute-start | bytes 294920 | tf_op jit(solution)/shard_map/ppermute | solution.py:276
  7.0 1.1 %collective-permute-start.7 = (bf16[3,128,128]{2,1,0:T(8,128)(2,1)}, bf16[3,128,128]{2,1,0:T(8,128)(2,1)S(1)}, u32[]{:S(2)}, u32[]{:S(2)}) collective-permute-start(bf16[3,128,128]{2,1,0:T(8,128)(2,1)} %get-tuple-element.26), channel_id=1, source_target_pairs={{0,28},{1,29},{2,30},{3,31},{4,24},{5,25},{6,26},{7,27},{8,20},{9,... | collective-permute-start | bytes 294920 | tf_op jit(solution)/shard_map/ppermute | solution.py:276
  8.2 0.4 collective-permute-start
  8.6 0.0 collective-permute-start.1
  8.6 3.1 %collective-permute-start.2 = (bf16[3,128,128]{2,1,0:T(8,128)(2,1)}, bf16[3,128,128]{2,1,0:T(8,128)(2,1)S(1)}, u32[]{:S(2)}, u32[]{:S(2)}) collective-permute-start(bf16[3,128,128]{2,1,0:T(8,128)(2,1)} %get-tuple-element.22), channel_id=1, source_target_pairs={{0,12},{1,13},{2,14},{3,15},{4,8},{5,9},{6,10},{7,11},{8,4},{9,5},... | collective-permute-start | bytes 294920 | tf_op jit(solution)/shard_map/ppermute | solution.py:276
  11.7 0.0 collective-permute-done.6
  11.7 4.4 %collective-permute-start.4 = (bf16[3,128,128]{2,1,0:T(8,128)(2,1)}, bf16[3,128,128]{2,1,0:T(8,128)(2,1)S(1)}, u32[]{:S(2)}, u32[]{:S(2)}) collective-permute-start(bf16[3,128,128]{2,1,0:T(8,128)(2,1)} %get-tuple-element.23), channel_id=1, source_target_pairs={{0,16},{1,17},{2,18},{3,19},{4,20},{5,21},{6,22},{7,23},{8,24},{9,... | collective-permute-start | bytes 294920 | tf_op jit(solution)/shard_map/ppermute | solution.py:276
  16.1 0.0 collective-permute-done.7
  16.1 2.7 %collective-permute-start.5 = (bf16[3,128,128]{2,1,0:T(8,128)(2,1)}, bf16[3,128,128]{2,1,0:T(8,128)(2,1)S(1)}, u32[]{:S(2)}, u32[]{:S(2)}) collective-permute-start(bf16[3,128,128]{2,1,0:T(8,128)(2,1)} %get-tuple-element.24), channel_id=1, source_target_pairs={{0,20},{1,21},{2,22},{3,23},{4,16},{5,17},{6,18},{7,19},{8,28},{9,... | collective-permute-start | bytes 294920 | tf_op jit(solution)/shard_map/ppermute | solution.py:276
  18.9 1.6 %collective-permute-start.10 = (bf16[3,128,128]{2,1,0:T(8,128)(2,1)}, bf16[3,128,128]{2,1,0:T(8,128)(2,1)S(1)}, u32[]{:S(2)}, u32[]{:S(2)}) collective-permute-start(bf16[3,128,128]{2,1,0:T(8,128)(2,1)} %get-tuple-element.19), channel_id=1, source_target_pairs={{0,1},{1,0},{2,3},{3,2},{4,5},{5,4},{6,7},{7,6},{8,9},{9,8},{10,11... | collective-permute-start | bytes 294920 | tf_op jit(solution)/shard_map/ppermute | solution.py:276
  20.5 0.0 collective-permute-done.1
  20.5 0.0 collective-permute-start.9
  20.5 1.1 %collective-permute-start.11 = (bf16[3,128,128]{2,1,0:T(8,128)(2,1)S(1)}, bf16[3,128,128]{2,1,0:T(8,128)(2,1)S(1)}, u32[]{:S(2)}, u32[]{:S(2)}) collective-permute-start(bf16[3,128,128]{2,1,0:T(8,128)(2,1)S(1)} %collective-permute-done), channel_id=1, source_target_pairs={{0,1},{1,0},{2,3},{3,2},{4,5},{5,4},{6,7},{7,6},{8,9},{9,8},{10,11... | collective-permute-start | bytes 294920 | tf_op jit(solution)/shard_map/ppermute | solution.py:276
  21.6 0.9 %pad_maximum_fusion.refs_0_ = bf16[4,3,128,128]{3,2,1,0:T(8,128)(2,1)S(1)} fusion(bf16[1,3,128,128]{3,2,1,0:T(8,128)(2,1)S(1)} %bitcast.17, bf16[1,3,128,128]{3,2,1,0:T(8,128)(2,1)S(1)} %bitcast.19, bf16[1,3,128,128]{3,2,1,0:T(8,128)(2,1)S(1)} %bitcast.20, bf16[1,3,128,128]{3,2,1,0:T(8,128)(2,1)} %bitcast.18), kind=kLoop, calls=%fused_computation | loop fusion | flops 589824 | bytes 786432 | tf_op jit(solution)/shard_map/stack | solution.py:298
  22.5 1.3 %collective-permute-done.4 = bf16[3,128,128]{2,1,0:T(8,128)(2,1)S(1)} collective-permute-done((bf16[3,128,128]{2,1,0:T(8,128)(2,1)}, bf16[3,128,128]{2,1,0:T(8,128)(2,1)S(1)}, u32[]{:S(2)}, u32[]{:S(2)}) %collective-permute-start.4) | collective-permute-done | bytes 98336 | tf_op jit(solution)/shard_map/ppermute | solution.py:276
  23.8 1.5 %collective-permute-start.12 = (bf16[3,128,128]{2,1,0:T(8,128)(2,1)S(1)}, bf16[3,128,128]{2,1,0:T(8,128)(2,1)S(1)}, u32[]{:S(2)}, u32[]{:S(2)}) collective-permute-start(bf16[3,128,128]{2,1,0:T(8,128)(2,1)S(1)} %collective-permute-done.1), channel_id=1, source_target_pairs={{0,1},{1,0},{2,3},{3,2},{4,5},{5,4},{6,7},{7,6},{8,9},{9,8},{10,11... | collective-permute-start | bytes 294920 | tf_op jit(solution)/shard_map/ppermute | solution.py:276
  25.3 0.0 collective-permute-done.5
  25.3 1.2 %collective-permute-start.13 = (bf16[3,128,128]{2,1,0:T(8,128)(2,1)S(1)}, bf16[3,128,128]{2,1,0:T(8,128)(2,1)S(1)}, u32[]{:S(2)}, u32[]{:S(2)}) collective-permute-start(bf16[3,128,128]{2,1,0:T(8,128)(2,1)S(1)} %collective-permute-done.2), channel_id=1, source_target_pairs={{0,1},{1,0},{2,3},{3,2},{4,5},{5,4},{6,7},{7,6},{8,9},{9,8},{10,11... | collective-permute-start | bytes 294920 | tf_op jit(solution)/shard_map/ppermute | solution.py:276
  26.5 0.1 collective-permute-start.8
  26.6 0.5 collective-permute-start.3
  27.1 1.9 %collective-permute-done.12 = bf16[3,128,128]{2,1,0:T(8,128)(2,1)S(1)} collective-permute-done((bf16[3,128,128]{2,1,0:T(8,128)(2,1)S(1)}, bf16[3,128,128]{2,1,0:T(8,128)(2,1)S(1)}, u32[]{:S(2)}, u32[]{:S(2)}) %collective-permute-start.12) | collective-permute-done | bytes 98336 | tf_op jit(solution)/shard_map/ppermute | solution.py:276
  29.0 1.4 %collective-permute-start.17 = (bf16[3,128,128]{2,1,0:T(8,128)(2,1)S(1)}, bf16[3,128,128]{2,1,0:T(8,128)(2,1)S(1)}, u32[]{:S(2)}, u32[]{:S(2)}) collective-permute-start(bf16[3,128,128]{2,1,0:T(8,128)(2,1)S(1)} %collective-permute-done.6), channel_id=1, source_target_pairs={{0,1},{1,0},{2,3},{3,2},{4,5},{5,4},{6,7},{7,6},{8,9},{9,8},{10,11... | collective-permute-start | bytes 294920 | tf_op jit(solution)/shard_map/ppermute | solution.py:276
  30.4 0.0 collective-permute-done.13
  30.4 1.3 %collective-permute-start.18 = (bf16[3,128,128]{2,1,0:T(8,128)(2,1)S(1)}, bf16[3,128,128]{2,1,0:T(8,128)(2,1)S(1)}, u32[]{:S(2)}, u32[]{:S(2)}) collective-permute-start(bf16[3,128,128]{2,1,0:T(8,128)(2,1)S(1)} %collective-permute-done.7), channel_id=1, source_target_pairs={{0,1},{1,0},{2,3},{3,2},{4,5},{5,4},{6,7},{7,6},{8,9},{9,8},{10,11... | collective-permute-start | bytes 294920 | tf_op jit(solution)/shard_map/ppermute | solution.py:276
  31.7 0.1 pad_maximum_fusion.1.refs_0_.refs_6_
  31.7 2.0 %collective-permute-done.17 = bf16[3,128,128]{2,1,0:T(8,128)(2,1)S(1)} collective-permute-done((bf16[3,128,128]{2,1,0:T(8,128)(2,1)S(1)}, bf16[3,128,128]{2,1,0:T(8,128)(2,1)S(1)}, u32[]{:S(2)}, u32[]{:S(2)}) %collective-permute-start.17) | collective-permute-done | bytes 98336 | tf_op jit(solution)/shard_map/ppermute | solution.py:276
  33.7 1.4 %collective-permute-start.15 = (bf16[3,128,128]{2,1,0:T(8,128)(2,1)S(1)}, bf16[3,128,128]{2,1,0:T(8,128)(2,1)S(1)}, u32[]{:S(2)}, u32[]{:S(2)}) collective-permute-start(bf16[3,128,128]{2,1,0:T(8,128)(2,1)S(1)} %collective-permute-done.4), channel_id=1, source_target_pairs={{0,1},{1,0},{2,3},{3,2},{4,5},{5,4},{6,7},{7,6},{8,9},{9,8},{10,11... | collective-permute-start | bytes 294920 | tf_op jit(solution)/shard_map/ppermute | solution.py:276
  35.1 1.0 %collective-permute-done.18 = bf16[3,128,128]{2,1,0:T(8,128)(2,1)S(1)} collective-permute-done((bf16[3,128,128]{2,1,0:T(8,128)(2,1)S(1)}, bf16[3,128,128]{2,1,0:T(8,128)(2,1)S(1)}, u32[]{:S(2)}, u32[]{:S(2)}) %collective-permute-start.18) | collective-permute-done | bytes 98336 | tf_op jit(solution)/shard_map/ppermute | solution.py:276
  36.1 1.3 %collective-permute-start.16 = (bf16[3,128,128]{2,1,0:T(8,128)(2,1)S(1)}, bf16[3,128,128]{2,1,0:T(8,128)(2,1)S(1)}, u32[]{:S(2)}, u32[]{:S(2)}) collective-permute-start(bf16[3,128,128]{2,1,0:T(8,128)(2,1)S(1)} %collective-permute-done.5), channel_id=1, source_target_pairs={{0,1},{1,0},{2,3},{3,2},{4,5},{5,4},{6,7},{7,6},{8,9},{9,8},{10,11... | collective-permute-start | bytes 294920 | tf_op jit(solution)/shard_map/ppermute | solution.py:276
  37.3 0.7 %pad_maximum_fusion.5.refs_9_ = bf16[2,3,128,128]{3,2,1,0:T(8,128)(2,1)} fusion(bf16[1,3,128,128]{3,2,1,0:T(8,128)(2,1)S(1)} %bitcast.31, bf16[1,3,128,128]{3,2,1,0:T(8,128)(2,1)S(1)} %bitcast.29), kind=kLoop, calls=%fused_computation.5 | loop fusion | flops 98304 | bytes 393216 | tf_op jit(solution)/shard_map/stack | solution.py:298
  38.0 0.3 collective-permute-done.15
  38.4 0.0 collective-permute-start.20
  38.4 2.3 %collective-permute-done.16 = bf16[3,128,128]{2,1,0:T(8,128)(2,1)S(1)} collective-permute-done((bf16[3,128,128]{2,1,0:T(8,128)(2,1)S(1)}, bf16[3,128,128]{2,1,0:T(8,128)(2,1)S(1)}, u32[]{:S(2)}, u32[]{:S(2)}) %collective-permute-start.16) | collective-permute-done | bytes 98336 | tf_op jit(solution)/shard_map/ppermute | solution.py:276
  40.7 0.0 collective-permute-start.14
  40.7 0.7 %pad_maximum_fusion.4.refs_8_ = bf16[2,3,128,128]{3,2,1,0:T(8,128)(2,1)} fusion(bf16[1,3,128,128]{3,2,1,0:T(8,128)(2,1)S(1)} %bitcast.32, bf16[1,3,128,128]{3,2,1,0:T(8,128)(2,1)S(1)} %bitcast.30), kind=kLoop, calls=%fused_computation.4 | loop fusion | flops 98304 | bytes 393216 | tf_op jit(solution)/shard_map/stack | solution.py:298
  41.4 0.5 collective-permute-start.19
  41.9 1.7 %constant_dynamic-slice_fusion.amp = bf16[512,2048]{1,0:T(8,128)(2,1)S(1)} fusion(bf16[1024,2048]{1,0:T(8,128)(2,1)} %param.7, s32[]{:T(128)S(6)} %select_n.3), kind=kLoop, calls=%fused_computation.6 | loop fusion | bytes 4194308 | tf_op jit(solution)/shard_map/dynamic_slice | solution.py:288
  43.6 2.1 %plan.1 = (s32[20]{0:T(128)}, f32[4,128,128]{2,1,0:T(8,128)}, f32[16,128]{1,0:T(8,128)}) custom-call(s32[8,16]{1,0:T(8,128)} %screening.3, s32[32]{0:T(128)} %tile_slot.3, s32[2,8]{1,0:T(2,128)} %bitcast.33, f32[4000]{0:T(1024)} %occupied.1, f32[32,128]{1,0:T(8,128)} %virtual.1), custom_call_target="tpu_custom_call" | custom-call | tf_op jit(solution)/shard_map/plan/pallas_call | solution.py:108
  45.7 0.7 %copy-done.1 = s32[20]{0:T(128)S(1)} copy-done((s32[20]{0:T(128)S(1)}, s32[20]{0:T(128)}, u32[]{:S(2)}) %copy-start.1) | copy-done | bytes 104
  46.4 2.0 %right.4.refs_13_ = bf16[4,3,128,1024]{3,2,1,0:T(8,128)(2,1)S(1)} custom-call(s32[20]{0:T(128)S(1)} %copy-done.1, bf16[512,2048]{1,0:T(8,128)(2,1)S(1)} %constant_dynamic-slice_fusion.amp, bf16[2,3,128,128]{3,2,1,0:T(8,128)(2,1)S(1)} %pad_maximum_fusion.2.refs_0_.refs_2_, bf16[2,3,128,128]{3,2,1,0:T(8,128)(2,1)S(1)} %pad_maximum_fusion.3.refs_1_.refs_3_, ...), custom_call_target="tpu_custom_call" | custom-call | flops 402653184 | tf_op jit(solution)/shard_map/right/pallas_call | solution.py:180
  48.3 0.0 collective-permute-done.3.refs_1_
  48.3 2.0 %right.3.refs_12_ = bf16[4,3,128,1024]{3,2,1,0:T(8,128)(2,1)S(1)} custom-call(s32[20]{0:T(128)S(1)} %copy-done.1, bf16[512,2048]{1,0:T(8,128)(2,1)S(1)} %constant_dynamic-slice_fusion.amp, bf16[4,3,128,128]{3,2,1,0:T(8,128)(2,1)S(1)} %pad_maximum_fusion.refs_0_, bf16[4,3,128,128]{3,2,1,0:T(8,128)(2,1)} %collective-permute-done.3.refs_1_), custom_call_target="tpu_custom_call" | custom-call | flops 402653184 | tf_op jit(solution)/shard_map/right/pallas_call | solution.py:180
  50.4 0.0 copy-start
  50.4 0.0 collective-permute-done.14.refs_1_.refs_7_
  50.4 2.1 %right.5.refs_14_ = bf16[4,3,128,1024]{3,2,1,0:T(8,128)(2,1)S(1)} custom-call(s32[20]{0:T(128)S(1)} %copy-done.1, bf16[512,2048]{1,0:T(8,128)(2,1)S(1)} %constant_dynamic-slice_fusion.amp, bf16[4,3,128,128]{3,2,1,0:T(8,128)(2,1)S(1)} %pad_maximum_fusion.1.refs_0_.refs_6_, bf16[4,3,128,128]{3,2,1,0:T(8,128)(2,1)} %collective-permute-done.14.refs_1_.refs_7_), custom_call_target="tpu_custom_call" | custom-call | flops 402653184 | tf_op jit(solution)/shard_map/right/pallas_call | solution.py:180
  52.5 0.0 collective-permute-done.19.refs_10_
  52.6 5.9 %left.1 = f32[512,2048]{1,0:T(8,128)} custom-call(s32[20]{0:T(128)S(1)} %copy-done.2, f32[4,128,128]{2,1,0:T(8,128)S(1)} %copy-done, f32[16,128]{1,0:T(8,128)S(1)} %copy-done.3, bf16[512,2048]{1,0:T(8,128)(2,1)S(1)} %constant_dynamic-slice_fusion.amp, bf16[4,3,128,128]{3,2,1,0:T(8,128)(2,1)S(1)} %pad_maximum_fusion.refs_0_, ...), custom_call_target="tpu_custom_call" | custom-call | tf_op jit(solution)/shard_map/left/pallas_call | solution.py:243
  (15 shorter events, 0.1 us)
Async XLA Ops:
  1.9 9.8 %collective-permute-start.6 = (bf16[3,128,128]{2,1,0:T(8,128)(2,1)}, bf16[3,128,128]{2,1,0:T(8,128)(2,1)S(1)}, u32[]{:S(2)}, u32[]{:S(2)}) collective-permute-start(bf16[3,128,128]{2,1,0:T(8,128)(2,1)} %get-tuple-element.25), channel_id=1, source_target_pairs={{0,24},{1,25},{2,26},{3,27},{4,28},{5,29},{6,30},{7,31},{8,16},{9,... | collective-permute-start | bytes 294920 | tf_op jit(solution)/shard_map/ppermute | solution.py:276
  7.0 9.0 %collective-permute-start.7 = (bf16[3,128,128]{2,1,0:T(8,128)(2,1)}, bf16[3,128,128]{2,1,0:T(8,128)(2,1)S(1)}, u32[]{:S(2)}, u32[]{:S(2)}) collective-permute-start(bf16[3,128,128]{2,1,0:T(8,128)(2,1)} %get-tuple-element.26), channel_id=1, source_target_pairs={{0,28},{1,29},{2,30},{3,31},{4,24},{5,25},{6,26},{7,27},{8,20},{9,... | collective-permute-start | bytes 294920 | tf_op jit(solution)/shard_map/ppermute | solution.py:276
  8.2 10.7 %collective-permute-start = (bf16[3,128,128]{2,1,0:T(8,128)(2,1)}, bf16[3,128,128]{2,1,0:T(8,128)(2,1)S(1)}, u32[]{:S(2)}, u32[]{:S(2)}) collective-permute-start(bf16[3,128,128]{2,1,0:T(8,128)(2,1)} %get-tuple-element.20), channel_id=1, source_target_pairs={{0,4},{1,5},{2,6},{3,7},{4,0},{5,1},{6,2},{7,3},{8,12},{9,13},{10,... | collective-permute-start | bytes 294920 | tf_op jit(solution)/shard_map/ppermute | solution.py:276
  8.6 11.9 %collective-permute-start.1 = (bf16[3,128,128]{2,1,0:T(8,128)(2,1)}, bf16[3,128,128]{2,1,0:T(8,128)(2,1)S(1)}, u32[]{:S(2)}, u32[]{:S(2)}) collective-permute-start(bf16[3,128,128]{2,1,0:T(8,128)(2,1)} %get-tuple-element.21), channel_id=1, source_target_pairs={{0,8},{1,9},{2,10},{3,11},{4,12},{5,13},{6,14},{7,15},{8,0},{9,1},... | collective-permute-start | bytes 294920 | tf_op jit(solution)/shard_map/ppermute | solution.py:276
  8.6 11.9 %collective-permute-start.2 = (bf16[3,128,128]{2,1,0:T(8,128)(2,1)}, bf16[3,128,128]{2,1,0:T(8,128)(2,1)S(1)}, u32[]{:S(2)}, u32[]{:S(2)}) collective-permute-start(bf16[3,128,128]{2,1,0:T(8,128)(2,1)} %get-tuple-element.22), channel_id=1, source_target_pairs={{0,12},{1,13},{2,14},{3,15},{4,8},{5,9},{6,10},{7,11},{8,4},{9,5},... | collective-permute-start | bytes 294920 | tf_op jit(solution)/shard_map/ppermute | solution.py:276
  11.7 12.1 %collective-permute-start.4 = (bf16[3,128,128]{2,1,0:T(8,128)(2,1)}, bf16[3,128,128]{2,1,0:T(8,128)(2,1)S(1)}, u32[]{:S(2)}, u32[]{:S(2)}) collective-permute-start(bf16[3,128,128]{2,1,0:T(8,128)(2,1)} %get-tuple-element.23), channel_id=1, source_target_pairs={{0,16},{1,17},{2,18},{3,19},{4,20},{5,21},{6,22},{7,23},{8,24},{9,... | collective-permute-start | bytes 294920 | tf_op jit(solution)/shard_map/ppermute | solution.py:276
  16.1 9.2 %collective-permute-start.5 = (bf16[3,128,128]{2,1,0:T(8,128)(2,1)}, bf16[3,128,128]{2,1,0:T(8,128)(2,1)S(1)}, u32[]{:S(2)}, u32[]{:S(2)}) collective-permute-start(bf16[3,128,128]{2,1,0:T(8,128)(2,1)} %get-tuple-element.24), channel_id=1, source_target_pairs={{0,20},{1,21},{2,22},{3,23},{4,16},{5,17},{6,18},{7,19},{8,28},{9,... | collective-permute-start | bytes 294920 | tf_op jit(solution)/shard_map/ppermute | solution.py:276
  18.9 7.6 %collective-permute-start.10 = (bf16[3,128,128]{2,1,0:T(8,128)(2,1)}, bf16[3,128,128]{2,1,0:T(8,128)(2,1)S(1)}, u32[]{:S(2)}, u32[]{:S(2)}) collective-permute-start(bf16[3,128,128]{2,1,0:T(8,128)(2,1)} %get-tuple-element.19), channel_id=1, source_target_pairs={{0,1},{1,0},{2,3},{3,2},{4,5},{5,4},{6,7},{7,6},{8,9},{9,8},{10,11... | collective-permute-start | bytes 294920 | tf_op jit(solution)/shard_map/ppermute | solution.py:276
  20.5 20.9 %collective-permute-start.9 = (bf16[2,3,128,128]{3,2,1,0:T(8,128)(2,1)S(1)}, bf16[2,3,128,128]{3,2,1,0:T(8,128)(2,1)S(1)}, u32[]{:S(2)}, u32[]{:S(2)}) collective-permute-start(bf16[2,3,128,128]{3,2,1,0:T(8,128)(2,1)S(1)} %pad_maximum_fusion.3.refs_1_.refs_3_), channel_id=1, source_target_pairs={{0,2},{1,3},{2,0},{3,1},{4,6},{5,7},{6,4},{7,5},{8,10},{9,11},{10,... | collective-permute-start | bytes 589832 | tf_op jit(solution)/shard_map/ppermute | solution.py:276
  20.5 6.1 %collective-permute-start.11 = (bf16[3,128,128]{2,1,0:T(8,128)(2,1)S(1)}, bf16[3,128,128]{2,1,0:T(8,128)(2,1)S(1)}, u32[]{:S(2)}, u32[]{:S(2)}) collective-permute-start(bf16[3,128,128]{2,1,0:T(8,128)(2,1)S(1)} %collective-permute-done), channel_id=1, source_target_pairs={{0,1},{1,0},{2,3},{3,2},{4,5},{5,4},{6,7},{7,6},{8,9},{9,8},{10,11... | collective-permute-start | bytes 294920 | tf_op jit(solution)/shard_map/ppermute | solution.py:276
  23.8 5.2 %collective-permute-start.12 = (bf16[3,128,128]{2,1,0:T(8,128)(2,1)S(1)}, bf16[3,128,128]{2,1,0:T(8,128)(2,1)S(1)}, u32[]{:S(2)}, u32[]{:S(2)}) collective-permute-start(bf16[3,128,128]{2,1,0:T(8,128)(2,1)S(1)} %collective-permute-done.1), channel_id=1, source_target_pairs={{0,1},{1,0},{2,3},{3,2},{4,5},{5,4},{6,7},{7,6},{8,9},{9,8},{10,11... | collective-permute-start | bytes 294920 | tf_op jit(solution)/shard_map/ppermute | solution.py:276
  25.3 5.1 %collective-permute-start.13 = (bf16[3,128,128]{2,1,0:T(8,128)(2,1)S(1)}, bf16[3,128,128]{2,1,0:T(8,128)(2,1)S(1)}, u32[]{:S(2)}, u32[]{:S(2)}) collective-permute-start(bf16[3,128,128]{2,1,0:T(8,128)(2,1)S(1)} %collective-permute-done.2), channel_id=1, source_target_pairs={{0,1},{1,0},{2,3},{3,2},{4,5},{5,4},{6,7},{7,6},{8,9},{9,8},{10,11... | collective-permute-start | bytes 294920 | tf_op jit(solution)/shard_map/ppermute | solution.py:276
  26.5 19.2 %collective-permute-start.8 = (bf16[2,3,128,128]{3,2,1,0:T(8,128)(2,1)S(1)}, bf16[2,3,128,128]{3,2,1,0:T(8,128)(2,1)}, u32[]{:S(2)}, u32[]{:S(2)}) collective-permute-start(bf16[2,3,128,128]{3,2,1,0:T(8,128)(2,1)S(1)} %pad_maximum_fusion.2.refs_0_.refs_2_), channel_id=1, source_target_pairs={{0,2},{1,3},{2,0},{3,1},{4,6},{5,7},{6,4},{7,5},{8,10},{9,11},{10,... | collective-permute-start | bytes 589832 | tf_op jit(solution)/shard_map/ppermute | solution.py:276
  26.6 21.7 %collective-permute-start.3 = (bf16[4,3,128,128]{3,2,1,0:T(8,128)(2,1)S(1)}, bf16[4,3,128,128]{3,2,1,0:T(8,128)(2,1)}, u32[]{:S(2)}, u32[]{:S(2)}) collective-permute-start(bf16[4,3,128,128]{3,2,1,0:T(8,128)(2,1)S(1)} %pad_maximum_fusion.refs_0_), channel_id=1, source_target_pairs={{0,2},{1,3},{2,0},{3,1},{4,6},{5,7},{6,4},{7,5},{8,10},{9,11},{10,... | collective-permute-start | bytes 1179656 | tf_op jit(solution)/shard_map/ppermute | solution.py:276
  29.0 4.7 %collective-permute-start.17 = (bf16[3,128,128]{2,1,0:T(8,128)(2,1)S(1)}, bf16[3,128,128]{2,1,0:T(8,128)(2,1)S(1)}, u32[]{:S(2)}, u32[]{:S(2)}) collective-permute-start(bf16[3,128,128]{2,1,0:T(8,128)(2,1)S(1)} %collective-permute-done.6), channel_id=1, source_target_pairs={{0,1},{1,0},{2,3},{3,2},{4,5},{5,4},{6,7},{7,6},{8,9},{9,8},{10,11... | collective-permute-start | bytes 294920 | tf_op jit(solution)/shard_map/ppermute | solution.py:276
  30.4 5.7 %collective-permute-start.18 = (bf16[3,128,128]{2,1,0:T(8,128)(2,1)S(1)}, bf16[3,128,128]{2,1,0:T(8,128)(2,1)S(1)}, u32[]{:S(2)}, u32[]{:S(2)}) collective-permute-start(bf16[3,128,128]{2,1,0:T(8,128)(2,1)S(1)} %collective-permute-done.7), channel_id=1, source_target_pairs={{0,1},{1,0},{2,3},{3,2},{4,5},{5,4},{6,7},{7,6},{8,9},{9,8},{10,11... | collective-permute-start | bytes 294920 | tf_op jit(solution)/shard_map/ppermute | solution.py:276
  33.7 4.6 %collective-permute-start.15 = (bf16[3,128,128]{2,1,0:T(8,128)(2,1)S(1)}, bf16[3,128,128]{2,1,0:T(8,128)(2,1)S(1)}, u32[]{:S(2)}, u32[]{:S(2)}) collective-permute-start(bf16[3,128,128]{2,1,0:T(8,128)(2,1)S(1)} %collective-permute-done.4), channel_id=1, source_target_pairs={{0,1},{1,0},{2,3},{3,2},{4,5},{5,4},{6,7},{7,6},{8,9},{9,8},{10,11... | collective-permute-start | bytes 294920 | tf_op jit(solution)/shard_map/ppermute | solution.py:276
  36.1 4.6 %collective-permute-start.16 = (bf16[3,128,128]{2,1,0:T(8,128)(2,1)S(1)}, bf16[3,128,128]{2,1,0:T(8,128)(2,1)S(1)}, u32[]{:S(2)}, u32[]{:S(2)}) collective-permute-start(bf16[3,128,128]{2,1,0:T(8,128)(2,1)S(1)} %collective-permute-done.5), channel_id=1, source_target_pairs={{0,1},{1,0},{2,3},{3,2},{4,5},{5,4},{6,7},{7,6},{8,9},{9,8},{10,11... | collective-permute-start | bytes 294920 | tf_op jit(solution)/shard_map/ppermute | solution.py:276
  38.4 14.1 %collective-permute-start.20 = (bf16[2,3,128,128]{3,2,1,0:T(8,128)(2,1)}, bf16[2,3,128,128]{3,2,1,0:T(8,128)(2,1)}, u32[]{:S(2)}, u32[]{:S(2)}) collective-permute-start(bf16[2,3,128,128]{3,2,1,0:T(8,128)(2,1)} %pad_maximum_fusion.5.refs_9_), channel_id=1, source_target_pairs={{0,2},{1,3},{2,0},{3,1},{4,6},{5,7},{6,4},{7,5},{8,10},{9,11},{10,... | collective-permute-start | bytes 589832 | tf_op jit(solution)/shard_map/ppermute | solution.py:276
  40.7 9.7 %collective-permute-start.14 = (bf16[4,3,128,128]{3,2,1,0:T(8,128)(2,1)S(1)}, bf16[4,3,128,128]{3,2,1,0:T(8,128)(2,1)}, u32[]{:S(2)}, u32[]{:S(2)}) collective-permute-start(bf16[4,3,128,128]{3,2,1,0:T(8,128)(2,1)S(1)} %pad_maximum_fusion.1.refs_0_.refs_6_), channel_id=1, source_target_pairs={{0,2},{1,3},{2,0},{3,1},{4,6},{5,7},{6,4},{7,5},{8,10},{9,11},{10,... | collective-permute-start | bytes 1179656 | tf_op jit(solution)/shard_map/ppermute | solution.py:276
  41.4 11.1 %collective-permute-start.19 = (bf16[2,3,128,128]{3,2,1,0:T(8,128)(2,1)}, bf16[2,3,128,128]{3,2,1,0:T(8,128)(2,1)}, u32[]{:S(2)}, u32[]{:S(2)}) collective-permute-start(bf16[2,3,128,128]{3,2,1,0:T(8,128)(2,1)} %pad_maximum_fusion.4.refs_8_), channel_id=1, source_target_pairs={{0,2},{1,3},{2,0},{3,1},{4,6},{5,7},{6,4},{7,5},{8,10},{9,11},{10,... | collective-permute-start | bytes 589832 | tf_op jit(solution)/shard_map/ppermute | solution.py:276
  45.7 0.7 %copy-start.1 = (s32[20]{0:T(128)S(1)}, s32[20]{0:T(128)}, u32[]{:S(2)}) copy-start(s32[20]{0:T(128)} %get-tuple-element.16.table) | copy-start | bytes 244
  50.4 2.1 %copy-start = (f32[4,128,128]{2,1,0:T(8,128)S(1)}, f32[4,128,128]{2,1,0:T(8,128)}, u32[]{:S(2)}) copy-start(f32[4,128,128]{2,1,0:T(8,128)} %get-tuple-element.17.row_den) | copy-start | bytes 786436
  50.4 2.1 %copy-start.2 = (s32[20]{0:T(128)S(1)}, s32[20]{0:T(128)}, u32[]{:S(2)}) copy-start(s32[20]{0:T(128)} %get-tuple-element.16.table) | copy-start | bytes 244
  50.4 2.1 %copy-start.3 = (f32[16,128]{1,0:T(8,128)S(1)}, f32[16,128]{1,0:T(8,128)}, u32[]{:S(2)}) copy-start(f32[16,128]{1,0:T(8,128)} %get-tuple-element.18.col_e) | copy-start | bytes 24580
